TPU v7x, 32 devices: a whole 2x2x4 slice. The times are simulated.
32 devices in a mesh: grp: 2 (over y), row: 4 (over z), col: 2 (over x), sub: 2 (over core).
Axes of the slice: x: 2, y: 2, z: 4, core: 2. Of those that a mesh axis runs over, the one named last changes fastest.
Arguments:
- pair: bfloat16 [96, 48, 128], P(('grp', 'row'), 'col'), parts along dimension 0, may hold values from -6 to 6
- length: int32 [2], P('grp'), parts along dimension 0, may hold values from 24 to 48
- chain: int32 [96], P('grp'), parts along dimension 0, may hold values from 0 to 3, never falling along the last dimension, each value on 1 to 24 neighbouring positions
- att_proj: bfloat16 [128, 4, 128], P(None, None, 'sub'), may hold values from -0.5 to 0.5
- att_bias: bfloat16 [128, 4], P(None, 'sub')
- chain_bias: float32 [4], P('sub'), may hold values from -2 to 2
- att_out: bfloat16 [128, 128], P('sub'), may hold values from -0.5 to 0.5
- mult_in: bfloat16 [128, 512], replicated, may hold values from -0.5 to 0.5
- mult_gate: bfloat16 [128, 128], replicated, may hold values from -0.5 to 0.5
- mult_out: bfloat16 [128, 128], replicated, may hold values from -0.5 to 0.5
- trans_up: bfloat16 [128, 512], replicated, may hold values from -0.5 to 0.5
- trans_down: bfloat16 [512, 128], replicated, may hold values from -0.25 to 0.25
Outputs:
- pair_out: bfloat16 [96, 48, 128], P(('grp', 'row'), ('col', 'sub')), parts along dimension 0
There are 2 independent parts, one for each index of `grp`. A program takes and returns all parts, laid end to end along the dimension named above; an argument that names none is the same for every part. Nothing has to cross between parts.
Inputs may be any that keep to these rules, and one draw needn't show every extreme that they name: chain numbers never fall along the residues; each chain has 1 to 24 residues.
All inputs are finite; a program needn't handle non-finite values.
Results may differ from a plain program's by a relative error of at most 0.012.
The roundings to bfloat16 on the way count: a program that leaves them out, or rounds other values in their place, can miss the bound.
Values may be sent and summed in bfloat16 or wider, within the bound.
No kernel may reach another device: no remote copies, remote signals or barrier semaphores. Data moves between devices by JAX's collectives and lax.ppermute only.
A program may use at most 64 MiB of HBM per device.

v0:
```python
import jax
import jax.numpy as jnp
from jax import lax
from jax.sharding import PartitionSpec as P


def norm(value):
    mean = jnp.mean(value, axis=-1, keepdims=True)
    centred = value - mean
    variance = jnp.mean(centred * centred, axis=-1, keepdims=True)
    return centred * lax.rsqrt(variance + 1e-05)


def local(
    pair,
    length,
    chain,
    att_proj,
    att_bias,
    chain_bias,
    att_out,
    mult_in,
    mult_gate,
    mult_out,
    trans_up,
    trans_down,
):
    rows, cols, width = pair.shape
    row_count = lax.axis_size("row")
    sub_count = lax.axis_size("sub")
    row_index = lax.axis_index("row")
    col_index = lax.axis_index("col")
    sub_index = lax.axis_index("sub")
    total = rows * row_count
    half = cols // sub_count
    heads_here = att_bias.shape[1]
    spread = att_out.shape[0]
    head_dim = spread // heads_here
    mult_width = mult_out.shape[0]
    valid = (jnp.arange(total) < length[0]).astype(jnp.float32)
    normed = norm(pair.astype(jnp.float32)).astype(jnp.bfloat16)
    flat = normed.reshape(rows * cols, width)
    projected = jnp.dot(
        flat, att_proj.reshape(width, 4 * spread), preferred_element_type=jnp.float32
    ).reshape(rows, cols, 4, spread)
    query = (projected[:, :, 0] * head_dim ** (-0.5)).astype(jnp.bfloat16)
    keys = projected[:, :, 1].astype(jnp.bfloat16)
    values = projected[:, :, 2].astype(jnp.bfloat16)
    gating = jax.nn.sigmoid(projected[:, :, 3])
    bias_local = (
        jnp.dot(flat, att_bias, preferred_element_type=jnp.float32)
        .reshape(rows, cols, heads_here)
        .transpose(2, 0, 1)
    )
    keys_all, values_all = (
        lax.all_gather(keys, "col", axis=1, tiled=True),
        lax.all_gather(values, "col", axis=1, tiled=True),
    )
    column_bias = lax.all_gather(bias_local, "row", axis=1, tiled=True)
    bias_here = lax.all_to_all(column_bias, "col", split_axis=1, concat_axis=2, tiled=True)
    chain_here = lax.dynamic_slice_in_dim(chain, col_index * cols, cols, 0)
    same = (chain_here[:, None] == chain[None, :]).astype(jnp.float32)
    bias_here = (
        bias_here
        + chain_bias[:, None, None] * same[None]
        + (valid[None, None, :] - 1.0) * 1000000000.0
    )

    def attend(block):
        block_query, block_keys, block_values = block
        scores = (
            jnp.einsum(
                "ajhd,akhd->ahjk", block_query, block_keys, preferred_element_type=jnp.float32
            )
            + bias_here[None]
        )
        weights = jax.nn.softmax(scores, axis=-1).astype(jnp.bfloat16)
        return jnp.einsum(
            "ahjk,akhd->ajhd", weights, block_values, preferred_element_type=jnp.float32
        )

    attended = lax.map(
        attend,
        (
            query.reshape(rows // 2, 2, cols, heads_here, head_dim),
            keys_all.reshape(rows // 2, 2, total, heads_here, head_dim),
            values_all.reshape(rows // 2, 2, total, heads_here, head_dim),
        ),
    )
    attended = (attended.reshape(rows, cols, spread) * gating).astype(jnp.bfloat16)
    update = jnp.dot(
        attended.reshape(rows * cols, spread), att_out, preferred_element_type=jnp.float32
    ).reshape(rows, cols, width)
    update_half = lax.psum_scatter(
        update.astype(jnp.bfloat16), "sub", scatter_dimension=1, tiled=True
    ).astype(jnp.float32)
    pair_half = lax.dynamic_slice_in_dim(pair, sub_index * half, half, 1).astype(jnp.float32)
    first = pair_half + update_half
    mixed = norm(first).astype(jnp.bfloat16)
    mixed_flat = mixed.reshape(rows * half, width)
    quad = jnp.dot(mixed_flat, mult_in, preferred_element_type=jnp.float32).reshape(
        rows, half, 4, mult_width
    )
    row_valid = lax.dynamic_slice_in_dim(valid, row_index * rows, rows, 0)
    col_valid = lax.dynamic_slice_in_dim(valid, col_index * cols + sub_index * half, half, 0)
    outer = row_valid[:, None, None] * col_valid[None, :, None]
    left = (outer * jax.nn.sigmoid(quad[:, :, 1]) * quad[:, :, 0]).astype(jnp.bfloat16)
    right = (outer * jax.nn.sigmoid(quad[:, :, 3]) * quad[:, :, 2]).astype(jnp.bfloat16)
    gate_out = jax.nn.sigmoid(jnp.dot(mixed_flat, mult_gate, preferred_element_type=jnp.float32))
    partial_value = jnp.einsum(
        "ikc,jkc->ijc",
        left,
        lax.all_gather(right, "row", axis=0, tiled=True),
        preferred_element_type=jnp.float32,
    )
    tri = lax.psum_scatter(
        partial_value.astype(jnp.bfloat16), ("col", "sub"), scatter_dimension=1, tiled=True
    ).astype(jnp.float32)
    tri_normed = norm(tri).astype(jnp.bfloat16).reshape(rows * half, mult_width)
    second = first + (
        gate_out * jnp.dot(tri_normed, mult_out, preferred_element_type=jnp.float32)
    ).reshape(rows, half, width)
    last_normed = norm(second).astype(jnp.bfloat16).reshape(rows * half, width)
    hidden = jax.nn.relu(jnp.dot(last_normed, trans_up, preferred_element_type=jnp.float32)).astype(
        jnp.bfloat16
    )
    result = second + jnp.dot(hidden, trans_down, preferred_element_type=jnp.float32).reshape(
        rows, half, width
    )
    return result.astype(jnp.bfloat16)


def solution(mesh):
    placed = (
        P(("grp", "row"), "col", None),
        P("grp"),
        P("grp"),
        P(None, None, "sub"),
        P(None, "sub"),
        P("sub"),
        P("sub", None),
        P(),
        P(),
        P(),
        P(),
        P(),
    )
    return jax.shard_map(
        local,
        mesh=mesh,
        in_specs=placed,
        out_specs=P(("grp", "row"), ("col", "sub"), None),
        check_vma=False,
    )
```

profile of v0, /device:TPU:0, one launch (start us, length us, event | category | flops | bytes accessed | tf_op | source)
XLA Modules:
  0.0 124.0 jit_solution(8940343694213639194)
XLA Ops:
  6.5 1.0 convert_reduce_fusion
  7.6 1.1 fusion.21
  8.7 1.2 convolution_bitcast_fusion.1
  9.9 14.8 %all_gather.14 = f32[2,48,24]{2,0,1:T(2,128)S(1)} all-gather(f32[2,12,24]{2,0,1:T(2,128)S(1)} %convolution_bitcast_fusion.1), channel_id=1, replica_groups=mesh['grp'=2,'row'=4,'col'=2,'sub'=2] {'row'}, dimensions={1}, use_global_device_ids=true | all-gather | bytes 11520 | tf_op jit(solution)/shard_map/all_gather | solution.py:59
  24.6 0.7 reshape.214
  25.4 3.2 %all-to-all-start = ((f32[2,1,1152]{2,1,0:T(1,128)}), f32[2,1,1152]{2,1,0:T(1,128)S(1)}, u32[]{:S(2)}, u32[]{:S(2)}) async-start(f32[2,1,1152]{2,1,0:T(1,128)} %reshape.214), calls=%async_computation | async-start | bytes 18432 | tf_op jit(solution)/shard_map/all_to_all | solution.py:60
  28.7 0.7 dynamic_slice.24
  29.4 0.7 compare_convert_fusion
  30.8 1.2 fusion.72
  32.0 5.4 %all-gather = bf16[12,48,1,64]{3,1,2,0:T(8,128)(2,1)S(1)} all-gather(bf16[12,24,1,64]{3,1,2,0:T(8,128)(2,1)S(1)} %get-tuple-element.85), channel_id=2, replica_groups=mesh['grp'=2,'row'=4,'col'=2,'sub'=2] {'col'}, dimensions={1}, use_global_device_ids=true | all-gather | bytes 110592 | tf_op jit(solution)/shard_map/all_gather | solution.py:57
  37.6 5.2 %all-gather.1 = bf16[12,48,1,64]{3,1,2,0:T(8,128)(2,1)S(1)} all-gather(bf16[12,24,1,64]{3,1,2,0:T(8,128)(2,1)S(1)} %get-tuple-element.84), channel_id=3, replica_groups=mesh['grp'=2,'row'=4,'col'=2,'sub'=2] {'col'}, dimensions={1}, use_global_device_ids=true | all-gather | bytes 110592 | tf_op jit(solution)/shard_map/all_gather | solution.py:56
  42.8 0.1 copy.68
  42.9 0.2 copy.69
  43.1 0.1 convert_element_type.87
  43.2 0.5 broadcast.191
  43.7 0.7 reduce
  44.4 0.1 reshape.215
  44.6 0.1 all_to_all.16
  44.8 4.9 %while.10 = (s32[]{:T(128)}, f32[6,2,24,2,32]{4,3,2,1,0:T(2,128)S(1)}, bf16[6,2,48,2,32]{2,4,3,1,0:T(8,128)(2,1)S(1)}, bf16[6,2,24,2,32]{4,3,2,1,0:T(2,128)(2,1)...) while((s32[]{:T(128)}, f32[6,2,24,2,32]{4,3,2,1,0:T(2,128)S(1)}, ...), condition=%wide.region_5.6_spmd, body=%wide.region_2.5_spmd.sunk | while | flops 917184 | bytes 438753 | solution.py:82
  44.8 0.1 convolution_add_fusion.2
  45.0 0.3 fusion.93
  45.3 0.3 convolution_bitcast_fusion.3
  45.7 0.1 convolution_add_fusion.2
  45.8 0.3 fusion.93
  46.1 0.3 convolution_bitcast_fusion.3
  46.5 0.1 convolution_add_fusion.2
  46.6 0.3 fusion.93
  46.9 0.3 convolution_bitcast_fusion.3
  47.3 0.1 convolution_add_fusion.2
  47.4 0.3 fusion.93
  47.7 0.3 convolution_bitcast_fusion.3
  48.1 0.1 convolution_add_fusion.2
  48.2 0.3 fusion.93
  48.5 0.3 convolution_bitcast_fusion.3
  48.9 0.1 convolution_add_fusion.2
  49.0 0.3 fusion.93
  49.3 0.3 convolution_bitcast_fusion.3
  49.7 0.2 reshape.195
  49.9 0.8 convolution_convert_fusion.1
  50.8 0.1 copy.87
  51.0 0.6 dynamic-slice
  52.2 17.7 %all-reduce.3.cloned.1.call-done = bf16[12,24,128]{2,1,0:T(8,128)(2,1)} async-done(((bf16[12,24,128]{2,1,0:T(8,128)(2,1)}), bf16[12,24,128]{2,1,0:T(8,128)(2,1)}) %all-reduce.3.cloned.1.call-update) | async-done | bytes 73744
  69.9 1.0 fusion.52
  71.0 1.1 multiply_reduce_fusion.1
  72.1 1.0 multiply_convert_fusion.1
  73.1 0.2 fusion.57
  73.3 0.1 fusion.36
  73.4 14.1 %all_gather.15 = bf16[48,12,128]{2,1,0:T(8,128)(2,1)S(1)} all-gather(bf16[12,12,128]{2,1,0:T(8,128)(2,1)S(1)} %get-tuple-element.83), channel_id=1, replica_groups=mesh['grp'=2,'row'=4,'col'=2,'sub'=2] {'row'}, dimensions={0}, use_global_device_ids=true | all-gather | bytes 184320 | tf_op jit(solution)/shard_map/all_gather | solution.py:113
  87.5 1.0 copy.77
  88.5 0.5 copy.78
  89.0 0.9 fusion.13
  89.9 1.2 copy.79
  91.2 0.2 fusion.18
  91.4 20.9 %reduce-scatter.3.cloned.1.call-done = bf16[12,12,128]{2,0,1:T(8,128)(2,1)} async-done(((bf16[12,48,128]{2,0,1:T(8,128)(2,1)}), bf16[12,12,128]{2,0,1:T(8,128)(2,1)}) %reduce-scatter.3.cloned.1.call-update) | async-done | bytes 36880 | tf_op jit(solution)/shard_map/reduce_scatter | solution.py:116
  112.3 0.9 convert_reduce_fusion.1
  113.3 0.1 copy.81
  113.4 1.0 fusion.33
  114.6 0.9 fusion.34
  115.5 0.1 convolution_multiply_fusion
  115.7 0.1 fusion.65
  115.9 0.2 multiply_reduce_fusion
  116.1 0.1 multiply_convert_fusion
  116.2 0.3 fusion.15
  116.6 0.6 add_convert_fusion
  (63 shorter events, 1.3 us)
Async XLA Ops:
  6.5 109.7 %copy-start = (bf16[512,128]{1,0:T(8,128)(2,1)S(1)}, bf16[512,128]{1,0:T(8,128)(2,1)}, u32[]{:S(2)}) copy-start(bf16[512,128]{1,0:T(8,128)(2,1)} %param.25) | copy-start | bytes 393220
  25.4 17.8 %all-to-all-start = ((f32[2,1,1152]{2,1,0:T(1,128)}), f32[2,1,1152]{2,1,0:T(1,128)S(1)}, u32[]{:S(2)}, u32[]{:S(2)}) async-start(f32[2,1,1152]{2,1,0:T(1,128)} %reshape.214), calls=%async_computation | async-start | bytes 18432 | tf_op jit(solution)/shard_map/all_to_all | solution.py:60
  28.6 41.3 %all-reduce.3.cloned.1.call-start = ((), (), s32[]{:S(2)}) async-start(), calls=%async_computation.3 | async-start | bytes 147456
  30.8 13.9 %copy-start.6 = (f32[2]{0:T(128)S(1)}, f32[2]{0:T(128)}, u32[]{:S(2)}) copy-start(f32[2]{0:T(128)} %param.19) | copy-start | bytes 28
  44.8 5.1 %copy-start.8 = (bf16[64,128]{1,0:T(8,128)(2,1)S(1)}, bf16[64,128]{1,0:T(8,128)(2,1)}, u32[]{:S(2)}) copy-start(bf16[64,128]{1,0:T(8,128)(2,1)} %param.20) | copy-start | bytes 49156
  44.8 6.1 %copy-start.4 = (bf16[128,512]{1,0:T(8,128)(2,1)S(1)}, bf16[128,512]{1,0:T(8,128)(2,1)}, u32[]{:S(2)}) copy-start(bf16[128,512]{1,0:T(8,128)(2,1)} %param.21) | copy-start | bytes 393220
  44.8 6.2 %copy-start.9 = (u32[32]{0:T(128)S(1)}, u32[32]{0:T(128)}, u32[]{:S(2)}) copy-start(u32[32]{0:T(128)} %constant.70) | copy-start | bytes 388
  49.7 20.3 %copy-start.1 = (bf16[12,24,128]{2,1,0:T(8,128)(2,1)S(1)}, bf16[12,24,128]{2,1,0:T(8,128)(2,1)}, u32[]{:S(2)}) copy-start(bf16[12,24,128]{2,1,0:T(8,128)(2,1)} %param.14) | copy-start | bytes 221188
  50.7 61.6 %reduce-scatter.3.cloned.1.call-start = ((), (), s32[]{:S(2)}) async-start(), calls=%async_computation.2 | async-start | bytes 245760 | tf_op jit(solution)/shard_map/reduce_scatter | solution.py:116
  89.0 2.2 %copy-start.7 = (bf16[128,128]{1,0:T(8,128)(2,1)S(1)}, bf16[128,128]{1,0:T(8,128)(2,1)}, u32[]{:S(2)}) copy-start(bf16[128,128]{1,0:T(8,128)(2,1)} %param.22) | copy-start | bytes 98308
  89.9 25.7 %copy-start.5 = (bf16[128,128]{1,0:T(8,128)(2,1)S(1)}, bf16[128,128]{1,0:T(8,128)(2,1)}, u32[]{:S(2)}) copy-start(bf16[128,128]{1,0:T(8,128)(2,1)} %param.23) | copy-start | bytes 98308
  89.9 25.8 %copy-start.2 = (bf16[12,24,128]{2,1,0:T(8,128)(2,1)S(1)}, bf16[12,24,128]{2,1,0:T(8,128)(2,1)}, u32[]{:S(2)}) copy-start(bf16[12,24,128]{2,1,0:T(8,128)(2,1)} %all-reduce.3.cloned.1.call-done) | copy-start | bytes 221188
  89.9 26.3 %copy-start.3 = (bf16[128,512]{1,0:T(8,128)(2,1)S(1)}, bf16[128,512]{1,0:T(8,128)(2,1)}, u32[]{:S(2)}) copy-start(bf16[128,512]{1,0:T(8,128)(2,1)} %param.24) | copy-start | bytes 393220
Sparse Core Ops, SparseCore 0:
  50.8 19.0 all-reduce.2
  91.3 20.9 reduce-scatter.2
where the time goes:
time: 125 us; the launch traced here: 124 us
  blocking collectives  39.5 us (32%)
  waiting for transfers between devices  38.7 us (31%)
  between operations  15.2 us (12%)
  other arithmetic  10.7 us (9%)
  matrix products  9.25 us (7%)
  local copies, waits for them, and re-layouts  7.19 us (6%)
  starting transfers between devices  3.31 us (3%)
    reduce_scatter x1, waiting for transfers between devices, local(): lax.psum_scatter(partial_value.astype(jnp.bfloat16), ('col', 'sub'), scat...  20.9 us
    unnamed x3, waiting for transfers between devices  17.8 us
    all_gather x1, blocking collectives, local(): column_bias = lax.all_gather(bias_local, 'row', axis=1, tiled=True)  14.8 us
    all_gather x1, blocking collectives, local(): lax.all_gather(right, 'row', axis=0, tiled=True)  14.1 us
    all_gather x1, blocking collectives, local(): lax.all_gather(values, 'col', axis=1, tiled=True)  5.44 us
    all_gather x1, blocking collectives, local(): lax.all_gather(keys, 'col', axis=1, tiled=True)  5.2 us
    reduce_sum x4, other arithmetic, norm(): variance = jnp.mean(centred * centred, axis=-1, keepdims=True)  3.31 us
    all_to_all x1, starting transfers between devices, local(): lax.all_to_all(column_bias, 'col', split_axis=1, concat_axis=2, tiled=True)  3.23 us
  transfers between devices with their start and end apart: 3, of which 2 were waited for; matrix products, arithmetic and copies ran while one was open for 3% of the time, Pallas kernels for 0%

commit v1 on v0

--- a/solution.py
+++ b/solution.py
@@ -1,6 +1,10 @@
+import functools
+
 import jax
 import jax.numpy as jnp
 from jax import lax
+from jax.experimental import pallas as pl
+from jax.experimental.pallas import tpu as pltpu
 from jax.sharding import PartitionSpec as P
 
 
@@ -130,6 +134,302 @@
     return result.astype(jnp.bfloat16)
 
 
+NT = (((1,), (1,)), ((), ()))
+TN = (((0,), (0,)), ((), ()))
+F32 = jnp.float32
+BF16 = jnp.bfloat16
+STEPS = (((0, 1), (2, 1)), ((3, 1), (1, 1)), ((1, 0), (1, 0)), ((2, 0), (3, 0)))
+
+
+def replicated(mesh):
+    shape = mesh.shape
+    return shape["row"] == 4 and shape["col"] == 2 and shape["sub"] == 2
+
+
+def dot(left, right, dims=(((1,), (0,)), ((), ()))):
+    return lax.dot_general(left, right, dims, preferred_element_type=F32)
+
+
+def fused(
+    length_ref,
+    chain_bias_ref,
+    chain_ref,
+    own_ref,
+    *refs,
+    rows,
+    cols,
+    heads,
+    head_dim,
+    tokens,
+    sources,
+):
+    count = len(sources)
+    block_refs = refs[:count]
+    (
+        proj_own_ref,
+        proj_other_ref,
+        att_bias_ref,
+        out_own_ref,
+        out_other_ref,
+        mult_in_ref,
+        mult_gate_ref,
+        mult_out_ref,
+        trans_up_ref,
+        trans_down_ref,
+        result_ref,
+        normed_ref,
+        raw_ref,
+        turn_ref,
+        bias_ref,
+        left_ref,
+        right_ref,
+        first_ref,
+        tile_ref,
+    ) = refs[count:]
+    width = own_ref.shape[-1]
+    total = normed_ref.shape[0]
+    wide = normed_ref.shape[1]
+    row_index = lax.axis_index("row")
+    col_index = lax.axis_index("col")
+    sub_index = lax.axis_index("sub")
+    other_rows = col_index * lax.axis_size("sub") + sub_index
+    length = length_ref[0]
+
+    normed_ref[:, total:, :] = jnp.zeros((total, wide - total, width), F32)
+
+    def place(ref, row_block, col_block):
+        value = ref[...].astype(F32)
+        at = (pl.ds(row_block * rows, rows), pl.ds(pl.multiple_of(col_block * cols, 8), cols))
+        raw_ref[at[0], at[1], :] = value
+        normed_ref[at[0], at[1], :] = norm(value)
+
+    place(own_ref, row_index, col_index)
+    for ref, (row_step, col_step) in zip(block_refs, sources):
+        row_off = jnp.where(sub_index == 0, row_step[0], row_step[1])
+        col_off = jnp.where(sub_index == 0, col_step[0], col_step[1])
+        place(ref, row_index ^ row_off, col_index ^ col_off)
+
+    def pair_tokens(start):
+        return normed_ref[pl.ds(start, 2)].reshape(2 * wide, width).astype(BF16)
+
+    att_bias = att_bias_ref[...]
+    for index in range(total // 2):
+        both = dot(att_bias, pair_tokens(2 * index), NT)
+        turn_ref[2 * index] = both
+        turn_ref[2 * index + 1] = pltpu.roll(both, wide, 1)
+    chain_row = jnp.broadcast_to(chain_ref[...].astype(F32), (2 * wide, 2 * wide))
+    same = (chain_row == chain_row.T).astype(F32)[:total]
+    key_place = lax.broadcasted_iota(jnp.int32, (total, 2 * wide), 1)
+    masked = jnp.where(key_place < length, 0.0, -1000000000.0)
+    for head in range(heads):
+        value = turn_ref[:, head, :] + chain_bias_ref[head] * same + masked
+        value = jnp.concatenate([value, jnp.zeros((wide - total, 2 * wide), F32)], axis=0)
+        value = jnp.concatenate([value, value], axis=0).T
+        bias_ref[pl.ds(head * total, total)] = value[:total]
+
+    def joined(own, other, part):
+        return jnp.concatenate([own[part], other[part]], axis=0)
+
+    key_weights = joined(proj_own_ref, proj_other_ref, 1)
+    turned_weights = jnp.concatenate(
+        [joined(proj_own_ref, proj_other_ref, part) for part in (0, 2, 3)], axis=0
+    )
+    out_weights = jnp.concatenate([out_own_ref[...], out_other_ref[...]], axis=0)
+    lane = lax.broadcasted_iota(jnp.int32, (1, 2 * wide), 1)
+    lane_first = (lane < wide).astype(BF16)
+    lane_second = (lane >= wide).astype(BF16)
+    channel = lax.broadcasted_iota(jnp.int32, (1, width), 1)
+    head_masks = [
+        ((channel >= head * head_dim) & (channel < (head + 1) * head_dim)).astype(BF16)
+        for head in range(heads)
+    ]
+    pad = jnp.zeros((wide - total, 2 * wide), BF16)
+
+    def attend(start):
+        flat = pair_tokens(start)
+        turned = dot(turned_weights, flat, NT)
+        query = (turned[:width] * head_dim ** (-0.5)).astype(BF16)
+        values = turned[width : 2 * width].astype(BF16)
+        gating = jax.nn.sigmoid(turned[2 * width :])
+        keys = dot(flat, key_weights, NT).astype(BF16)
+        spread_keys = jnp.concatenate(
+            [
+                jnp.concatenate(
+                    [keys[at : at + total] * mask for mask in head_masks], axis=0
+                )
+                for at in (0, wide)
+            ],
+            axis=1,
+        )
+        spread_query = jnp.concatenate([query * lane_first, query * lane_second], axis=0)
+        scores = dot(spread_keys, spread_query) + bias_ref[...]
+        attended = []
+        for head in range(heads):
+            part = scores[head * total : (head + 1) * total]
+            part = jnp.exp(part - jnp.max(part, axis=0, keepdims=True))
+            weights = (part / jnp.sum(part, axis=0, keepdims=True)).astype(BF16)
+            spread_weights = jnp.concatenate(
+                [weights * lane_first, pad, weights * lane_second, pad], axis=0
+            )
+            attended.append(
+                dot(values[head * head_dim : (head + 1) * head_dim], spread_weights)
+            )
+        attended = (jnp.concatenate(attended, axis=0) * gating).astype(BF16)
+        update = dot(attended, out_weights, TN)
+        return raw_ref[pl.ds(start, 2)].reshape(2 * wide, width) + update
+
+    col_valid = (lax.broadcasted_iota(jnp.int32, (total, width), 0) < length).astype(F32)
+
+    def halves(start, step, first, into_ref, column):
+        mixed = norm(first).astype(BF16)
+        both = dot(mixed, mult_in_ref[:, column : column + 2 * width])
+        side = jax.nn.sigmoid(both[:, width:]) * both[:, :width]
+        for which in range(2):
+            row_valid = (start + which < length).astype(F32)
+            value = side[which * wide : which * wide + total] * (col_valid * row_valid)
+            into_ref[2 * step + which] = value.astype(BF16).astype(F32)
+
+    def own_step(step, carry):
+        start = row_index * rows + 2 * step
+        first = attend(start)
+        first_ref[pl.ds(2 * step, 2)] = first.reshape(2, wide, width)
+        halves(start, step, first, left_ref, 0)
+        return carry
+
+    def other_step(step, carry):
+        start = other_rows * rows + 2 * step
+        halves(start, step, attend(start), right_ref, 2 * width)
+        return carry
+
+    lax.fori_loop(0, rows // 2, own_step, 0)
+    lax.fori_loop(0, rows // 2, other_step, 0)
+
+    half = rows
+    for block in range(total // half):
+
+        @pl.when(other_rows == block)
+        def _():
+            tile_ref[:, :half, :] = first_ref[:, block * half : (block + 1) * half, :]
+
+    def triangle(step, carry):
+        left = left_ref[step]
+        sums = [
+            jnp.sum(left * right_ref[other], axis=0, keepdims=True) for other in range(half)
+        ]
+        first_ref[step, :half, :] = jnp.concatenate(sums, axis=0)
+        return carry
+
+    lax.fori_loop(0, rows, triangle, 0)
+    deep = tile_ref.shape[1]
+    first = tile_ref[...].reshape(rows * deep, width)
+    tri = first_ref[:, :deep, :].reshape(rows * deep, width)
+    mixed = norm(first).astype(BF16)
+    gate = jax.nn.sigmoid(dot(mixed, mult_gate_ref[...]))
+    second = first + gate * dot(norm(tri).astype(BF16), mult_out_ref[...])
+    hidden = jax.nn.relu(dot(norm(second).astype(BF16), trans_up_ref[...])).astype(BF16)
+    result = second + dot(hidden, trans_down_ref[...])
+    result_ref[...] = result.astype(BF16).reshape(rows, deep, width)[:, :half, :]
+
+
+def gathered(
+    pair,
+    length,
+    chain,
+    att_proj,
+    att_bias,
+    chain_bias,
+    att_out,
+    mult_in,
+    mult_gate,
+    mult_out,
+    trans_up,
+    trans_down,
+):
+    rows, cols, width = pair.shape
+    row_count = lax.axis_size("row")
+    col_count = lax.axis_size("col")
+    sub_count = lax.axis_size("sub")
+    total = rows * row_count
+    heads = att_bias.shape[1] * sub_count
+    head_dim = att_out.shape[0] // att_bias.shape[1]
+    axes = ("row", "col", "sub")
+
+    def place(row, col, sub):
+        return (row * col_count + col) * sub_count + sub
+
+    def exchange(value, offsets):
+        routes = [
+            (place(row, col, sub), place(row ^ offsets[sub][0], col ^ offsets[sub][1], sub))
+            for row in range(row_count)
+            for col in range(col_count)
+            for sub in range(sub_count)
+        ]
+        return lax.ppermute(value, axes, routes)
+
+    swap = functools.partial(lax.ppermute, axis_name="sub", perm=[(0, 1), (1, 0)])
+    proj_other = swap(att_proj)
+    out_other = swap(att_out)
+    bias_other = swap(att_bias)
+    chain_other = swap(chain_bias)
+    blocks, sources = [], []
+    fetched = [exchange(pair, offsets) for offsets in STEPS]
+    for value, offsets in zip(fetched, STEPS):
+        mine = tuple(zip(offsets[0], offsets[1]))
+        blocks.append(value)
+        sources.append(mine)
+        if offsets[0] != offsets[1]:
+            blocks.append(swap(value))
+            sources.append(tuple((b, a) for a, b in mine))
+    att_bias_rows = jnp.concatenate([att_bias.T, bias_other.T], axis=0)
+    att_bias_rows = jnp.pad(att_bias_rows, ((0, 8 - heads), (0, 0)))
+    wide = 64
+    deep = 16
+    smem = pl.BlockSpec(memory_space=pltpu.SMEM)
+    vmem = pl.BlockSpec(memory_space=pltpu.VMEM)
+    operands = [
+        length,
+        jnp.concatenate([chain_bias, chain_other]),
+        jnp.pad(chain, (0, 2 * wide - total)).reshape(1, 2 * wide),
+        pair,
+        *blocks,
+        att_proj.transpose(1, 2, 0),
+        proj_other.transpose(1, 2, 0),
+        att_bias_rows,
+        att_out,
+        out_other,
+        mult_in,
+        mult_gate,
+        mult_out,
+        trans_up,
+        trans_down,
+    ]
+    return pl.pallas_call(
+        functools.partial(
+            fused,
+            rows=rows,
+            cols=cols,
+            heads=heads,
+            head_dim=head_dim,
+            tokens=wide,
+            sources=tuple(sources),
+        ),
+        out_shape=jax.ShapeDtypeStruct((rows, cols // sub_count, width), jnp.bfloat16),
+        in_specs=[smem, smem] + [vmem] * (len(operands) - 2),
+        out_specs=vmem,
+        scratch_shapes=[
+            pltpu.VMEM((total, wide, width), F32),
+            pltpu.VMEM((total, wide, width), F32),
+            pltpu.VMEM((total, 8, 2 * wide), F32),
+            pltpu.VMEM((heads * total, 2 * wide), F32),
+            pltpu.VMEM((rows, total, width), F32),
+            pltpu.VMEM((rows, total, width), F32),
+            pltpu.VMEM((rows, wide, width), F32),
+            pltpu.VMEM((rows, deep, width), F32),
+        ],
+        compiler_params=pltpu.CompilerParams(vmem_limit_bytes=48 * 1024 * 1024),
+    )(*operands)
+
+
 def solution(mesh):
     placed = (
         P(("grp", "row"), "col", None),
@@ -145,8 +445,9 @@
         P(),
         P(),
     )
+    fits = replicated(mesh)
     return jax.shard_map(
-        local,
+        gathered if fits else local,
         mesh=mesh,
         in_specs=placed,
         out_specs=P(("grp", "row"), ("col", "sub"), None),

time: 125 us -> 36.9 us (0.30)
  blocking collectives: 39.5 us -> 0 us
  waiting for transfers between devices: 38.7 us -> 3.81 us
  Pallas kernels: 0 us -> 15.7 us
  between operations: 15.2 us -> 0.67 us
  other arithmetic: 10.7 us -> 1.39 us
  matrix products: 9.25 us -> 0 us
  starting transfers between devices: 3.31 us -> 8.23 us
    all_gather x4 -> x0, blocking collectives: 39.5 us -> none  [the longest x1 14.8 us: local(): column_bias = lax.all_gather(bias_local, 'row', axis=1, tiled=True)]
    reduce_scatter x1 -> x0, waiting for transfers between devices: 20.9 us -> none  [local(): lax.psum_scatter(partial_value.astype(jnp.bfloat16), ('col', 'sub'), scat...]
    unnamed x3 -> x0, waiting for transfers between devices: 17.8 us -> none
    pallas_call x0 -> x1, Pallas kernels: none -> 15.7 us  [gathered(): pl.pallas_call(functools.partial(fused, rows=rows, cols=cols, heads=heads...]
    ppermute x0 -> x11, starting transfers between devices: none -> 8.23 us  [the longest x4 7.2 us: exchange(): return lax.ppermute(value, axes, routes)]
    dot_general x20 -> x0, matrix products: 7.41 us -> none  [the longest x6 1.67 us: attend(): jnp.einsum('ahjk,akhd->ajhd', weights, block_values, preferred_element_ty...]
    reduce_sum x8 -> x0, other arithmetic: 6.33 us -> none  [the longest x4 3.31 us: norm(): variance = jnp.mean(centred * centred, axis=-1, keepdims=True)]
    unnamed x23 -> x16, local copies, waits for them, and re-layouts: 1.51 us -> 5.95 us
  transfers between devices with their start and end apart: 3 -> 11, of which waited for: 2 -> 4; matrix products, arithmetic and copies ran while one was open for 3% -> 6% of each run, Pallas kernels for 0% -> 0%
where the time goes in v1:
time: 36.9 us; the launch traced here: 36.4 us
  Pallas kernels  15.7 us (43%)
  starting transfers between devices  8.23 us (22%)
  local copies, waits for them, and re-layouts  6.61 us (18%)
  waiting for transfers between devices  3.81 us (10%)
  other arithmetic  1.39 us (4%)
  between operations  0.67 us (2%)
    pallas_call x1, Pallas kernels, gathered(): pl.pallas_call(functools.partial(fused, rows=rows, cols=cols, heads=heads...  15.7 us
    ppermute x4, starting transfers between devices, exchange(): return lax.ppermute(value, axes, routes)  7.2 us
    unnamed x16, local copies, waits for them, and re-layouts  5.95 us
    ppermute x4, waiting for transfers between devices, exchange(): return lax.ppermute(value, axes, routes)  3.58 us
  transfers between devices with their start and end apart: 11, of which 4 were waited for; matrix products, arithmetic and copies ran while one was open for 6% of the time, Pallas kernels for 0%

profile of v1, /device:TPU:0, one launch (start us, length us, event | category | flops | bytes accessed | tf_op | source)
XLA Modules:
  0.0 36.4 jit_solution(12711592311966331552)
XLA Ops:
  0.0 0.0 copy-start.7
  0.0 6.0 %collective-permute-start.3 = (bf16[12,24,128]{2,1,0:T(8,128)(2,1)}, bf16[12,24,128]{2,1,0:T(8,128)(2,1)S(1)}, u32[]{:S(2)}, u32[]{:S(2)}) collective-permute-start(bf16[12,24,128]{2,1,0:T(8,128)(2,1)} %own_ref.1), channel_id=1, source_target_pairs={{0,14},{1,7},{2,12},{3,5},{4,10},{5,3},{6,8},{7,1},{8,6},{9,15},{1... | collective-permute-start | bytes 221192 | tf_op jit(solution)/shard_map/ppermute | solution.py:367
  6.0 0.5 %collective-permute-start.1 = (bf16[12,24,128]{2,1,0:T(8,128)(2,1)}, bf16[12,24,128]{2,1,0:T(8,128)(2,1)S(1)}, u32[]{:S(2)}, u32[]{:S(2)}) collective-permute-start(bf16[12,24,128]{2,1,0:T(8,128)(2,1)} %own_ref.1), channel_id=1, source_target_pairs={{0,2},{1,11},{2,0},{3,9},{4,6},{5,15},{6,4},{7,13},{8,10},{9,3},{1... | collective-permute-start | bytes 221192 | tf_op jit(solution)/shard_map/ppermute | solution.py:367
  6.5 0.0 collective-permute-start.6
  6.5 0.0 collective-permute-start.9
  6.5 0.5 %collective-permute-start = (f32[2]{0:T(128)}, f32[2]{0:T(128)S(1)}, u32[]{:S(2)}, u32[]{:S(2)}) collective-permute-start(f32[2]{0:T(128)} %param.17), channel_id=1, source_target_pairs={{0,1},{1,0},{2,3},{3,2},{4,5},{5,4},{6,7},{7,6},{8,9},{9,8},{10,11... | collective-permute-start | bytes 32 | tf_op jit(solution)/shard_map/ppermute | solution.py:373
  7.7 0.7 %pad_bitcast_fusion.chain_ref = s32[1,128]{1,0:T(1,128)S(1)} fusion(s32[48]{0:T(128)} %param.14), kind=kLoop, calls=%fused_computation.5 | loop fusion | bytes 704 | tf_op jit(solution)/shard_map/reshape | solution.py:392
  8.4 0.0 collective-permute-done
  8.4 0.0 collective-permute-start.10
  8.4 0.7 %pad_maximum_fusion.chain_bias_ref = f32[4]{0:T(128)S(1)} fusion(f32[2]{0:T(128)S(1)} %collective-permute-done, f32[2]{0:T(128)} %param.17), kind=kLoop, calls=%fused_computation.4 | loop fusion | flops 4 | bytes 32 | tf_op jit(solution)/shard_map/concatenate | solution.py:391
  9.1 0.0 collective-permute-done.9
  9.1 0.7 %collective-permute-start.5 = (bf16[12,24,128]{2,1,0:T(8,128)(2,1)}, bf16[12,24,128]{2,1,0:T(8,128)(2,1)S(1)}, u32[]{:S(2)}, u32[]{:S(2)}) collective-permute-start(bf16[12,24,128]{2,1,0:T(8,128)(2,1)} %own_ref.1), channel_id=1, source_target_pairs={{0,4},{1,5},{2,6},{3,7},{4,0},{5,1},{6,2},{7,3},{8,12},{9,13},{10,... | collective-permute-start | bytes 221192 | tf_op jit(solution)/shard_map/ppermute | solution.py:367
  9.8 0.0 collective-permute-done.10.refs_11_
  9.8 0.2 collective-permute-start.8
  10.0 0.0 collective-permute-done.3.refs_2_
  10.0 0.3 collective-permute-start.4
  10.3 0.8 %collective-permute-done.1.refs_0_ = bf16[12,24,128]{2,1,0:T(8,128)(2,1)S(1)} collective-permute-done((bf16[12,24,128]{2,1,0:T(8,128)(2,1)}, bf16[12,24,128]{2,1,0:T(8,128)(2,1)S(1)}, u32[]{:S(2)}, u32[]{:S(2)}) %collective-permute-start.1) | collective-permute-done | bytes 73760 | tf_op jit(solution)/shard_map/ppermute | solution.py:367
  11.1 0.0 collective-permute-start.2
  11.1 2.4 %collective-permute-done.6.refs_5_ = bf16[12,24,128]{2,1,0:T(8,128)(2,1)S(1)} collective-permute-done((bf16[12,24,128]{2,1,0:T(8,128)(2,1)}, bf16[12,24,128]{2,1,0:T(8,128)(2,1)S(1)}, u32[]{:S(2)}, u32[]{:S(2)}) %collective-permute-start.6) | collective-permute-done | bytes 73760 | tf_op jit(solution)/shard_map/ppermute | solution.py:367
  13.5 0.0 collective-permute-start.7
  13.5 0.7 %fusion.2.refs_9_ = bf16[8,128]{1,0:T(8,128)(2,1)S(1)} fusion(bf16[2,128]{1,0:T(2,128)(2,1)S(1)} %bitcast.9, bf16[2,128]{1,0:T(2,128)(2,1)} %bitcast.8), kind=kLoop, calls=%fused_computation.3 | loop fusion | flops 7168 | bytes 3072 | tf_op jit(solution)/shard_map/concatenate | solution.py:383
  14.2 0.0 collective-permute-done.8
  14.2 0.4 %collective-permute-done.5.refs_4_ = bf16[12,24,128]{2,1,0:T(8,128)(2,1)S(1)} collective-permute-done((bf16[12,24,128]{2,1,0:T(8,128)(2,1)}, bf16[12,24,128]{2,1,0:T(8,128)(2,1)S(1)}, u32[]{:S(2)}, u32[]{:S(2)}) %collective-permute-start.5) | collective-permute-done | bytes 73760 | tf_op jit(solution)/shard_map/ppermute | solution.py:367
  14.5 0.0 collective-permute-done.4.refs_3_
  14.5 0.0 collective-permute-done.2.refs_1_
  14.5 0.2 collective-permute-done.7.refs_6_
  14.8 0.0 copy-done.7
  14.8 0.0 copy-start
  14.8 0.9 %copy-done = bf16[128,512]{1,0:T(8,128)(2,1)S(1)} copy-done((bf16[128,512]{1,0:T(8,128)(2,1)S(1)}, bf16[128,512]{1,0:T(8,128)(2,1)}, u32[]{:S(2)}) %copy-start) | copy-done | bytes 131096
  15.7 0.0 copy-start.1
  15.7 0.9 %copy-done.1 = bf16[128,512]{1,0:T(8,128)(2,1)S(1)} copy-done((bf16[128,512]{1,0:T(8,128)(2,1)S(1)}, bf16[128,512]{1,0:T(8,128)(2,1)}, u32[]{:S(2)}) %copy-start.1) | copy-done | bytes 131096
  16.6 0.0 copy-start.2
  16.6 0.9 %copy-done.2 = bf16[512,128]{1,0:T(8,128)(2,1)S(1)} copy-done((bf16[512,128]{1,0:T(8,128)(2,1)S(1)}, bf16[512,128]{1,0:T(8,128)(2,1)}, u32[]{:S(2)}) %copy-start.2) | copy-done | bytes 131096
  17.5 0.0 copy-start.3
  17.5 0.9 %copy-done.3 = bf16[12,24,128]{2,1,0:T(8,128)(2,1)S(1)} copy-done((bf16[12,24,128]{2,1,0:T(8,128)(2,1)S(1)}, bf16[12,24,128]{2,1,0:T(8,128)(2,1)}, u32[]{:S(2)}) %copy-start.3) | copy-done | bytes 73752
  18.4 0.0 copy-start.4
  18.4 0.8 %copy-done.4 = bf16[128,4,64]{0,2,1:T(8,128)(2,1)S(1)} copy-done((bf16[128,4,64]{0,2,1:T(8,128)(2,1)S(1)}, bf16[128,4,64]{0,2,1:T(8,128)(2,1)}, u32[]{:S(2)}) %copy-start.4) | copy-done | bytes 65560
  19.2 0.0 copy-start.5
  19.2 0.8 %copy-done.5 = bf16[128,128]{1,0:T(8,128)(2,1)S(1)} copy-done((bf16[128,128]{1,0:T(8,128)(2,1)S(1)}, bf16[128,128]{1,0:T(8,128)(2,1)}, u32[]{:S(2)}) %copy-start.5) | copy-done | bytes 32792
  20.0 0.0 copy-start.6
  20.0 0.8 %copy-done.6 = bf16[128,128]{1,0:T(8,128)(2,1)S(1)} copy-done((bf16[128,128]{1,0:T(8,128)(2,1)S(1)}, bf16[128,128]{1,0:T(8,128)(2,1)}, u32[]{:S(2)}) %copy-start.6) | copy-done | bytes 32792
  20.7 15.7 %shard_map.118 = bf16[12,12,128]{2,1,0:T(8,128)(2,1)} custom-call(s32[1]{0:T(128)S(6)} %copy.13.length_ref, f32[4]{0:T(128)S(1)} %pad_maximum_fusion.chain_bias_ref, s32[1,128]{1,0:T(1,128)S(1)} %pad_bitcast_fusion.chain_ref, bf16[12,24,128]{2,1,0:T(8,128)(2,1)S(1)} %copy-done.3, bf16[12,24,128]{2,1,0:T(8,128)(2,1)S(1)} %collective-permute-done.1.refs_0_, ...), custom_call_target="tpu_custom_call" | custom-call | tf_op jit(solution)/shard_map/pallas_call | solution.py:406
Async XLA Ops:
  0.0 14.8 %copy-start.7 = (bf16[64,128]{1,0:T(8,128)(2,1)S(1)}, bf16[64,128]{1,0:T(8,128)(2,1)}, u32[]{:S(2)}) copy-start(bf16[64,128]{1,0:T(8,128)(2,1)} %refs_10_.1) | copy-start | bytes 49156
  0.0 10.0 %collective-permute-start.3 = (bf16[12,24,128]{2,1,0:T(8,128)(2,1)}, bf16[12,24,128]{2,1,0:T(8,128)(2,1)S(1)}, u32[]{:S(2)}, u32[]{:S(2)}) collective-permute-start(bf16[12,24,128]{2,1,0:T(8,128)(2,1)} %own_ref.1), channel_id=1, source_target_pairs={{0,14},{1,7},{2,12},{3,5},{4,10},{5,3},{6,8},{7,1},{8,6},{9,15},{1... | collective-permute-start | bytes 221192 | tf_op jit(solution)/shard_map/ppermute | solution.py:367
  6.0 5.1 %collective-permute-start.1 = (bf16[12,24,128]{2,1,0:T(8,128)(2,1)}, bf16[12,24,128]{2,1,0:T(8,128)(2,1)S(1)}, u32[]{:S(2)}, u32[]{:S(2)}) collective-permute-start(bf16[12,24,128]{2,1,0:T(8,128)(2,1)} %own_ref.1), channel_id=1, source_target_pairs={{0,2},{1,11},{2,0},{3,9},{4,6},{5,15},{6,4},{7,13},{8,10},{9,3},{1... | collective-permute-start | bytes 221192 | tf_op jit(solution)/shard_map/ppermute | solution.py:367
  6.5 6.9 %collective-permute-start.6 = (bf16[12,24,128]{2,1,0:T(8,128)(2,1)}, bf16[12,24,128]{2,1,0:T(8,128)(2,1)S(1)}, u32[]{:S(2)}, u32[]{:S(2)}) collective-permute-start(bf16[12,24,128]{2,1,0:T(8,128)(2,1)} %own_ref.1), channel_id=1, source_target_pairs={{0,8},{1,13},{2,10},{3,15},{4,12},{5,9},{6,14},{7,11},{8,0},{9,5},... | collective-permute-start | bytes 221192 | tf_op jit(solution)/shard_map/ppermute | solution.py:367
  6.5 2.6 %collective-permute-start.9 = (bf16[128,2]{0,1:T(2,128)(2,1)}, bf16[128,2]{0,1:T(2,128)(2,1)S(1)}, u32[]{:S(2)}, u32[]{:S(2)}) collective-permute-start(bf16[128,2]{0,1:T(2,128)(2,1)} %param.16), channel_id=1, source_target_pairs={{0,1},{1,0},{2,3},{3,2},{4,5},{5,4},{6,7},{7,6},{8,9},{9,8},{10,11... | collective-permute-start | bytes 1544 | tf_op jit(solution)/shard_map/ppermute | solution.py:372
  6.5 1.8 %collective-permute-start = (f32[2]{0:T(128)}, f32[2]{0:T(128)S(1)}, u32[]{:S(2)}, u32[]{:S(2)}) collective-permute-start(f32[2]{0:T(128)} %param.17), channel_id=1, source_target_pairs={{0,1},{1,0},{2,3},{3,2},{4,5},{5,4},{6,7},{7,6},{8,9},{9,8},{10,11... | collective-permute-start | bytes 32 | tf_op jit(solution)/shard_map/ppermute | solution.py:373
  8.4 1.4 %collective-permute-start.10 = (bf16[64,128]{1,0:T(8,128)(2,1)}, bf16[64,128]{1,0:T(8,128)(2,1)S(1)}, u32[]{:S(2)}, u32[]{:S(2)}) collective-permute-start(bf16[64,128]{1,0:T(8,128)(2,1)} %refs_10_.1), channel_id=1, source_target_pairs={{0,1},{1,0},{2,3},{3,2},{4,5},{5,4},{6,7},{7,6},{8,9},{9,8},{10,11... | collective-permute-start | bytes 49160 | tf_op jit(solution)/shard_map/ppermute | solution.py:371
  9.1 5.4 %collective-permute-start.5 = (bf16[12,24,128]{2,1,0:T(8,128)(2,1)}, bf16[12,24,128]{2,1,0:T(8,128)(2,1)S(1)}, u32[]{:S(2)}, u32[]{:S(2)}) collective-permute-start(bf16[12,24,128]{2,1,0:T(8,128)(2,1)} %own_ref.1), channel_id=1, source_target_pairs={{0,4},{1,5},{2,6},{3,7},{4,0},{5,1},{6,2},{7,3},{8,12},{9,13},{10,... | collective-permute-start | bytes 221192 | tf_op jit(solution)/shard_map/ppermute | solution.py:367
  9.8 4.4 %collective-permute-start.8 = (bf16[128,4,64]{0,2,1:T(8,128)(2,1)}, bf16[128,4,64]{0,2,1:T(8,128)(2,1)S(1)}, u32[]{:S(2)}, u32[]{:S(2)}) collective-permute-start(bf16[128,4,64]{0,2,1:T(8,128)(2,1)} %param.15), channel_id=1, source_target_pairs={{0,1},{1,0},{2,3},{3,2},{4,5},{5,4},{6,7},{7,6},{8,9},{9,8},{10,11... | collective-permute-start | bytes 196616 | tf_op jit(solution)/shard_map/ppermute | solution.py:370
  10.0 4.5 %collective-permute-start.4 = (bf16[12,24,128]{2,1,0:T(8,128)(2,1)S(1)}, bf16[12,24,128]{2,1,0:T(8,128)(2,1)S(1)}, u32[]{:S(2)}, u32[]{:S(2)}) collective-permute-start(bf16[12,24,128]{2,1,0:T(8,128)(2,1)S(1)} %collective-permute-done.3.refs_2_), channel_id=1, source_target_pairs={{0,1},{1,0},{2,3},{3,2},{4,5},{5,4},{6,7},{7,6},{8,9},{9,8},{10,11... | collective-permute-start | bytes 221192 | tf_op jit(solution)/shard_map/ppermute | solution.py:381
  11.1 3.4 %collective-permute-start.2 = (bf16[12,24,128]{2,1,0:T(8,128)(2,1)S(1)}, bf16[12,24,128]{2,1,0:T(8,128)(2,1)S(1)}, u32[]{:S(2)}, u32[]{:S(2)}) collective-permute-start(bf16[12,24,128]{2,1,0:T(8,128)(2,1)S(1)} %collective-permute-done.1.refs_0_), channel_id=1, source_target_pairs={{0,1},{1,0},{2,3},{3,2},{4,5},{5,4},{6,7},{7,6},{8,9},{9,8},{10,11... | collective-permute-start | bytes 221192 | tf_op jit(solution)/shard_map/ppermute | solution.py:381
  13.5 1.3 %collective-permute-start.7 = (bf16[12,24,128]{2,1,0:T(8,128)(2,1)S(1)}, bf16[12,24,128]{2,1,0:T(8,128)(2,1)S(1)}, u32[]{:S(2)}, u32[]{:S(2)}) collective-permute-start(bf16[12,24,128]{2,1,0:T(8,128)(2,1)S(1)} %collective-permute-done.6.refs_5_), channel_id=1, source_target_pairs={{0,1},{1,0},{2,3},{3,2},{4,5},{5,4},{6,7},{7,6},{8,9},{9,8},{10,11... | collective-permute-start | bytes 221192 | tf_op jit(solution)/shard_map/ppermute | solution.py:381
  14.8 0.9 %copy-start = (bf16[128,512]{1,0:T(8,128)(2,1)S(1)}, bf16[128,512]{1,0:T(8,128)(2,1)}, u32[]{:S(2)}) copy-start(bf16[128,512]{1,0:T(8,128)(2,1)} %refs_12_.1) | copy-start | bytes 393220
  15.7 0.9 %copy-start.1 = (bf16[128,512]{1,0:T(8,128)(2,1)S(1)}, bf16[128,512]{1,0:T(8,128)(2,1)}, u32[]{:S(2)}) copy-start(bf16[128,512]{1,0:T(8,128)(2,1)} %refs_15_.1) | copy-start | bytes 393220
  16.6 0.9 %copy-start.2 = (bf16[512,128]{1,0:T(8,128)(2,1)S(1)}, bf16[512,128]{1,0:T(8,128)(2,1)}, u32[]{:S(2)}) copy-start(bf16[512,128]{1,0:T(8,128)(2,1)} %refs_16_.1) | copy-start | bytes 393220
  17.5 0.9 %copy-start.3 = (bf16[12,24,128]{2,1,0:T(8,128)(2,1)S(1)}, bf16[12,24,128]{2,1,0:T(8,128)(2,1)}, u32[]{:S(2)}) copy-start(bf16[12,24,128]{2,1,0:T(8,128)(2,1)} %own_ref.1) | copy-start | bytes 221188
  18.4 0.8 %copy-start.4 = (bf16[128,4,64]{0,2,1:T(8,128)(2,1)S(1)}, bf16[128,4,64]{0,2,1:T(8,128)(2,1)}, u32[]{:S(2)}) copy-start(bf16[128,4,64]{0,2,1:T(8,128)(2,1)} %param.15) | copy-start | bytes 196612
  19.2 0.8 %copy-start.5 = (bf16[128,128]{1,0:T(8,128)(2,1)S(1)}, bf16[128,128]{1,0:T(8,128)(2,1)}, u32[]{:S(2)}) copy-start(bf16[128,128]{1,0:T(8,128)(2,1)} %refs_13_.1) | copy-start | bytes 98308
  20.0 0.8 %copy-start.6 = (bf16[128,128]{1,0:T(8,128)(2,1)S(1)}, bf16[128,128]{1,0:T(8,128)(2,1)}, u32[]{:S(2)}) copy-start(bf16[128,128]{1,0:T(8,128)(2,1)} %refs_14_.1) | copy-start | bytes 98308

commit v2 on v1

--- a/solution.py
+++ b/solution.py
@@ -138,6 +138,7 @@
 TN = (((0,), (0,)), ((), ()))
 F32 = jnp.float32
 BF16 = jnp.bfloat16
+UNROLL = 6
 STEPS = (((0, 1), (2, 1)), ((3, 1), (1, 1)), ((1, 0), (1, 0)), ((2, 0), (3, 0)))
 
 
@@ -171,12 +172,14 @@
         att_bias_ref,
         out_own_ref,
         out_other_ref,
+        *kept_refs,
+        result_ref,
         mult_in_ref,
         mult_gate_ref,
         mult_out_ref,
         trans_up_ref,
         trans_down_ref,
-        result_ref,
+        copy_sems,
         normed_ref,
         raw_ref,
         turn_ref,
@@ -186,6 +189,17 @@
         first_ref,
         tile_ref,
     ) = refs[count:]
+    copies = [
+        pltpu.make_async_copy(kept, held, copy_sems.at[at])
+        for at, (kept, held) in enumerate(
+            zip(
+                kept_refs,
+                (mult_in_ref, mult_gate_ref, mult_out_ref, trans_up_ref, trans_down_ref),
+            )
+        )
+    ]
+    for copy in copies:
+        copy.start()
     width = own_ref.shape[-1]
     total = normed_ref.shape[0]
     wide = normed_ref.shape[1]
@@ -245,38 +259,45 @@
     ]
     pad = jnp.zeros((wide - total, 2 * wide), BF16)
 
-    def attend(start):
-        flat = pair_tokens(start)
-        turned = dot(turned_weights, flat, NT)
-        query = (turned[:width] * head_dim ** (-0.5)).astype(BF16)
-        values = turned[width : 2 * width].astype(BF16)
-        gating = jax.nn.sigmoid(turned[2 * width :])
-        keys = dot(flat, key_weights, NT).astype(BF16)
-        spread_keys = jnp.concatenate(
-            [
-                jnp.concatenate(
-                    [keys[at : at + total] * mask for mask in head_masks], axis=0
+    def attend(starts):
+        flats = [pair_tokens(start) for start in starts]
+        turned = [dot(turned_weights, flat, NT) for flat in flats]
+        keys = [dot(flat, key_weights, NT).astype(BF16) for flat in flats]
+        scores = []
+        for key, turn in zip(keys, turned):
+            query = (turn[:width] * head_dim ** (-0.5)).astype(BF16)
+            spread_keys = jnp.concatenate(
+                [
+                    jnp.concatenate(
+                        [key[at : at + total] * mask for mask in head_masks], axis=0
+                    )
+                    for at in (0, wide)
+                ],
+                axis=1,
+            )
+            spread_query = jnp.concatenate([query * lane_first, query * lane_second], axis=0)
+            scores.append(dot(spread_keys, spread_query))
+        attended = []
+        for score, turn in zip(scores, turned):
+            values = turn[width : 2 * width].astype(BF16)
+            parts = []
+            for head in range(heads):
+                rows_of = slice(head * total, (head + 1) * total)
+                part = score[rows_of] + bias_ref[rows_of]
+                part = jnp.exp(part - jnp.max(part, axis=0, keepdims=True))
+                weights = (part / jnp.sum(part, axis=0, keepdims=True)).astype(BF16)
+                spread_weights = jnp.concatenate(
+                    [weights * lane_first, pad, weights * lane_second, pad], axis=0
                 )
-                for at in (0, wide)
-            ],
-            axis=1,
-        )
-        spread_query = jnp.concatenate([query * lane_first, query * lane_second], axis=0)
-        scores = dot(spread_keys, spread_query) + bias_ref[...]
-        attended = []
-        for head in range(heads):
-            part = scores[head * total : (head + 1) * total]
-            part = jnp.exp(part - jnp.max(part, axis=0, keepdims=True))
-            weights = (part / jnp.sum(part, axis=0, keepdims=True)).astype(BF16)
-            spread_weights = jnp.concatenate(
-                [weights * lane_first, pad, weights * lane_second, pad], axis=0
-            )
-            attended.append(
-                dot(values[head * head_dim : (head + 1) * head_dim], spread_weights)
-            )
-        attended = (jnp.concatenate(attended, axis=0) * gating).astype(BF16)
-        update = dot(attended, out_weights, TN)
-        return raw_ref[pl.ds(start, 2)].reshape(2 * wide, width) + update
+                parts.append(
+                    dot(values[head * head_dim : (head + 1) * head_dim], spread_weights)
+                )
+            gating = jax.nn.sigmoid(turn[2 * width :])
+            attended.append((jnp.concatenate(parts, axis=0) * gating).astype(BF16))
+        return [
+            raw_ref[pl.ds(start, 2)].reshape(2 * wide, width) + dot(value, out_weights, TN)
+            for start, value in zip(starts, attended)
+        ]
 
     col_valid = (lax.broadcasted_iota(jnp.int32, (total, width), 0) < length).astype(F32)
 
@@ -289,20 +310,21 @@
             value = side[which * wide : which * wide + total] * (col_valid * row_valid)
             into_ref[2 * step + which] = value.astype(BF16).astype(F32)
 
-    def own_step(step, carry):
-        start = row_index * rows + 2 * step
-        first = attend(start)
-        first_ref[pl.ds(2 * step, 2)] = first.reshape(2, wide, width)
-        halves(start, step, first, left_ref, 0)
+    def group(step, carry):
+        steps = [step * UNROLL + at for at in range(UNROLL)]
+        own = [row_index * rows + 2 * at for at in steps]
+        others = [other_rows * rows + 2 * at for at in steps]
+        firsts = attend(own + others)
+        for at, start, first in zip(steps, own, firsts):
+            first_ref[pl.ds(2 * at, 2)] = first.reshape(2, wide, width)
+            halves(start, at, first, left_ref, 0)
+        for at, start, first in zip(steps, others, firsts[UNROLL:]):
+            halves(start, at, first, right_ref, 2 * width)
         return carry
 
-    def other_step(step, carry):
-        start = other_rows * rows + 2 * step
-        halves(start, step, attend(start), right_ref, 2 * width)
-        return carry
-
-    lax.fori_loop(0, rows // 2, own_step, 0)
-    lax.fori_loop(0, rows // 2, other_step, 0)
+    for copy in copies[:1]:
+        copy.wait()
+    lax.fori_loop(0, rows // 2 // UNROLL, group, 0)
 
     half = rows
     for block in range(total // half):
@@ -320,6 +342,8 @@
         return carry
 
     lax.fori_loop(0, rows, triangle, 0)
+    for copy in copies[1:]:
+        copy.wait()
     deep = tile_ref.shape[1]
     first = tile_ref[...].reshape(rows * deep, width)
     tri = first_ref[:, :deep, :].reshape(rows * deep, width)
@@ -386,6 +410,7 @@
     deep = 16
     smem = pl.BlockSpec(memory_space=pltpu.SMEM)
     vmem = pl.BlockSpec(memory_space=pltpu.VMEM)
+    hbm = pl.BlockSpec(memory_space=pltpu.HBM)
     operands = [
         length,
         jnp.concatenate([chain_bias, chain_other]),
@@ -414,9 +439,11 @@
             sources=tuple(sources),
         ),
         out_shape=jax.ShapeDtypeStruct((rows, cols // sub_count, width), jnp.bfloat16),
-        in_specs=[smem, smem] + [vmem] * (len(operands) - 2),
+        in_specs=[smem, smem] + [vmem] * (len(operands) - 7) + [hbm] * 5,
         out_specs=vmem,
         scratch_shapes=[
+            *[pltpu.VMEM(each.shape, each.dtype) for each in operands[-5:]],
+            pltpu.SemaphoreType.DMA((5,)),
             pltpu.VMEM((total, wide, width), F32),
             pltpu.VMEM((total, wide, width), F32),
             pltpu.VMEM((total, 8, 2 * wide), F32),

time: 36.9 us -> 27.9 us (0.76)
  Pallas kernels: 15.7 us -> 6.74 us
    pallas_call x1, Pallas kernels: 15.7 us -> 6.74 us  [gathered(): pl.pallas_call(functools.partial(fused, rows=rows, cols=cols, heads=heads...]
  transfers between devices with their start and end apart: 11 -> 11, of which waited for: 4 -> 4; matrix products, arithmetic and copies ran while one was open for 6% -> 7% of each run, Pallas kernels for 0% -> 0%
where the time goes in v2:
time: 27.9 us; the launch traced here: 27.5 us
  starting transfers between devices  8.23 us (29%)
  Pallas kernels  6.74 us (24%)
  local copies, waits for them, and re-layouts  6.61 us (24%)
  waiting for transfers between devices  3.81 us (14%)
  other arithmetic  1.39 us (5%)
  between operations  0.67 us (2%)
    ppermute x4, starting transfers between devices, exchange(): return lax.ppermute(value, axes, routes)  7.2 us
    pallas_call x1, Pallas kernels, gathered(): pl.pallas_call(functools.partial(fused, rows=rows, cols=cols, heads=heads...  6.74 us
    unnamed x16, local copies, waits for them, and re-layouts  5.95 us
    ppermute x4, waiting for transfers between devices, exchange(): return lax.ppermute(value, axes, routes)  3.58 us
    concatenate x1, other arithmetic, gathered(): jnp.concatenate([chain_bias, chain_other])  0.73 us
    concatenate x1, other arithmetic, gathered(): att_bias_rows = jnp.concatenate([att_bias.T, bias_other.T], axis=0)  0.66 us
    reshape x1, local copies, waits for them, and re-layouts, gathered(): jnp.pad(chain, (0, 2 * wide - total)).reshape(1, 2 * wide)  0.66 us
  transfers between devices with their start and end apart: 11, of which 4 were waited for; matrix products, arithmetic and copies ran while one was open for 7% of the time, Pallas kernels for 0%

profile of v2, /device:TPU:0, one launch (start us, length us, event | category | flops | bytes accessed | tf_op | source)
XLA Modules:
  0.0 27.5 jit_solution(10080864325304160481)
XLA Ops:
  0.0 0.0 copy-start.7
  0.0 6.0 %collective-permute-start.3 = (bf16[12,24,128]{2,1,0:T(8,128)(2,1)}, bf16[12,24,128]{2,1,0:T(8,128)(2,1)S(1)}, u32[]{:S(2)}, u32[]{:S(2)}) collective-permute-start(bf16[12,24,128]{2,1,0:T(8,128)(2,1)} %own_ref.1), channel_id=1, source_target_pairs={{0,14},{1,7},{2,12},{3,5},{4,10},{5,3},{6,8},{7,1},{8,6},{9,15},{1... | collective-permute-start | bytes 221192 | tf_op jit(solution)/shard_map/ppermute | solution.py:391
  6.0 0.5 %collective-permute-start.1 = (bf16[12,24,128]{2,1,0:T(8,128)(2,1)}, bf16[12,24,128]{2,1,0:T(8,128)(2,1)S(1)}, u32[]{:S(2)}, u32[]{:S(2)}) collective-permute-start(bf16[12,24,128]{2,1,0:T(8,128)(2,1)} %own_ref.1), channel_id=1, source_target_pairs={{0,2},{1,11},{2,0},{3,9},{4,6},{5,15},{6,4},{7,13},{8,10},{9,3},{1... | collective-permute-start | bytes 221192 | tf_op jit(solution)/shard_map/ppermute | solution.py:391
  6.5 0.0 collective-permute-start.6
  6.5 0.0 collective-permute-start.9
  6.5 0.5 %collective-permute-start = (f32[2]{0:T(128)}, f32[2]{0:T(128)S(1)}, u32[]{:S(2)}, u32[]{:S(2)}) collective-permute-start(f32[2]{0:T(128)} %param.17), channel_id=1, source_target_pairs={{0,1},{1,0},{2,3},{3,2},{4,5},{5,4},{6,7},{7,6},{8,9},{9,8},{10,11... | collective-permute-start | bytes 32 | tf_op jit(solution)/shard_map/ppermute | solution.py:397
  7.7 0.7 %pad_bitcast_fusion.chain_ref = s32[1,128]{1,0:T(1,128)S(1)} fusion(s32[48]{0:T(128)} %param.14), kind=kLoop, calls=%fused_computation.5 | loop fusion | bytes 704 | tf_op jit(solution)/shard_map/reshape | solution.py:417
  8.4 0.0 collective-permute-done
  8.4 0.0 collective-permute-start.10
  8.4 0.7 %pad_maximum_fusion.chain_bias_ref = f32[4]{0:T(128)S(1)} fusion(f32[2]{0:T(128)S(1)} %collective-permute-done, f32[2]{0:T(128)} %param.17), kind=kLoop, calls=%fused_computation.4 | loop fusion | flops 4 | bytes 32 | tf_op jit(solution)/shard_map/concatenate | solution.py:416
  9.1 0.0 collective-permute-done.9
  9.1 0.7 %collective-permute-start.5 = (bf16[12,24,128]{2,1,0:T(8,128)(2,1)}, bf16[12,24,128]{2,1,0:T(8,128)(2,1)S(1)}, u32[]{:S(2)}, u32[]{:S(2)}) collective-permute-start(bf16[12,24,128]{2,1,0:T(8,128)(2,1)} %own_ref.1), channel_id=1, source_target_pairs={{0,4},{1,5},{2,6},{3,7},{4,0},{5,1},{6,2},{7,3},{8,12},{9,13},{10,... | collective-permute-start | bytes 221192 | tf_op jit(solution)/shard_map/ppermute | solution.py:391
  9.8 0.0 collective-permute-done.10.refs_11_
  9.8 0.2 collective-permute-start.8
  10.0 0.0 collective-permute-done.3.refs_2_
  10.0 0.3 %collective-permute-start.4 = (bf16[12,24,128]{2,1,0:T(8,128)(2,1)S(1)}, bf16[12,24,128]{2,1,0:T(8,128)(2,1)S(1)}, u32[]{:S(2)}, u32[]{:S(2)}) collective-permute-start(bf16[12,24,128]{2,1,0:T(8,128)(2,1)S(1)} %collective-permute-done.3.refs_2_), channel_id=1, source_target_pairs={{0,1},{1,0},{2,3},{3,2},{4,5},{5,4},{6,7},{7,6},{8,9},{9,8},{10,11... | collective-permute-start | bytes 221192 | tf_op jit(solution)/shard_map/ppermute | solution.py:405
  10.3 0.8 %collective-permute-done.1.refs_0_ = bf16[12,24,128]{2,1,0:T(8,128)(2,1)S(1)} collective-permute-done((bf16[12,24,128]{2,1,0:T(8,128)(2,1)}, bf16[12,24,128]{2,1,0:T(8,128)(2,1)S(1)}, u32[]{:S(2)}, u32[]{:S(2)}) %collective-permute-start.1) | collective-permute-done | bytes 73760 | tf_op jit(solution)/shard_map/ppermute | solution.py:391
  11.1 0.0 collective-permute-start.2
  11.1 2.4 %collective-permute-done.6.refs_5_ = bf16[12,24,128]{2,1,0:T(8,128)(2,1)S(1)} collective-permute-done((bf16[12,24,128]{2,1,0:T(8,128)(2,1)}, bf16[12,24,128]{2,1,0:T(8,128)(2,1)S(1)}, u32[]{:S(2)}, u32[]{:S(2)}) %collective-permute-start.6) | collective-permute-done | bytes 73760 | tf_op jit(solution)/shard_map/ppermute | solution.py:391
  13.5 0.0 collective-permute-start.7
  13.5 0.7 %fusion.2.refs_9_ = bf16[8,128]{1,0:T(8,128)(2,1)S(1)} fusion(bf16[2,128]{1,0:T(2,128)(2,1)S(1)} %bitcast.9, bf16[2,128]{1,0:T(2,128)(2,1)} %bitcast.8), kind=kLoop, calls=%fused_computation.3 | loop fusion | flops 7168 | bytes 3072 | tf_op jit(solution)/shard_map/concatenate | solution.py:407
  14.2 0.0 collective-permute-done.8
  14.2 0.4 %collective-permute-done.5.refs_4_ = bf16[12,24,128]{2,1,0:T(8,128)(2,1)S(1)} collective-permute-done((bf16[12,24,128]{2,1,0:T(8,128)(2,1)}, bf16[12,24,128]{2,1,0:T(8,128)(2,1)S(1)}, u32[]{:S(2)}, u32[]{:S(2)}) %collective-permute-start.5) | collective-permute-done | bytes 73760 | tf_op jit(solution)/shard_map/ppermute | solution.py:391
  14.5 0.0 collective-permute-done.4.refs_3_
  14.5 0.0 collective-permute-done.2.refs_1_
  14.5 0.2 collective-permute-done.7.refs_6_
  14.8 0.0 copy-done.7
  14.8 0.0 copy-start
  14.8 0.9 %copy-done = bf16[128,512]{1,0:T(8,128)(2,1)S(1)} copy-done((bf16[128,512]{1,0:T(8,128)(2,1)S(1)}, bf16[128,512]{1,0:T(8,128)(2,1)}, u32[]{:S(2)}) %copy-start) | copy-done | bytes 131096
  15.7 0.0 copy-start.1
  15.7 0.9 %copy-done.1 = bf16[128,512]{1,0:T(8,128)(2,1)S(1)} copy-done((bf16[128,512]{1,0:T(8,128)(2,1)S(1)}, bf16[128,512]{1,0:T(8,128)(2,1)}, u32[]{:S(2)}) %copy-start.1) | copy-done | bytes 131096
  16.6 0.0 copy-start.2
  16.6 0.9 %copy-done.2 = bf16[512,128]{1,0:T(8,128)(2,1)S(1)} copy-done((bf16[512,128]{1,0:T(8,128)(2,1)S(1)}, bf16[512,128]{1,0:T(8,128)(2,1)}, u32[]{:S(2)}) %copy-start.2) | copy-done | bytes 131096
  17.5 0.0 copy-start.3
  17.5 0.9 %copy-done.3 = bf16[12,24,128]{2,1,0:T(8,128)(2,1)S(1)} copy-done((bf16[12,24,128]{2,1,0:T(8,128)(2,1)S(1)}, bf16[12,24,128]{2,1,0:T(8,128)(2,1)}, u32[]{:S(2)}) %copy-start.3) | copy-done | bytes 73752
  18.4 0.0 copy-start.4
  18.4 0.8 %copy-done.4 = bf16[128,4,64]{0,2,1:T(8,128)(2,1)S(1)} copy-done((bf16[128,4,64]{0,2,1:T(8,128)(2,1)S(1)}, bf16[128,4,64]{0,2,1:T(8,128)(2,1)}, u32[]{:S(2)}) %copy-start.4) | copy-done | bytes 65560
  19.2 0.0 copy-start.5
  19.2 0.8 %copy-done.5 = bf16[128,128]{1,0:T(8,128)(2,1)S(1)} copy-done((bf16[128,128]{1,0:T(8,128)(2,1)S(1)}, bf16[128,128]{1,0:T(8,128)(2,1)}, u32[]{:S(2)}) %copy-start.5) | copy-done | bytes 32792
  20.0 0.0 copy-start.6
  20.0 0.8 %copy-done.6 = bf16[128,128]{1,0:T(8,128)(2,1)S(1)} copy-done((bf16[128,128]{1,0:T(8,128)(2,1)S(1)}, bf16[128,128]{1,0:T(8,128)(2,1)}, u32[]{:S(2)}) %copy-start.6) | copy-done | bytes 32792
  20.7 6.7 %shard_map.118 = bf16[12,12,128]{2,1,0:T(8,128)(2,1)} custom-call(s32[1]{0:T(128)S(6)} %copy.13.length_ref, f32[4]{0:T(128)S(1)} %pad_maximum_fusion.chain_bias_ref, s32[1,128]{1,0:T(1,128)S(1)} %pad_bitcast_fusion.chain_ref, bf16[12,24,128]{2,1,0:T(8,128)(2,1)S(1)} %copy-done.3, bf16[12,24,128]{2,1,0:T(8,128)(2,1)S(1)} %collective-permute-done.1.refs_0_, ...), custom_call_target="tpu_custom_call" | custom-call | tf_op jit(solution)/shard_map/pallas_call | solution.py:431
Async XLA Ops:
  0.0 14.8 %copy-start.7 = (bf16[64,128]{1,0:T(8,128)(2,1)S(1)}, bf16[64,128]{1,0:T(8,128)(2,1)}, u32[]{:S(2)}) copy-start(bf16[64,128]{1,0:T(8,128)(2,1)} %refs_10_.1) | copy-start | bytes 49156
  0.0 10.0 %collective-permute-start.3 = (bf16[12,24,128]{2,1,0:T(8,128)(2,1)}, bf16[12,24,128]{2,1,0:T(8,128)(2,1)S(1)}, u32[]{:S(2)}, u32[]{:S(2)}) collective-permute-start(bf16[12,24,128]{2,1,0:T(8,128)(2,1)} %own_ref.1), channel_id=1, source_target_pairs={{0,14},{1,7},{2,12},{3,5},{4,10},{5,3},{6,8},{7,1},{8,6},{9,15},{1... | collective-permute-start | bytes 221192 | tf_op jit(solution)/shard_map/ppermute | solution.py:391
  6.0 5.1 %collective-permute-start.1 = (bf16[12,24,128]{2,1,0:T(8,128)(2,1)}, bf16[12,24,128]{2,1,0:T(8,128)(2,1)S(1)}, u32[]{:S(2)}, u32[]{:S(2)}) collective-permute-start(bf16[12,24,128]{2,1,0:T(8,128)(2,1)} %own_ref.1), channel_id=1, source_target_pairs={{0,2},{1,11},{2,0},{3,9},{4,6},{5,15},{6,4},{7,13},{8,10},{9,3},{1... | collective-permute-start | bytes 221192 | tf_op jit(solution)/shard_map/ppermute | solution.py:391
  6.5 6.9 %collective-permute-start.6 = (bf16[12,24,128]{2,1,0:T(8,128)(2,1)}, bf16[12,24,128]{2,1,0:T(8,128)(2,1)S(1)}, u32[]{:S(2)}, u32[]{:S(2)}) collective-permute-start(bf16[12,24,128]{2,1,0:T(8,128)(2,1)} %own_ref.1), channel_id=1, source_target_pairs={{0,8},{1,13},{2,10},{3,15},{4,12},{5,9},{6,14},{7,11},{8,0},{9,5},... | collective-permute-start | bytes 221192 | tf_op jit(solution)/shard_map/ppermute | solution.py:391
  6.5 2.6 %collective-permute-start.9 = (bf16[128,2]{0,1:T(2,128)(2,1)}, bf16[128,2]{0,1:T(2,128)(2,1)S(1)}, u32[]{:S(2)}, u32[]{:S(2)}) collective-permute-start(bf16[128,2]{0,1:T(2,128)(2,1)} %param.16), channel_id=1, source_target_pairs={{0,1},{1,0},{2,3},{3,2},{4,5},{5,4},{6,7},{7,6},{8,9},{9,8},{10,11... | collective-permute-start | bytes 1544 | tf_op jit(solution)/shard_map/ppermute | solution.py:396
  6.5 1.8 %collective-permute-start = (f32[2]{0:T(128)}, f32[2]{0:T(128)S(1)}, u32[]{:S(2)}, u32[]{:S(2)}) collective-permute-start(f32[2]{0:T(128)} %param.17), channel_id=1, source_target_pairs={{0,1},{1,0},{2,3},{3,2},{4,5},{5,4},{6,7},{7,6},{8,9},{9,8},{10,11... | collective-permute-start | bytes 32 | tf_op jit(solution)/shard_map/ppermute | solution.py:397
  8.4 1.4 %collective-permute-start.10 = (bf16[64,128]{1,0:T(8,128)(2,1)}, bf16[64,128]{1,0:T(8,128)(2,1)S(1)}, u32[]{:S(2)}, u32[]{:S(2)}) collective-permute-start(bf16[64,128]{1,0:T(8,128)(2,1)} %refs_10_.1), channel_id=1, source_target_pairs={{0,1},{1,0},{2,3},{3,2},{4,5},{5,4},{6,7},{7,6},{8,9},{9,8},{10,11... | collective-permute-start | bytes 49160 | tf_op jit(solution)/shard_map/ppermute | solution.py:395
  9.1 5.4 %collective-permute-start.5 = (bf16[12,24,128]{2,1,0:T(8,128)(2,1)}, bf16[12,24,128]{2,1,0:T(8,128)(2,1)S(1)}, u32[]{:S(2)}, u32[]{:S(2)}) collective-permute-start(bf16[12,24,128]{2,1,0:T(8,128)(2,1)} %own_ref.1), channel_id=1, source_target_pairs={{0,4},{1,5},{2,6},{3,7},{4,0},{5,1},{6,2},{7,3},{8,12},{9,13},{10,... | collective-permute-start | bytes 221192 | tf_op jit(solution)/shard_map/ppermute | solution.py:391
  9.8 4.4 %collective-permute-start.8 = (bf16[128,4,64]{0,2,1:T(8,128)(2,1)}, bf16[128,4,64]{0,2,1:T(8,128)(2,1)S(1)}, u32[]{:S(2)}, u32[]{:S(2)}) collective-permute-start(bf16[128,4,64]{0,2,1:T(8,128)(2,1)} %param.15), channel_id=1, source_target_pairs={{0,1},{1,0},{2,3},{3,2},{4,5},{5,4},{6,7},{7,6},{8,9},{9,8},{10,11... | collective-permute-start | bytes 196616 | tf_op jit(solution)/shard_map/ppermute | solution.py:394
  10.0 4.5 %collective-permute-start.4 = (bf16[12,24,128]{2,1,0:T(8,128)(2,1)S(1)}, bf16[12,24,128]{2,1,0:T(8,128)(2,1)S(1)}, u32[]{:S(2)}, u32[]{:S(2)}) collective-permute-start(bf16[12,24,128]{2,1,0:T(8,128)(2,1)S(1)} %collective-permute-done.3.refs_2_), channel_id=1, source_target_pairs={{0,1},{1,0},{2,3},{3,2},{4,5},{5,4},{6,7},{7,6},{8,9},{9,8},{10,11... | collective-permute-start | bytes 221192 | tf_op jit(solution)/shard_map/ppermute | solution.py:405
  11.1 3.4 %collective-permute-start.2 = (bf16[12,24,128]{2,1,0:T(8,128)(2,1)S(1)}, bf16[12,24,128]{2,1,0:T(8,128)(2,1)S(1)}, u32[]{:S(2)}, u32[]{:S(2)}) collective-permute-start(bf16[12,24,128]{2,1,0:T(8,128)(2,1)S(1)} %collective-permute-done.1.refs_0_), channel_id=1, source_target_pairs={{0,1},{1,0},{2,3},{3,2},{4,5},{5,4},{6,7},{7,6},{8,9},{9,8},{10,11... | collective-permute-start | bytes 221192 | tf_op jit(solution)/shard_map/ppermute | solution.py:405
  13.5 1.3 %collective-permute-start.7 = (bf16[12,24,128]{2,1,0:T(8,128)(2,1)S(1)}, bf16[12,24,128]{2,1,0:T(8,128)(2,1)S(1)}, u32[]{:S(2)}, u32[]{:S(2)}) collective-permute-start(bf16[12,24,128]{2,1,0:T(8,128)(2,1)S(1)} %collective-permute-done.6.refs_5_), channel_id=1, source_target_pairs={{0,1},{1,0},{2,3},{3,2},{4,5},{5,4},{6,7},{7,6},{8,9},{9,8},{10,11... | collective-permute-start | bytes 221192 | tf_op jit(solution)/shard_map/ppermute | solution.py:405
  14.8 0.9 %copy-start = (bf16[128,512]{1,0:T(8,128)(2,1)S(1)}, bf16[128,512]{1,0:T(8,128)(2,1)}, u32[]{:S(2)}) copy-start(bf16[128,512]{1,0:T(8,128)(2,1)} %refs_12_.1) | copy-start | bytes 393220
  15.7 0.9 %copy-start.1 = (bf16[128,512]{1,0:T(8,128)(2,1)S(1)}, bf16[128,512]{1,0:T(8,128)(2,1)}, u32[]{:S(2)}) copy-start(bf16[128,512]{1,0:T(8,128)(2,1)} %refs_15_.1) | copy-start | bytes 393220
  16.6 0.9 %copy-start.2 = (bf16[512,128]{1,0:T(8,128)(2,1)S(1)}, bf16[512,128]{1,0:T(8,128)(2,1)}, u32[]{:S(2)}) copy-start(bf16[512,128]{1,0:T(8,128)(2,1)} %refs_16_.1) | copy-start | bytes 393220
  17.5 0.9 %copy-start.3 = (bf16[12,24,128]{2,1,0:T(8,128)(2,1)S(1)}, bf16[12,24,128]{2,1,0:T(8,128)(2,1)}, u32[]{:S(2)}) copy-start(bf16[12,24,128]{2,1,0:T(8,128)(2,1)} %own_ref.1) | copy-start | bytes 221188
  18.4 0.8 %copy-start.4 = (bf16[128,4,64]{0,2,1:T(8,128)(2,1)S(1)}, bf16[128,4,64]{0,2,1:T(8,128)(2,1)}, u32[]{:S(2)}) copy-start(bf16[128,4,64]{0,2,1:T(8,128)(2,1)} %param.15) | copy-start | bytes 196612
  19.2 0.8 %copy-start.5 = (bf16[128,128]{1,0:T(8,128)(2,1)S(1)}, bf16[128,128]{1,0:T(8,128)(2,1)}, u32[]{:S(2)}) copy-start(bf16[128,128]{1,0:T(8,128)(2,1)} %refs_13_.1) | copy-start | bytes 98308
  20.0 0.8 %copy-start.6 = (bf16[128,128]{1,0:T(8,128)(2,1)S(1)}, bf16[128,128]{1,0:T(8,128)(2,1)}, u32[]{:S(2)}) copy-start(bf16[128,128]{1,0:T(8,128)(2,1)} %refs_14_.1) | copy-start | bytes 98308

commit v3 on v1

--- a/solution.py
+++ b/solution.py
@@ -138,7 +138,10 @@
 TN = (((0,), (0,)), ((), ()))
 F32 = jnp.float32
 BF16 = jnp.bfloat16
-STEPS = (((0, 1), (2, 1)), ((3, 1), (1, 1)), ((1, 0), (1, 0)), ((2, 0), (3, 0)))
+WIDE = 64
+GROUP = 6
+LIMIT = 16 * 1024 * 1024
+STEPS = (((0, 1), (0, 1)), ((3, 1), (2, 1)), ((1, 0), (1, 1)), ((2, 0), (3, 0)))
 
 
 def replicated(mesh):
@@ -150,27 +153,184 @@
     return lax.dot_general(left, right, dims, preferred_element_type=F32)
 
 
-def fused(
+def flat_pair(ref, start):
+    return ref[pl.ds(start, 2)].reshape(2 * ref.shape[1], ref.shape[2])
+
+
+def head_masks(heads, width):
+    channel = lax.broadcasted_iota(jnp.int32, (1, width), 1)
+    size = width // heads
+    return [
+        ((channel >= head * size) & (channel < (head + 1) * size)).astype(BF16)
+        for head in range(heads)
+    ]
+
+
+def lane_masks():
+    lane = lax.broadcasted_iota(jnp.int32, (1, 2 * WIDE), 1)
+    return (lane < WIDE).astype(BF16), (lane >= WIDE).astype(BF16)
+
+
+def project(tokens, turned_weights, key_weights, heads, total):
+    width = tokens[0].shape[1]
+    first_lanes, second_lanes = lane_masks()
+    masks = head_masks(heads, width)
+    turned = [dot(turned_weights, flat, NT) for flat in tokens]
+    keys = [dot(flat, key_weights, NT).astype(BF16) for flat in tokens]
+    scores = []
+    for key, turn in zip(keys, turned):
+        query = (turn[:width] * (width // heads) ** (-0.5)).astype(BF16)
+        spread_keys = jnp.concatenate(
+            [
+                jnp.concatenate([key[at : at + total] * mask for mask in masks], axis=0)
+                for at in (0, WIDE)
+            ],
+            axis=1,
+        )
+        spread_query = jnp.concatenate([query * first_lanes, query * second_lanes], axis=0)
+        scores.append(dot(spread_keys, spread_query))
+    values = [turn[width : 2 * width].astype(BF16) for turn in turned]
+    gates = [jax.nn.sigmoid(turn[2 * width :]) for turn in turned]
+    return scores, values, gates
+
+
+def bias_rows(weights, tokens, turn_ref, row):
+    both = dot(weights, tokens, NT)
+    turn_ref[row] = both
+    turn_ref[row + 1] = pltpu.roll(both, WIDE, 1)
+
+
+def prepare(
     length_ref,
-    chain_bias_ref,
+    chain_hbm,
+    own_hbm,
+    proj_hbm,
+    att_bias_hbm,
+    chain_bias_hbm,
+    out_hbm,
+    mult_in_hbm,
+    mult_gate_hbm,
+    mult_out_hbm,
+    trans_up_hbm,
+    trans_down_hbm,
+    near_ref,
+    proj_other_ref,
+    att_bias_other_ref,
+    chain_bias_other_ref,
+    out_other_ref,
+    turned_weights_ref,
+    key_weights_ref,
+    out_weights_ref,
+    att_bias_ref,
+    plain_bias_ref,
+    valid_ref,
+    raw_ref,
+    normed_ref,
+    scores_ref,
+    values_ref,
+    gates_ref,
+    turn_ref,
+    mult_in_ref,
+    mult_gate_ref,
+    mult_out_ref,
+    trans_up_ref,
+    trans_down_ref,
     chain_ref,
     own_ref,
+    proj_ref,
+    att_bias_own_ref,
+    chain_bias_ref,
+    out_ref,
+    copy_sems,
+):
+    pairs = (
+        (own_hbm, own_ref),
+        (proj_hbm, proj_ref),
+        (chain_hbm, chain_ref),
+        (att_bias_hbm, att_bias_own_ref),
+        (chain_bias_hbm, chain_bias_ref),
+        (out_hbm, out_ref),
+        (mult_in_hbm, mult_in_ref),
+        (mult_gate_hbm, mult_gate_ref),
+        (mult_out_hbm, mult_out_ref),
+        (trans_up_hbm, trans_up_ref),
+        (trans_down_hbm, trans_down_ref),
+    )
+    copies = [
+        pltpu.make_async_copy(src, dst, copy_sems.at[at]) for at, (src, dst) in enumerate(pairs)
+    ]
+    for copy in copies:
+        copy.start()
+    rows, cols, width = own_ref.shape
+    heads = plain_bias_ref.shape[0]
+    total = plain_bias_ref.shape[1]
+    col_index = lax.axis_index("col")
+    normed_ref[:, total:, :] = jnp.zeros((rows, WIDE - total, width), F32)
+    att_bias_ref[...] = jnp.zeros(att_bias_ref.shape, F32)
+    for copy in copies[:6]:
+        copy.wait()
+    for ref, col in ((own_ref, col_index), (near_ref, 1 - col_index)):
+        value = ref[...].astype(F32)
+        at = pl.ds(pl.multiple_of(col * cols, 8), cols)
+        raw_ref[:, at, :] = value
+        normed_ref[:, at, :] = norm(value)
+    for part, at in ((1, None), (0, 0), (2, 1), (3, 2)):
+        both = jnp.concatenate([proj_ref[part], proj_other_ref[part]], axis=0)
+        if at is None:
+            key_weights_ref[...] = both
+        else:
+            turned_weights_ref[at * width : (at + 1) * width] = both
+    out_weights_ref[...] = jnp.concatenate([out_ref[...], out_other_ref[...]], axis=0)
+    att_bias_ref[0 : heads // 2] = att_bias_own_ref[...].astype(F32)
+    att_bias_ref[heads // 2 : heads] = att_bias_other_ref[...].astype(F32)
+    length = length_ref[0]
+    side = 2 * WIDE
+    chain = chain_ref[...].astype(F32)
+    chain = jnp.concatenate([chain, jnp.zeros((1, side - total), F32)], axis=1)
+    chain = jnp.broadcast_to(chain, (side, side))
+    same = (chain == chain.T).astype(F32)[:total]
+    place = lax.broadcasted_iota(jnp.int32, (total, side), 1)
+    masked = jnp.where(place < length, 0.0, -1000000000.0)
+    for head in range(heads):
+        from_ref = chain_bias_ref if head < heads // 2 else chain_bias_other_ref
+        at = head % (heads // 2)
+        plain_bias_ref[head, :, :] = from_ref[:, at : at + 1] * same + masked
+    down = lax.broadcasted_iota(jnp.int32, (total, width), 0)
+    valid_ref[...] = (down < length).astype(F32)
+    tokens = [flat_pair(normed_ref, 2 * at).astype(BF16) for at in range(rows // 2)]
+    weights = att_bias_ref[...].astype(BF16)
+    for at in range(rows // 2):
+        bias_rows(weights, tokens[at], turn_ref, 2 * at)
+    scores, values, gates = project(
+        tokens, turned_weights_ref[...], key_weights_ref[...], heads, total
+    )
+    for at in range(rows // 2):
+        scores_ref[at] = scores[at]
+        values_ref[at] = values[at]
+        gates_ref[at] = gates[at]
+    for copy in copies[6:]:
+        copy.wait()
+
+
+def finish(
     *refs,
-    rows,
-    cols,
-    heads,
-    head_dim,
-    tokens,
     sources,
 ):
     count = len(sources)
     block_refs = refs[:count]
     (
-        proj_own_ref,
-        proj_other_ref,
+        turned_weights_ref,
+        key_weights_ref,
+        out_weights_ref,
         att_bias_ref,
-        out_own_ref,
-        out_other_ref,
+        plain_bias_ref,
+        valid_ref,
+        raw_own_ref,
+        normed_own_ref,
+        scores_ref,
+        values_ref,
+        gates_ref,
+        turn_own_ref,
         mult_in_ref,
         mult_gate_ref,
         mult_out_ref,
@@ -186,123 +346,120 @@
         first_ref,
         tile_ref,
     ) = refs[count:]
-    width = own_ref.shape[-1]
+    rows, cols, width = block_refs[0].shape
     total = normed_ref.shape[0]
-    wide = normed_ref.shape[1]
+    heads = plain_bias_ref.shape[0]
+    head_dim = width // heads
     row_index = lax.axis_index("row")
     col_index = lax.axis_index("col")
     sub_index = lax.axis_index("sub")
     other_rows = col_index * lax.axis_size("sub") + sub_index
-    length = length_ref[0]
-
-    normed_ref[:, total:, :] = jnp.zeros((total, wide - total, width), F32)
-
-    def place(ref, row_block, col_block):
-        value = ref[...].astype(F32)
-        at = (pl.ds(row_block * rows, rows), pl.ds(pl.multiple_of(col_block * cols, 8), cols))
-        raw_ref[at[0], at[1], :] = value
-        normed_ref[at[0], at[1], :] = norm(value)
-
-    place(own_ref, row_index, col_index)
+    side = 2 * WIDE
+
+    normed_ref[:, total:, :] = jnp.zeros((total, WIDE - total, width), F32)
     for ref, (row_step, col_step) in zip(block_refs, sources):
         row_off = jnp.where(sub_index == 0, row_step[0], row_step[1])
         col_off = jnp.where(sub_index == 0, col_step[0], col_step[1])
-        place(ref, row_index ^ row_off, col_index ^ col_off)
-
-    def pair_tokens(start):
-        return normed_ref[pl.ds(start, 2)].reshape(2 * wide, width).astype(BF16)
-
-    att_bias = att_bias_ref[...]
-    for index in range(total // 2):
-        both = dot(att_bias, pair_tokens(2 * index), NT)
-        turn_ref[2 * index] = both
-        turn_ref[2 * index + 1] = pltpu.roll(both, wide, 1)
-    chain_row = jnp.broadcast_to(chain_ref[...].astype(F32), (2 * wide, 2 * wide))
-    same = (chain_row == chain_row.T).astype(F32)[:total]
-    key_place = lax.broadcasted_iota(jnp.int32, (total, 2 * wide), 1)
-    masked = jnp.where(key_place < length, 0.0, -1000000000.0)
+        value = ref[...].astype(F32)
+        down = pl.ds((row_index ^ row_off) * rows, rows)
+        along = pl.ds(pl.multiple_of((col_index ^ col_off) * cols, 8), cols)
+        raw_ref[down, along, :] = value
+        normed_ref[down, along, :] = norm(value)
+    own_rows = pl.ds(row_index * rows, rows)
+    weights = att_bias_ref[...].astype(BF16)
+    for step in range(1, total // rows):
+        start = (row_index ^ step) * rows
+        for at in range(rows // 2):
+            tokens = flat_pair(normed_ref, start + 2 * at).astype(BF16)
+            bias_rows(weights, tokens, turn_ref, start + 2 * at)
+    turn_ref[own_rows] = turn_own_ref[...]
     for head in range(heads):
-        value = turn_ref[:, head, :] + chain_bias_ref[head] * same + masked
-        value = jnp.concatenate([value, jnp.zeros((wide - total, 2 * wide), F32)], axis=0)
+        value = turn_ref[:, head, :] + plain_bias_ref[head]
+        value = jnp.concatenate([value, jnp.zeros((WIDE - total, side), F32)], axis=0)
         value = jnp.concatenate([value, value], axis=0).T
         bias_ref[pl.ds(head * total, total)] = value[:total]
 
-    def joined(own, other, part):
-        return jnp.concatenate([own[part], other[part]], axis=0)
-
-    key_weights = joined(proj_own_ref, proj_other_ref, 1)
-    turned_weights = jnp.concatenate(
-        [joined(proj_own_ref, proj_other_ref, part) for part in (0, 2, 3)], axis=0
-    )
-    out_weights = jnp.concatenate([out_own_ref[...], out_other_ref[...]], axis=0)
-    lane = lax.broadcasted_iota(jnp.int32, (1, 2 * wide), 1)
-    lane_first = (lane < wide).astype(BF16)
-    lane_second = (lane >= wide).astype(BF16)
-    channel = lax.broadcasted_iota(jnp.int32, (1, width), 1)
-    head_masks = [
-        ((channel >= head * head_dim) & (channel < (head + 1) * head_dim)).astype(BF16)
-        for head in range(heads)
-    ]
-    pad = jnp.zeros((wide - total, 2 * wide), BF16)
-
-    def attend(start):
-        flat = pair_tokens(start)
-        turned = dot(turned_weights, flat, NT)
-        query = (turned[:width] * head_dim ** (-0.5)).astype(BF16)
-        values = turned[width : 2 * width].astype(BF16)
-        gating = jax.nn.sigmoid(turned[2 * width :])
-        keys = dot(flat, key_weights, NT).astype(BF16)
-        spread_keys = jnp.concatenate(
-            [
-                jnp.concatenate(
-                    [keys[at : at + total] * mask for mask in head_masks], axis=0
+    first_lanes, second_lanes = lane_masks()
+    pad = jnp.zeros((WIDE - total, side), BF16)
+    out_weights = out_weights_ref[...]
+
+    def attend(scores, values, gates):
+        weights = []
+        for head in range(heads):
+            at = slice(head * total, (head + 1) * total)
+            bias = bias_ref[at]
+            parts = [score[at] + bias for score in scores]
+            parts = [jnp.exp(part - jnp.max(part, axis=0, keepdims=True)) for part in parts]
+            weights.append(
+                [(part / jnp.sum(part, axis=0, keepdims=True)).astype(BF16) for part in parts]
+            )
+        attended = []
+        for at in range(len(scores)):
+            parts = []
+            for head in range(heads):
+                each = weights[head][at]
+                spread_weights = jnp.concatenate(
+                    [each * first_lanes, pad, each * second_lanes, pad], axis=0
                 )
-                for at in (0, wide)
-            ],
-            axis=1,
-        )
-        spread_query = jnp.concatenate([query * lane_first, query * lane_second], axis=0)
-        scores = dot(spread_keys, spread_query) + bias_ref[...]
-        attended = []
-        for head in range(heads):
-            part = scores[head * total : (head + 1) * total]
-            part = jnp.exp(part - jnp.max(part, axis=0, keepdims=True))
-            weights = (part / jnp.sum(part, axis=0, keepdims=True)).astype(BF16)
-            spread_weights = jnp.concatenate(
-                [weights * lane_first, pad, weights * lane_second, pad], axis=0
+                parts.append(
+                    dot(values[at][head * head_dim : (head + 1) * head_dim], spread_weights)
+                )
+            attended.append((jnp.concatenate(parts, axis=0) * gates[at]).astype(BF16))
+        return [dot(each, out_weights, TN) for each in attended]
+
+    def halves(firsts, starts, column):
+        mixed = [norm(first).astype(BF16) for first in firsts]
+        boths = [dot(each, mult_in_ref[:, column : column + 2 * width]) for each in mixed]
+        values = [jax.nn.sigmoid(both[:, width:]) * both[:, :width] for both in boths]
+        results = []
+        for value, start in zip(values, starts):
+            for which in range(2):
+                row_valid = valid_ref[pl.ds(start + which, 1), :]
+                each = value[which * WIDE : which * WIDE + total] * (valid_ref[...] * row_valid)
+                results.append(each.astype(BF16).astype(F32))
+        return results
+
+    steps = range(rows // 2)
+    start = other_rows * rows
+
+    @pl.when(other_rows == row_index)
+    def _():
+        raw_ref[own_rows] = raw_own_ref[...]
+        normed_ref[own_rows] = normed_own_ref[...]
+
+    tokens = [flat_pair(normed_ref, start + 2 * at).astype(BF16) for at in steps]
+    scores, values, gates = project(
+        tokens, turned_weights_ref[...], key_weights_ref[...], heads, total
+    )
+    def run(own, group):
+        if own:
+            updates = attend(
+                [scores_ref[at] for at in group],
+                [values_ref[at] for at in group],
+                [gates_ref[at] for at in group],
             )
-            attended.append(
-                dot(values[head * head_dim : (head + 1) * head_dim], spread_weights)
+            raws = [flat_pair(raw_own_ref, 2 * at) for at in group]
+            starts = [row_index * rows + 2 * at for at in group]
+        else:
+            updates = attend(
+                [scores[at] for at in group],
+                [values[at] for at in group],
+                [gates[at] for at in group],
             )
-        attended = (jnp.concatenate(attended, axis=0) * gating).astype(BF16)
-        update = dot(attended, out_weights, TN)
-        return raw_ref[pl.ds(start, 2)].reshape(2 * wide, width) + update
-
-    col_valid = (lax.broadcasted_iota(jnp.int32, (total, width), 0) < length).astype(F32)
-
-    def halves(start, step, first, into_ref, column):
-        mixed = norm(first).astype(BF16)
-        both = dot(mixed, mult_in_ref[:, column : column + 2 * width])
-        side = jax.nn.sigmoid(both[:, width:]) * both[:, :width]
-        for which in range(2):
-            row_valid = (start + which < length).astype(F32)
-            value = side[which * wide : which * wide + total] * (col_valid * row_valid)
-            into_ref[2 * step + which] = value.astype(BF16).astype(F32)
-
-    def own_step(step, carry):
-        start = row_index * rows + 2 * step
-        first = attend(start)
-        first_ref[pl.ds(2 * step, 2)] = first.reshape(2, wide, width)
-        halves(start, step, first, left_ref, 0)
-        return carry
-
-    def other_step(step, carry):
-        start = other_rows * rows + 2 * step
-        halves(start, step, attend(start), right_ref, 2 * width)
-        return carry
-
-    lax.fori_loop(0, rows // 2, own_step, 0)
-    lax.fori_loop(0, rows // 2, other_step, 0)
+            starts = [start + 2 * at for at in group]
+            raws = [flat_pair(raw_ref, at) for at in starts]
+        firsts = [raw + update for raw, update in zip(raws, updates)]
+        if own:
+            for at, first in zip(group, firsts):
+                first_ref[2 * at : 2 * at + 2] = first.reshape(2, WIDE, width)
+        results = halves(firsts, starts, 0 if own else 2 * width)
+        into_ref = left_ref if own else right_ref
+        for at, each in enumerate(results):
+            into_ref[2 * group[0] + at] = each
+
+    for own in (True, False):
+        for at in range(0, rows // 2, GROUP):
+            run(own, list(range(at, at + GROUP)))
 
     half = rows
     for block in range(total // half):
@@ -351,8 +508,8 @@
     sub_count = lax.axis_size("sub")
     total = rows * row_count
     heads = att_bias.shape[1] * sub_count
-    head_dim = att_out.shape[0] // att_bias.shape[1]
     axes = ("row", "col", "sub")
+    side = 2 * WIDE
 
     def place(row, col, sub):
         return (row * col_count + col) * sub_count + sub
@@ -367,66 +524,94 @@
         return lax.ppermute(value, axes, routes)
 
     swap = functools.partial(lax.ppermute, axis_name="sub", perm=[(0, 1), (1, 0)])
+    near = exchange(pair, STEPS[0])
+    fetched = [exchange(pair, offsets) for offsets in STEPS[1:]]
     proj_other = swap(att_proj)
     out_other = swap(att_out)
     bias_other = swap(att_bias)
     chain_other = swap(chain_bias)
     blocks, sources = [], []
-    fetched = [exchange(pair, offsets) for offsets in STEPS]
-    for value, offsets in zip(fetched, STEPS):
+    for value, offsets in zip(fetched, STEPS[1:]):
         mine = tuple(zip(offsets[0], offsets[1]))
         blocks.append(value)
         sources.append(mine)
         if offsets[0] != offsets[1]:
             blocks.append(swap(value))
             sources.append(tuple((b, a) for a, b in mine))
-    att_bias_rows = jnp.concatenate([att_bias.T, bias_other.T], axis=0)
-    att_bias_rows = jnp.pad(att_bias_rows, ((0, 8 - heads), (0, 0)))
-    wide = 64
-    deep = 16
     smem = pl.BlockSpec(memory_space=pltpu.SMEM)
     vmem = pl.BlockSpec(memory_space=pltpu.VMEM)
-    operands = [
-        length,
-        jnp.concatenate([chain_bias, chain_other]),
-        jnp.pad(chain, (0, 2 * wide - total)).reshape(1, 2 * wide),
+    hbm = pl.BlockSpec(memory_space=pltpu.HBM)
+    params = [
+        chain.reshape(1, total),
         pair,
-        *blocks,
         att_proj.transpose(1, 2, 0),
-        proj_other.transpose(1, 2, 0),
-        att_bias_rows,
+        att_bias.T,
+        chain_bias.reshape(1, -1),
         att_out,
-        out_other,
         mult_in,
         mult_gate,
         mult_out,
         trans_up,
         trans_down,
     ]
+    params = [pltpu.with_memory_space_constraint(each, pltpu.HBM) for each in params]
+    early = [
+        near,
+        proj_other.transpose(1, 2, 0),
+        bias_other.T,
+        chain_other.reshape(1, -1),
+        out_other,
+    ]
+    shape = jax.ShapeDtypeStruct
+    scratch = lambda each: pltpu.VMEM(each.shape, each.dtype)
+    ready = pl.pallas_call(
+        prepare,
+        out_shape=[
+            shape((3 * width, width), BF16),
+            shape((width, width), BF16),
+            shape((width, width), BF16),
+            shape((8, width), F32),
+            shape((heads, total, side), F32),
+            shape((total, width), F32),
+            shape((rows, WIDE, width), F32),
+            shape((rows, WIDE, width), F32),
+            shape((rows // 2, heads * total, side), F32),
+            shape((rows // 2, width, side), BF16),
+            shape((rows // 2, width, side), F32),
+            shape((rows, 8, side), F32),
+            *[shape(each.shape, each.dtype) for each in params[-5:]],
+        ],
+        in_specs=[smem] + [hbm] * len(params) + [vmem] * len(early),
+        out_specs=[vmem] * 17,
+        scratch_shapes=[
+            scratch(params[0]),
+            scratch(params[1]),
+            scratch(params[2]),
+            scratch(params[3]),
+            scratch(params[4]),
+            scratch(params[5]),
+            pltpu.SemaphoreType.DMA((len(params),)),
+        ],
+        compiler_params=pltpu.CompilerParams(vmem_limit_bytes=LIMIT),
+    )(length, *params, *early)
+    operands = [*blocks, *ready]
+    deep = 16
     return pl.pallas_call(
-        functools.partial(
-            fused,
-            rows=rows,
-            cols=cols,
-            heads=heads,
-            head_dim=head_dim,
-            tokens=wide,
-            sources=tuple(sources),
-        ),
-        out_shape=jax.ShapeDtypeStruct((rows, cols // sub_count, width), jnp.bfloat16),
-        in_specs=[smem, smem] + [vmem] * (len(operands) - 2),
+        functools.partial(finish, sources=tuple(sources)),
+        out_shape=shape((rows, cols // sub_count, width), BF16),
+        in_specs=[vmem] * len(operands),
         out_specs=vmem,
         scratch_shapes=[
-            pltpu.VMEM((total, wide, width), F32),
-            pltpu.VMEM((total, wide, width), F32),
-            pltpu.VMEM((total, 8, 2 * wide), F32),
-            pltpu.VMEM((heads * total, 2 * wide), F32),
+            pltpu.VMEM((total, WIDE, width), F32),
+            pltpu.VMEM((total, WIDE, width), F32),
+            pltpu.VMEM((total, 8, side), F32),
+            pltpu.VMEM((heads * total, side), F32),
             pltpu.VMEM((rows, total, width), F32),
             pltpu.VMEM((rows, total, width), F32),
-            pltpu.VMEM((rows, wide, width), F32),
+            pltpu.VMEM((rows, WIDE, width), F32),
             pltpu.VMEM((rows, deep, width), F32),
         ],
-        compiler_params=pltpu.CompilerParams(vmem_limit_bytes=48 * 1024 * 1024),
+        compiler_params=pltpu.CompilerParams(vmem_limit_bytes=LIMIT),
     )(*operands)
 
 

time: 36.9 us -> 21.7 us (0.59)
  Pallas kernels: 15.7 us -> 7.2 us
  local copies, waits for them, and re-layouts: 6.61 us -> 0 us
  other arithmetic: 1.39 us -> 0 us
  waiting for transfers between devices: 3.81 us -> 5 us
  starting transfers between devices: 8.23 us -> 8.63 us
    pallas_call x1 -> x2, Pallas kernels: 15.7 us -> 7.2 us  [the longest x1 5.21 us: gathered(): pl.pallas_call(functools.partial(finish, sources=tuple(sources)), out_sha...]
    unnamed x16 -> x0, local copies, waits for them, and re-layouts: 5.95 us -> none
    concatenate x2 -> x0, other arithmetic: 1.39 us -> none  [the longest x1 0.73 us: gathered(): jnp.concatenate([chain_bias, chain_other])]
    ppermute x4, waiting for transfers between devices: 3.58 us -> 2.34 us  [exchange(): return lax.ppermute(value, axes, routes)]
    ppermute x1, waiting for transfers between devices: 0.01 us -> 0.95 us  [gathered(): chain_other = swap(chain_bias)]
    ppermute x1, waiting for transfers between devices: 0.01 us -> 0.95 us  [gathered(): bias_other = swap(att_bias)]
    ppermute x1, waiting for transfers between devices: 0.01 us -> 0.74 us  [gathered(): proj_other = swap(att_proj)]
    reshape x1 -> x0, local copies, waits for them, and re-layouts: 0.66 us -> none  [gathered(): jnp.pad(chain, (0, 2 * wide - total)).reshape(1, 2 * wide)]
  transfers between devices with their start and end apart: 11 -> 11, of which waited for: 4 -> 5; matrix products, arithmetic and copies ran while one was open for 6% -> 0% of each run, Pallas kernels for 0% -> 9%
where the time goes in v3:
time: 21.7 us; the launch traced here: 21.5 us
  starting transfers between devices  8.63 us (40%)
  Pallas kernels  7.2 us (33%)
  waiting for transfers between devices  5 us (23%)
  between operations  0.69 us (3%)
    ppermute x4, starting transfers between devices, exchange(): return lax.ppermute(value, axes, routes)  7.14 us
    pallas_call x1, Pallas kernels, gathered(): pl.pallas_call(functools.partial(finish, sources=tuple(sources)), out_sha...  5.21 us
    ppermute x4, waiting for transfers between devices, exchange(): return lax.ppermute(value, axes, routes)  2.34 us
    pallas_call x1, Pallas kernels, gathered(): pl.pallas_call(prepare, out_shape=[shape((3 * width, width), BF16), shape...  1.99 us
    ppermute x1, waiting for transfers between devices, gathered(): chain_other = swap(chain_bias)  0.95 us
    ppermute x1, waiting for transfers between devices, gathered(): bias_other = swap(att_bias)  0.95 us
    ppermute x1, waiting for transfers between devices, gathered(): proj_other = swap(att_proj)  0.74 us
    ppermute x3, starting transfers between devices, gathered(): blocks.append(swap(value))  0.57 us
  transfers between devices with their start and end apart: 11, of which 5 were waited for; matrix products, arithmetic and copies ran while one was open for 0% of the time, Pallas kernels for 9%

profile of v3, /device:TPU:0, one launch (start us, length us, event | category | flops | bytes accessed | tf_op | source)
XLA Modules:
  0.0 21.5 jit_solution(16737622251798379689)
XLA Ops:
  0.0 6.0 %collective-permute-start = (bf16[12,24,128]{2,1,0:T(8,128)(2,1)}, bf16[12,24,128]{2,1,0:T(8,128)(2,1)S(1)}, u32[]{:S(2)}, u32[]{:S(2)}) collective-permute-start(bf16[12,24,128]{2,1,0:T(8,128)(2,1)} %own_hbm.1), channel_id=1, source_target_pairs={{0,14},{1,11},{2,12},{3,9},{4,10},{5,15},{6,8},{7,13},{8,6},{9,3},... | collective-permute-start | bytes 221192 | tf_op jit(solution)/shard_map/ppermute | solution.py:524
  6.0 0.0 collective-permute-start.2
  6.0 0.8 %collective-permute-start.4 = (bf16[12,24,128]{2,1,0:T(8,128)(2,1)}, bf16[12,24,128]{2,1,0:T(8,128)(2,1)S(1)}, u32[]{:S(2)}, u32[]{:S(2)}) collective-permute-start(bf16[12,24,128]{2,1,0:T(8,128)(2,1)} %own_hbm.1), channel_id=1, source_target_pairs={{0,8},{1,13},{2,10},{3,15},{4,12},{5,9},{6,14},{7,11},{8,0},{9,5},... | collective-permute-start | bytes 221192 | tf_op jit(solution)/shard_map/ppermute | solution.py:524
  6.8 0.0 collective-permute-start.10
  6.8 0.5 %collective-permute-start.9 = (f32[2]{0:T(128)}, f32[2]{0:T(128)S(1)}, u32[]{:S(2)}, u32[]{:S(2)}) collective-permute-start(f32[2]{0:T(128)} %param.17), channel_id=1, source_target_pairs={{0,1},{1,0},{2,3},{3,2},{4,5},{5,4},{6,7},{7,6},{8,9},{9,8},{10,11... | collective-permute-start | bytes 32 | tf_op jit(solution)/shard_map/ppermute | solution.py:532
  7.3 1.0 %collective-permute-done.9 = f32[2]{0:T(128)S(1)} collective-permute-done((f32[2]{0:T(128)}, f32[2]{0:T(128)S(1)}, u32[]{:S(2)}, u32[]{:S(2)}) %collective-permute-start.9) | collective-permute-done | bytes 40 | tf_op jit(solution)/shard_map/ppermute | solution.py:532
  8.3 0.3 %collective-permute-start.8 = (bf16[128,2]{0,1:T(2,128)(2,1)}, bf16[128,2]{0,1:T(2,128)(2,1)S(1)}, u32[]{:S(2)}, u32[]{:S(2)}) collective-permute-start(bf16[128,2]{0,1:T(2,128)(2,1)} %param.16), channel_id=1, source_target_pairs={{0,1},{1,0},{2,3},{3,2},{4,5},{5,4},{6,7},{7,6},{8,9},{9,8},{10,11... | collective-permute-start | bytes 1544 | tf_op jit(solution)/shard_map/ppermute | solution.py:531
  8.6 1.0 %collective-permute-done.8 = bf16[128,2]{0,1:T(2,128)(2,1)S(1)} collective-permute-done((bf16[128,2]{0,1:T(2,128)(2,1)}, bf16[128,2]{0,1:T(2,128)(2,1)S(1)}, u32[]{:S(2)}, u32[]{:S(2)}) %collective-permute-start.8) | collective-permute-done | bytes 544 | tf_op jit(solution)/shard_map/ppermute | solution.py:531
  9.6 0.3 %collective-permute-start.6 = (bf16[12,24,128]{2,1,0:T(8,128)(2,1)}, bf16[12,24,128]{2,1,0:T(8,128)(2,1)S(1)}, u32[]{:S(2)}, u32[]{:S(2)}) collective-permute-start(bf16[12,24,128]{2,1,0:T(8,128)(2,1)} %own_hbm.1), channel_id=1, source_target_pairs={{0,2},{1,3},{2,0},{3,1},{4,6},{5,7},{6,4},{7,5},{8,10},{9,11},{10,... | collective-permute-start | bytes 221192 | tf_op jit(solution)/shard_map/ppermute | solution.py:524
  9.9 0.0 collective-permute-done.refs_0_
  9.9 0.1 collective-permute-start.1
  10.0 2.2 %collective-permute-done.2.refs_2_ = bf16[12,24,128]{2,1,0:T(8,128)(2,1)S(1)} collective-permute-done((bf16[12,24,128]{2,1,0:T(8,128)(2,1)}, bf16[12,24,128]{2,1,0:T(8,128)(2,1)S(1)}, u32[]{:S(2)}, u32[]{:S(2)}) %collective-permute-start.2) | collective-permute-done | bytes 73760 | tf_op jit(solution)/shard_map/ppermute | solution.py:524
  12.2 0.0 collective-permute-start.3
  12.2 0.0 collective-permute-done.4.refs_4_
  12.2 0.5 %collective-permute-start.5 = (bf16[12,24,128]{2,1,0:T(8,128)(2,1)S(1)}, bf16[12,24,128]{2,1,0:T(8,128)(2,1)S(1)}, u32[]{:S(2)}, u32[]{:S(2)}) collective-permute-start(bf16[12,24,128]{2,1,0:T(8,128)(2,1)S(1)} %collective-permute-done.4.refs_4_), channel_id=1, source_target_pairs={{0,1},{1,0},{2,3},{3,2},{4,5},{5,4},{6,7},{7,6},{8,9},{9,8},{10,11... | collective-permute-start | bytes 221192 | tf_op jit(solution)/shard_map/ppermute | solution.py:539
  12.7 0.0 collective-permute-done.10.out_other_ref
  12.7 0.1 collective-permute-start.7
  13.4 0.7 %collective-permute-done.7 = bf16[128,4,64]{0,2,1:T(8,128)(2,1)S(1)} collective-permute-done((bf16[128,4,64]{0,2,1:T(8,128)(2,1)}, bf16[128,4,64]{0,2,1:T(8,128)(2,1)S(1)}, u32[]{:S(2)}, u32[]{:S(2)}) %collective-permute-start.7) | collective-permute-done | bytes 65568 | tf_op jit(solution)/shard_map/ppermute | solution.py:529
  14.1 0.1 collective-permute-done.6.near_ref
  14.3 2.0 %shard_map.118 = (bf16[384,128]{1,0:T(8,128)(2,1)S(1)}, bf16[128,128]{1,0:T(8,128)(2,1)S(1)}, bf16[128,128]{1,0:T(8,128)(2,1)S(1)}, f32[8,128]{1,0:T(8,128)S(1)}...) custom-call(s32[1]{0:T(128)S(6)} %copy.13.length_ref, ...), custom_call_target="tpu_custom_call" | custom-call | tf_op jit(solution)/shard_map/pallas_call | solution.py:567
  16.3 0.0 collective-permute-done.1.refs_1_
  16.3 0.0 collective-permute-done.3.refs_3_
  16.3 0.0 collective-permute-done.5.refs_5_
  16.3 5.2 %shard_map.119 = bf16[12,12,128]{2,1,0:T(8,128)(2,1)} custom-call(bf16[12,24,128]{2,1,0:T(8,128)(2,1)S(1)} %collective-permute-done.refs_0_, bf16[12,24,128]{2,1,0:T(8,128)(2,1)S(1)} %collective-permute-done.1.refs_1_, bf16[12,24,128]{2,1,0:T(8,128)(2,1)S(1)} %collective-permute-done.2.refs_2_, bf16[12,24,128]{2,1,0:T(8,128)(2,1)S(1)} %collective-permute-done.3.refs_3_, ...), custom_call_target="tpu_custom_call" | custom-call | tf_op jit(solution)/shard_map/pallas_call | solution.py:599
Async XLA Ops:
  0.0 9.9 %collective-permute-start = (bf16[12,24,128]{2,1,0:T(8,128)(2,1)}, bf16[12,24,128]{2,1,0:T(8,128)(2,1)S(1)}, u32[]{:S(2)}, u32[]{:S(2)}) collective-permute-start(bf16[12,24,128]{2,1,0:T(8,128)(2,1)} %own_hbm.1), channel_id=1, source_target_pairs={{0,14},{1,11},{2,12},{3,9},{4,10},{5,15},{6,8},{7,13},{8,6},{9,3},... | collective-permute-start | bytes 221192 | tf_op jit(solution)/shard_map/ppermute | solution.py:524
  6.0 6.1 %collective-permute-start.2 = (bf16[12,24,128]{2,1,0:T(8,128)(2,1)}, bf16[12,24,128]{2,1,0:T(8,128)(2,1)S(1)}, u32[]{:S(2)}, u32[]{:S(2)}) collective-permute-start(bf16[12,24,128]{2,1,0:T(8,128)(2,1)} %own_hbm.1), channel_id=1, source_target_pairs={{0,4},{1,7},{2,6},{3,5},{4,0},{5,3},{6,2},{7,1},{8,12},{9,15},{10,... | collective-permute-start | bytes 221192 | tf_op jit(solution)/shard_map/ppermute | solution.py:524
  6.0 6.1 %collective-permute-start.4 = (bf16[12,24,128]{2,1,0:T(8,128)(2,1)}, bf16[12,24,128]{2,1,0:T(8,128)(2,1)S(1)}, u32[]{:S(2)}, u32[]{:S(2)}) collective-permute-start(bf16[12,24,128]{2,1,0:T(8,128)(2,1)} %own_hbm.1), channel_id=1, source_target_pairs={{0,8},{1,13},{2,10},{3,15},{4,12},{5,9},{6,14},{7,11},{8,0},{9,5},... | collective-permute-start | bytes 221192 | tf_op jit(solution)/shard_map/ppermute | solution.py:524
  6.8 5.9 %collective-permute-start.10 = (bf16[64,128]{1,0:T(8,128)(2,1)}, bf16[64,128]{1,0:T(8,128)(2,1)S(1)}, u32[]{:S(2)}, u32[]{:S(2)}) collective-permute-start(bf16[64,128]{1,0:T(8,128)(2,1)} %out_hbm.1), channel_id=1, source_target_pairs={{0,1},{1,0},{2,3},{3,2},{4,5},{5,4},{6,7},{7,6},{8,9},{9,8},{10,11... | collective-permute-start | bytes 49160 | tf_op jit(solution)/shard_map/ppermute | solution.py:530
  6.8 1.5 %collective-permute-start.9 = (f32[2]{0:T(128)}, f32[2]{0:T(128)S(1)}, u32[]{:S(2)}, u32[]{:S(2)}) collective-permute-start(f32[2]{0:T(128)} %param.17), channel_id=1, source_target_pairs={{0,1},{1,0},{2,3},{3,2},{4,5},{5,4},{6,7},{7,6},{8,9},{9,8},{10,11... | collective-permute-start | bytes 32 | tf_op jit(solution)/shard_map/ppermute | solution.py:532
  8.3 1.3 %collective-permute-start.8 = (bf16[128,2]{0,1:T(2,128)(2,1)}, bf16[128,2]{0,1:T(2,128)(2,1)S(1)}, u32[]{:S(2)}, u32[]{:S(2)}) collective-permute-start(bf16[128,2]{0,1:T(2,128)(2,1)} %param.16), channel_id=1, source_target_pairs={{0,1},{1,0},{2,3},{3,2},{4,5},{5,4},{6,7},{7,6},{8,9},{9,8},{10,11... | collective-permute-start | bytes 1544 | tf_op jit(solution)/shard_map/ppermute | solution.py:531
  9.6 4.7 %collective-permute-start.6 = (bf16[12,24,128]{2,1,0:T(8,128)(2,1)}, bf16[12,24,128]{2,1,0:T(8,128)(2,1)S(1)}, u32[]{:S(2)}, u32[]{:S(2)}) collective-permute-start(bf16[12,24,128]{2,1,0:T(8,128)(2,1)} %own_hbm.1), channel_id=1, source_target_pairs={{0,2},{1,3},{2,0},{3,1},{4,6},{5,7},{6,4},{7,5},{8,10},{9,11},{10,... | collective-permute-start | bytes 221192 | tf_op jit(solution)/shard_map/ppermute | solution.py:524
  9.9 6.4 %collective-permute-start.1 = (bf16[12,24,128]{2,1,0:T(8,128)(2,1)S(1)}, bf16[12,24,128]{2,1,0:T(8,128)(2,1)S(1)}, u32[]{:S(2)}, u32[]{:S(2)}) collective-permute-start(bf16[12,24,128]{2,1,0:T(8,128)(2,1)S(1)} %collective-permute-done.refs_0_), channel_id=1, source_target_pairs={{0,1},{1,0},{2,3},{3,2},{4,5},{5,4},{6,7},{7,6},{8,9},{9,8},{10,11... | collective-permute-start | bytes 221192 | tf_op jit(solution)/shard_map/ppermute | solution.py:539
  12.2 4.1 %collective-permute-start.3 = (bf16[12,24,128]{2,1,0:T(8,128)(2,1)S(1)}, bf16[12,24,128]{2,1,0:T(8,128)(2,1)S(1)}, u32[]{:S(2)}, u32[]{:S(2)}) collective-permute-start(bf16[12,24,128]{2,1,0:T(8,128)(2,1)S(1)} %collective-permute-done.2.refs_2_), channel_id=1, source_target_pairs={{0,1},{1,0},{2,3},{3,2},{4,5},{5,4},{6,7},{7,6},{8,9},{9,8},{10,11... | collective-permute-start | bytes 221192 | tf_op jit(solution)/shard_map/ppermute | solution.py:539
  12.2 4.1 %collective-permute-start.5 = (bf16[12,24,128]{2,1,0:T(8,128)(2,1)S(1)}, bf16[12,24,128]{2,1,0:T(8,128)(2,1)S(1)}, u32[]{:S(2)}, u32[]{:S(2)}) collective-permute-start(bf16[12,24,128]{2,1,0:T(8,128)(2,1)S(1)} %collective-permute-done.4.refs_4_), channel_id=1, source_target_pairs={{0,1},{1,0},{2,3},{3,2},{4,5},{5,4},{6,7},{7,6},{8,9},{9,8},{10,11... | collective-permute-start | bytes 221192 | tf_op jit(solution)/shard_map/ppermute | solution.py:539
  12.7 1.5 %collective-permute-start.7 = (bf16[128,4,64]{0,2,1:T(8,128)(2,1)}, bf16[128,4,64]{0,2,1:T(8,128)(2,1)S(1)}, u32[]{:S(2)}, u32[]{:S(2)}) collective-permute-start(bf16[128,4,64]{0,2,1:T(8,128)(2,1)} %param.15), channel_id=1, source_target_pairs={{0,1},{1,0},{2,3},{3,2},{4,5},{5,4},{6,7},{7,6},{8,9},{9,8},{10,11... | collective-permute-start | bytes 196616 | tf_op jit(solution)/shard_map/ppermute | solution.py:529

commit v4 on v3

--- a/solution.py
+++ b/solution.py
@@ -141,7 +141,7 @@
 WIDE = 64
 GROUP = 6
 LIMIT = 16 * 1024 * 1024
-STEPS = (((0, 1), (0, 1)), ((3, 1), (2, 1)), ((1, 0), (1, 1)), ((2, 0), (3, 0)))
+STEPS = (((0, 1), (0, 1)), ((3, 1), (2, 1)), ((3, 0), (1, 0)), ((1, 1), (2, 0)))
 
 
 def replicated(mesh):
@@ -192,6 +192,17 @@
     values = [turn[width : 2 * width].astype(BF16) for turn in turned]
     gates = [jax.nn.sigmoid(turn[2 * width :]) for turn in turned]
     return scores, values, gates
+
+
+def block_norm(ref):
+    block = ref[...]
+    flat = block.reshape(-1, block.shape[-1])
+    ones = jnp.full((block.shape[-1], block.shape[-1]), 1.0 / block.shape[-1], BF16)
+    value = flat.astype(F32)
+    centred = value - dot(flat, ones)
+    variance = jnp.mean(centred * centred, axis=-1, keepdims=True)
+    result = centred * lax.rsqrt(variance + 1e-05)
+    return value.reshape(block.shape), result.reshape(block.shape)
 
 
 def bias_rows(weights, tokens, turn_ref, row):
@@ -270,10 +281,10 @@
     for copy in copies[:6]:
         copy.wait()
     for ref, col in ((own_ref, col_index), (near_ref, 1 - col_index)):
-        value = ref[...].astype(F32)
         at = pl.ds(pl.multiple_of(col * cols, 8), cols)
+        value, result = block_norm(ref)
         raw_ref[:, at, :] = value
-        normed_ref[:, at, :] = norm(value)
+        normed_ref[:, at, :] = result
     for part, at in ((1, None), (0, 0), (2, 1), (3, 2)):
         both = jnp.concatenate([proj_ref[part], proj_other_ref[part]], axis=0)
         if at is None:
@@ -312,13 +323,63 @@
         copy.wait()
 
 
-def finish(
-    *refs,
-    sources,
-):
+def scatter(block_refs, sources, raw_ref, normed_ref):
+    sub_index = lax.axis_index("sub")
+    for ref, (row_step, col_step) in zip(block_refs, sources):
+        rows, cols, _ = ref.shape
+        row_block = lax.axis_index("row") ^ jnp.where(sub_index == 0, *row_step)
+        col_block = lax.axis_index("col") ^ jnp.where(sub_index == 0, *col_step)
+        down = pl.ds(row_block * rows, rows)
+        along = pl.ds(pl.multiple_of(col_block * cols, 8), cols)
+        value, result = block_norm(ref)
+        raw_ref[down, along, :] = value
+        normed_ref[down, along, :] = result
+
+
+def whole_rows(att_bias_ref, normed_ref, turn_ref, rows, row_step):
+    weights = att_bias_ref[...].astype(BF16)
+    start = (lax.axis_index("row") ^ jnp.where(lax.axis_index("sub") == 0, *row_step)) * rows
+    for at in range(rows // 2):
+        tokens = flat_pair(normed_ref, start + 2 * at).astype(BF16)
+        bias_rows(weights, tokens, turn_ref, start + 2 * at)
+
+
+def collect(*refs, sources, row_steps, late_step):
     count = len(sources)
-    block_refs = refs[:count]
     (
+        att_bias_ref,
+        raw_own_ref,
+        normed_own_ref,
+        turn_own_ref,
+        turn_ref,
+        raw_other_ref,
+        normed_other_ref,
+        normed_late_ref,
+        raw_ref,
+        normed_ref,
+    ) = refs[count:]
+    total, wide, width = normed_ref.shape
+    rows = raw_own_ref.shape[0]
+    row_index = lax.axis_index("row")
+    sub_index = lax.axis_index("sub")
+    normed_ref[:, total:, :] = jnp.zeros((total, wide - total, width), F32)
+    scatter(refs[:count], sources, raw_ref, normed_ref)
+    own_rows = pl.ds(row_index * rows, rows)
+    raw_ref[own_rows] = raw_own_ref[...]
+    normed_ref[own_rows] = normed_own_ref[...]
+    turn_ref[own_rows] = turn_own_ref[...]
+    for row_step in row_steps:
+        whole_rows(att_bias_ref, normed_ref, turn_ref, rows, row_step)
+    other_rows = lax.axis_index("col") * lax.axis_size("sub") + sub_index
+    late_rows = row_index ^ jnp.where(sub_index == 0, *late_step)
+    raw_other_ref[...] = raw_ref[pl.ds(other_rows * rows, rows)]
+    normed_other_ref[...] = normed_ref[pl.ds(other_rows * rows, rows)]
+    normed_late_ref[...] = normed_ref[pl.ds(late_rows * rows, rows)]
+
+
+def finish(*refs, source):
+    (
+        block_ref,
         turned_weights_ref,
         key_weights_ref,
         out_weights_ref,
@@ -326,28 +387,33 @@
         plain_bias_ref,
         valid_ref,
         raw_own_ref,
-        normed_own_ref,
+        _,
         scores_ref,
         values_ref,
         gates_ref,
-        turn_own_ref,
+        _,
         mult_in_ref,
         mult_gate_ref,
         mult_out_ref,
         trans_up_ref,
         trans_down_ref,
+        turn_early_ref,
+        raw_early_ref,
+        normed_early_ref,
+        late_early_ref,
         result_ref,
+        raw_ref,
         normed_ref,
-        raw_ref,
+        late_ref,
         turn_ref,
         bias_ref,
         left_ref,
         right_ref,
         first_ref,
         tile_ref,
-    ) = refs[count:]
-    rows, cols, width = block_refs[0].shape
-    total = normed_ref.shape[0]
+    ) = refs
+    rows, cols, width = block_ref.shape
+    total = valid_ref.shape[0]
     heads = plain_bias_ref.shape[0]
     head_dim = width // heads
     row_index = lax.axis_index("row")
@@ -356,23 +422,26 @@
     other_rows = col_index * lax.axis_size("sub") + sub_index
     side = 2 * WIDE
 
-    normed_ref[:, total:, :] = jnp.zeros((total, WIDE - total, width), F32)
-    for ref, (row_step, col_step) in zip(block_refs, sources):
-        row_off = jnp.where(sub_index == 0, row_step[0], row_step[1])
-        col_off = jnp.where(sub_index == 0, col_step[0], col_step[1])
-        value = ref[...].astype(F32)
-        down = pl.ds((row_index ^ row_off) * rows, rows)
-        along = pl.ds(pl.multiple_of((col_index ^ col_off) * cols, 8), cols)
-        raw_ref[down, along, :] = value
-        normed_ref[down, along, :] = norm(value)
-    own_rows = pl.ds(row_index * rows, rows)
+    row_step, col_step = source
+    late_rows = row_index ^ jnp.where(sub_index == 0, *row_step)
+    col_block = col_index ^ jnp.where(sub_index == 0, *col_step)
+    along = pl.ds(pl.multiple_of(col_block * cols, 8), cols)
+    value, result = block_norm(block_ref)
+    late_ref[...] = late_early_ref[...]
+    late_ref[:, along, :] = result
+    turn_ref[...] = turn_early_ref[...]
     weights = att_bias_ref[...].astype(BF16)
-    for step in range(1, total // rows):
-        start = (row_index ^ step) * rows
-        for at in range(rows // 2):
-            tokens = flat_pair(normed_ref, start + 2 * at).astype(BF16)
-            bias_rows(weights, tokens, turn_ref, start + 2 * at)
-    turn_ref[own_rows] = turn_own_ref[...]
+    for at in range(rows // 2):
+        tokens = flat_pair(late_ref, 2 * at).astype(BF16)
+        bias_rows(weights, tokens, turn_ref, late_rows * rows + 2 * at)
+    raw_ref[...] = raw_early_ref[...]
+    normed_ref[...] = normed_early_ref[...]
+
+    @pl.when(other_rows == late_rows)
+    def _():
+        raw_ref[:, along, :] = value
+        normed_ref[:, along, :] = late_ref[:, along, :]
+
     for head in range(heads):
         value = turn_ref[:, head, :] + plain_bias_ref[head]
         value = jnp.concatenate([value, jnp.zeros((WIDE - total, side), F32)], axis=0)
@@ -422,15 +491,11 @@
     steps = range(rows // 2)
     start = other_rows * rows
 
-    @pl.when(other_rows == row_index)
-    def _():
-        raw_ref[own_rows] = raw_own_ref[...]
-        normed_ref[own_rows] = normed_own_ref[...]
-
-    tokens = [flat_pair(normed_ref, start + 2 * at).astype(BF16) for at in steps]
+    tokens = [flat_pair(normed_ref, 2 * at).astype(BF16) for at in steps]
     scores, values, gates = project(
         tokens, turned_weights_ref[...], key_weights_ref[...], heads, total
     )
+
     def run(own, group):
         if own:
             updates = attend(
@@ -447,7 +512,7 @@
                 [gates[at] for at in group],
             )
             starts = [start + 2 * at for at in group]
-            raws = [flat_pair(raw_ref, at) for at in starts]
+            raws = [flat_pair(raw_ref, 2 * at) for at in group]
         firsts = [raw + update for raw, update in zip(raws, updates)]
         if own:
             for at, first in zip(group, firsts):
@@ -524,14 +589,18 @@
         return lax.ppermute(value, axes, routes)
 
     swap = functools.partial(lax.ppermute, axis_name="sub", perm=[(0, 1), (1, 0)])
-    near = exchange(pair, STEPS[0])
-    fetched = [exchange(pair, offsets) for offsets in STEPS[1:]]
+    fetched = []
+    for offsets in STEPS:
+        fetched.append(exchange(pair, offsets))
     proj_other = swap(att_proj)
     out_other = swap(att_out)
     bias_other = swap(att_bias)
     chain_other = swap(chain_bias)
     blocks, sources = [], []
-    for value, offsets in zip(fetched, STEPS[1:]):
+    for value, offsets in zip(fetched, STEPS):
+        if offsets == ((0, 1), (0, 1)):
+            near = value
+            continue
         mine = tuple(zip(offsets[0], offsets[1]))
         blocks.append(value)
         sources.append(mine)
@@ -594,16 +663,27 @@
         ],
         compiler_params=pltpu.CompilerParams(vmem_limit_bytes=LIMIT),
     )(length, *params, *early)
-    operands = [*blocks, *ready]
+    last = sources[-1][0]
+    others = [[step for step in range(1, row_count) if step != late] for late in last]
+    merged = pl.pallas_call(
+        functools.partial(
+            collect, sources=tuple(sources[:-1]), row_steps=tuple(zip(*others)), late_step=last
+        ),
+        out_shape=[shape((total, 8, side), F32)] + [shape((rows, WIDE, width), F32)] * 3,
+        in_specs=[vmem] * (len(blocks) + 3),
+        out_specs=[vmem] * 4,
+        scratch_shapes=[pltpu.VMEM((total, WIDE, width), F32)] * 2,
+        compiler_params=pltpu.CompilerParams(vmem_limit_bytes=LIMIT),
+    )(*blocks[:-1], ready[3], ready[6], ready[7], ready[11])
+    operands = [blocks[-1], *ready, *merged]
     deep = 16
     return pl.pallas_call(
-        functools.partial(finish, sources=tuple(sources)),
+        functools.partial(finish, source=sources[-1]),
         out_shape=shape((rows, cols // sub_count, width), BF16),
         in_specs=[vmem] * len(operands),
         out_specs=vmem,
         scratch_shapes=[
-            pltpu.VMEM((total, WIDE, width), F32),
-            pltpu.VMEM((total, WIDE, width), F32),
+            *[pltpu.VMEM((rows, WIDE, width), F32)] * 3,
             pltpu.VMEM((total, 8, side), F32),
             pltpu.VMEM((heads * total, side), F32),
             pltpu.VMEM((rows, total, width), F32),

time: 21.7 us -> 22.7 us (1.046)
  Pallas kernels: 7.2 us -> 7.63 us
  waiting for transfers between devices: 5 us -> 5.35 us
  starting transfers between devices: 8.63 us -> 8.9 us
    ppermute x4, waiting for transfers between devices: 2.34 us -> 2.97 us  [exchange(): return lax.ppermute(value, axes, routes)]
    ppermute x3, starting transfers between devices: 0.57 us -> 0.07 us  [gathered(): blocks.append(swap(value))]
    ppermute x1, starting transfers between devices: 0.07 us -> 0.51 us  [gathered(): proj_other = swap(att_proj)]
    pallas_call x1 -> x2, Pallas kernels: 5.21 us -> 5.57 us  [the longest x1 4.55 us: gathered(): pl.pallas_call(functools.partial(finish, source=sources[-1]), out_shape=s...]
    ppermute x4, starting transfers between devices: 7.14 us -> 7.47 us  [exchange(): return lax.ppermute(value, axes, routes)]
    ppermute x1, waiting for transfers between devices: 0.74 us -> 0.46 us  [gathered(): proj_other = swap(att_proj)]
  transfers between devices with their start and end apart: 11 -> 11, of which waited for: 5 -> 5; matrix products, arithmetic and copies ran while one was open for 0% -> 0% of each run, Pallas kernels for 9% -> 14%
where the time goes in v4:
time: 22.7 us; the launch traced here: 22.6 us
  starting transfers between devices  8.9 us (39%)
  Pallas kernels  7.63 us (34%)
  waiting for transfers between devices  5.35 us (24%)
  between operations  0.69 us (3%)
    ppermute x4, starting transfers between devices, exchange(): return lax.ppermute(value, axes, routes)  7.47 us
    pallas_call x1, Pallas kernels, gathered(): pl.pallas_call(functools.partial(finish, source=sources[-1]), out_shape=s...  4.55 us
    ppermute x4, waiting for transfers between devices, exchange(): return lax.ppermute(value, axes, routes)  2.97 us
    pallas_call x1, Pallas kernels, gathered(): pl.pallas_call(prepare, out_shape=[shape((3 * width, width), BF16), shape...  2.06 us
    pallas_call x1, Pallas kernels, gathered(): pl.pallas_call(functools.partial(collect, sources=tuple(sources[:-1]), ro...  1.01 us
    ppermute x1, waiting for transfers between devices, gathered(): chain_other = swap(chain_bias)  0.95 us
    ppermute x1, waiting for transfers between devices, gathered(): bias_other = swap(att_bias)  0.95 us
    ppermute x1, starting transfers between devices, gathered(): proj_other = swap(att_proj)  0.51 us
  transfers between devices with their start and end apart: 11, of which 5 were waited for; matrix products, arithmetic and copies ran while one was open for 0% of the time, Pallas kernels for 14%

profile of v4, /device:TPU:0, one launch (start us, length us, event | category | flops | bytes accessed | tf_op | source)
XLA Modules:
  0.0 22.6 jit_solution(15231816029647648424)
XLA Ops:
  0.0 5.1 %collective-permute-start.9 = (bf16[12,24,128]{2,1,0:T(8,128)(2,1)}, bf16[12,24,128]{2,1,0:T(8,128)(2,1)S(1)}, u32[]{:S(2)}, u32[]{:S(2)}) collective-permute-start(bf16[12,24,128]{2,1,0:T(8,128)(2,1)} %own_hbm.1), channel_id=1, source_target_pairs={{0,12},{1,5},{2,14},{3,7},{4,8},{5,1},{6,10},{7,3},{8,4},{9,13},{1... | collective-permute-start | bytes 221192 | tf_op jit(solution)/shard_map/ppermute | solution.py:589
  5.1 1.1 %collective-permute-start.7 = (bf16[12,24,128]{2,1,0:T(8,128)(2,1)}, bf16[12,24,128]{2,1,0:T(8,128)(2,1)S(1)}, u32[]{:S(2)}, u32[]{:S(2)}) collective-permute-start(bf16[12,24,128]{2,1,0:T(8,128)(2,1)} %own_hbm.1), channel_id=1, source_target_pairs={{0,14},{1,11},{2,12},{3,9},{4,10},{5,15},{6,8},{7,13},{8,6},{9,3},... | collective-permute-start | bytes 221192 | tf_op jit(solution)/shard_map/ppermute | solution.py:589
  6.2 0.0 collective-permute-start
  6.2 0.0 collective-permute-start.6
  6.2 0.5 %collective-permute-start.5 = (f32[2]{0:T(128)}, f32[2]{0:T(128)S(1)}, u32[]{:S(2)}, u32[]{:S(2)}) collective-permute-start(f32[2]{0:T(128)} %param.17), channel_id=1, source_target_pairs={{0,1},{1,0},{2,3},{3,2},{4,5},{5,4},{6,7},{7,6},{8,9},{9,8},{10,11... | collective-permute-start | bytes 32 | tf_op jit(solution)/shard_map/ppermute | solution.py:598
  6.7 1.0 %collective-permute-done.5 = f32[2]{0:T(128)S(1)} collective-permute-done((f32[2]{0:T(128)}, f32[2]{0:T(128)S(1)}, u32[]{:S(2)}, u32[]{:S(2)}) %collective-permute-start.5) | collective-permute-done | bytes 40 | tf_op jit(solution)/shard_map/ppermute | solution.py:598
  7.7 0.3 %collective-permute-start.4 = (bf16[128,2]{0,1:T(2,128)(2,1)}, bf16[128,2]{0,1:T(2,128)(2,1)S(1)}, u32[]{:S(2)}, u32[]{:S(2)}) collective-permute-start(bf16[128,2]{0,1:T(2,128)(2,1)} %param.16), channel_id=1, source_target_pairs={{0,1},{1,0},{2,3},{3,2},{4,5},{5,4},{6,7},{7,6},{8,9},{9,8},{10,11... | collective-permute-start | bytes 1544 | tf_op jit(solution)/shard_map/ppermute | solution.py:597
  8.0 1.0 %collective-permute-done.4 = bf16[128,2]{0,1:T(2,128)(2,1)S(1)} collective-permute-done((bf16[128,2]{0,1:T(2,128)(2,1)}, bf16[128,2]{0,1:T(2,128)(2,1)S(1)}, u32[]{:S(2)}, u32[]{:S(2)}) %collective-permute-start.4) | collective-permute-done | bytes 544 | tf_op jit(solution)/shard_map/ppermute | solution.py:597
  9.0 1.2 %collective-permute-start.2 = (bf16[12,24,128]{2,1,0:T(8,128)(2,1)}, bf16[12,24,128]{2,1,0:T(8,128)(2,1)S(1)}, u32[]{:S(2)}, u32[]{:S(2)}) collective-permute-start(bf16[12,24,128]{2,1,0:T(8,128)(2,1)} %own_hbm.1), channel_id=1, source_target_pairs={{0,2},{1,3},{2,0},{3,1},{4,6},{5,7},{6,4},{7,5},{8,10},{9,11},{10,... | collective-permute-start | bytes 221192 | tf_op jit(solution)/shard_map/ppermute | solution.py:589
  10.2 0.0 collective-permute-done.9.refs_2_
  10.2 0.1 collective-permute-start.10
  10.3 2.2 %collective-permute-done.7.refs_0_ = bf16[12,24,128]{2,1,0:T(8,128)(2,1)S(1)} collective-permute-done((bf16[12,24,128]{2,1,0:T(8,128)(2,1)}, bf16[12,24,128]{2,1,0:T(8,128)(2,1)S(1)}, u32[]{:S(2)}, u32[]{:S(2)}) %collective-permute-start.7) | collective-permute-done | bytes 73760 | tf_op jit(solution)/shard_map/ppermute | solution.py:589
  12.5 0.0 collective-permute-start.8
  12.5 0.7 %collective-permute-done.refs_4_ = bf16[12,24,128]{2,1,0:T(8,128)(2,1)S(1)} collective-permute-done((bf16[12,24,128]{2,1,0:T(8,128)(2,1)}, bf16[12,24,128]{2,1,0:T(8,128)(2,1)S(1)}, u32[]{:S(2)}, u32[]{:S(2)}) %collective-permute-start) | collective-permute-done | bytes 73760 | tf_op jit(solution)/shard_map/ppermute | solution.py:589
  13.3 0.0 collective-permute-start.1
  13.3 0.0 collective-permute-done.6.out_other_ref
  13.3 0.5 %collective-permute-start.3 = (bf16[128,4,64]{0,2,1:T(8,128)(2,1)}, bf16[128,4,64]{0,2,1:T(8,128)(2,1)S(1)}, u32[]{:S(2)}, u32[]{:S(2)}) collective-permute-start(bf16[128,4,64]{0,2,1:T(8,128)(2,1)} %param.15), channel_id=1, source_target_pairs={{0,1},{1,0},{2,3},{3,2},{4,5},{5,4},{6,7},{7,6},{8,9},{9,8},{10,11... | collective-permute-start | bytes 196616 | tf_op jit(solution)/shard_map/ppermute | solution.py:595
  14.4 0.5 %collective-permute-done.3 = bf16[128,4,64]{0,2,1:T(8,128)(2,1)S(1)} collective-permute-done((bf16[128,4,64]{0,2,1:T(8,128)(2,1)}, bf16[128,4,64]{0,2,1:T(8,128)(2,1)S(1)}, u32[]{:S(2)}, u32[]{:S(2)}) %collective-permute-start.3) | collective-permute-done | bytes 65568 | tf_op jit(solution)/shard_map/ppermute | solution.py:595
  14.9 0.0 collective-permute-done.2.near_ref
  14.9 2.1 %shard_map.118 = (bf16[384,128]{1,0:T(8,128)(2,1)S(1)}, bf16[128,128]{1,0:T(8,128)(2,1)S(1)}, bf16[128,128]{1,0:T(8,128)(2,1)S(1)}, f32[8,128]{1,0:T(8,128)S(1)}...) custom-call(s32[1]{0:T(128)S(6)} %copy.13.length_ref, ...), custom_call_target="tpu_custom_call" | custom-call | tf_op jit(solution)/shard_map/pallas_call | solution.py:636
  17.0 0.0 collective-permute-done.10.refs_3_
  17.0 0.0 collective-permute-done.8.refs_1_
  17.0 1.0 %shard_map.119 = (f32[48,8,128]{2,1,0:T(8,128)S(1)}, f32[12,64,128]{2,1,0:T(8,128)S(1)}, f32[12,64,128]{2,1,0:T(8,128)S(1)}, f32[12,64,128]{2,1,0:T(8,128)S(1)}) custom-call(bf16[12,24,128]{2,1,0:T(8,128)(2,1)S(1)} %collective-permute-done.7.refs_0_, bf16[12,24,128]{2,1,0:T(8,128)(2,1)S(1)} %collective-permute-done.8.refs_1_, ...), custom_call_target="tpu_custom_call" | custom-call | tf_op jit(solution)/shard_map/pallas_call | solution.py:668
  18.0 0.0 collective-permute-done.1.refs_0_
  18.0 4.6 %shard_map.120 = bf16[12,12,128]{2,1,0:T(8,128)(2,1)} custom-call(bf16[12,24,128]{2,1,0:T(8,128)(2,1)S(1)} %collective-permute-done.1.refs_0_, bf16[384,128]{1,0:T(8,128)(2,1)S(1)} %get-tuple-element.26.refs_1_, bf16[128,128]{1,0:T(8,128)(2,1)S(1)} %get-tuple-element.27.refs_2_, bf16[128,128]{1,0:T(8,128)(2,1)S(1)} %get-tuple-element.28.refs_3_, ...), custom_call_target="tpu_custom_call" | custom-call | tf_op jit(solution)/shard_map/pallas_call | solution.py:680
Async XLA Ops:
  0.0 10.2 %collective-permute-start.9 = (bf16[12,24,128]{2,1,0:T(8,128)(2,1)}, bf16[12,24,128]{2,1,0:T(8,128)(2,1)S(1)}, u32[]{:S(2)}, u32[]{:S(2)}) collective-permute-start(bf16[12,24,128]{2,1,0:T(8,128)(2,1)} %own_hbm.1), channel_id=1, source_target_pairs={{0,12},{1,5},{2,14},{3,7},{4,8},{5,1},{6,10},{7,3},{8,4},{9,13},{1... | collective-permute-start | bytes 221192 | tf_op jit(solution)/shard_map/ppermute | solution.py:589
  5.1 7.4 %collective-permute-start.7 = (bf16[12,24,128]{2,1,0:T(8,128)(2,1)}, bf16[12,24,128]{2,1,0:T(8,128)(2,1)S(1)}, u32[]{:S(2)}, u32[]{:S(2)}) collective-permute-start(bf16[12,24,128]{2,1,0:T(8,128)(2,1)} %own_hbm.1), channel_id=1, source_target_pairs={{0,14},{1,11},{2,12},{3,9},{4,10},{5,15},{6,8},{7,13},{8,6},{9,3},... | collective-permute-start | bytes 221192 | tf_op jit(solution)/shard_map/ppermute | solution.py:589
  6.2 7.0 %collective-permute-start = (bf16[12,24,128]{2,1,0:T(8,128)(2,1)}, bf16[12,24,128]{2,1,0:T(8,128)(2,1)S(1)}, u32[]{:S(2)}, u32[]{:S(2)}) collective-permute-start(bf16[12,24,128]{2,1,0:T(8,128)(2,1)} %own_hbm.1), channel_id=1, source_target_pairs={{0,6},{1,9},{2,4},{3,11},{4,2},{5,13},{6,0},{7,15},{8,14},{9,1},{1... | collective-permute-start | bytes 221192 | tf_op jit(solution)/shard_map/ppermute | solution.py:589
  6.2 7.0 %collective-permute-start.6 = (bf16[64,128]{1,0:T(8,128)(2,1)}, bf16[64,128]{1,0:T(8,128)(2,1)S(1)}, u32[]{:S(2)}, u32[]{:S(2)}) collective-permute-start(bf16[64,128]{1,0:T(8,128)(2,1)} %out_hbm.1), channel_id=1, source_target_pairs={{0,1},{1,0},{2,3},{3,2},{4,5},{5,4},{6,7},{7,6},{8,9},{9,8},{10,11... | collective-permute-start | bytes 49160 | tf_op jit(solution)/shard_map/ppermute | solution.py:596
  6.2 1.5 %collective-permute-start.5 = (f32[2]{0:T(128)}, f32[2]{0:T(128)S(1)}, u32[]{:S(2)}, u32[]{:S(2)}) collective-permute-start(f32[2]{0:T(128)} %param.17), channel_id=1, source_target_pairs={{0,1},{1,0},{2,3},{3,2},{4,5},{5,4},{6,7},{7,6},{8,9},{9,8},{10,11... | collective-permute-start | bytes 32 | tf_op jit(solution)/shard_map/ppermute | solution.py:598
  7.7 1.3 %collective-permute-start.4 = (bf16[128,2]{0,1:T(2,128)(2,1)}, bf16[128,2]{0,1:T(2,128)(2,1)S(1)}, u32[]{:S(2)}, u32[]{:S(2)}) collective-permute-start(bf16[128,2]{0,1:T(2,128)(2,1)} %param.16), channel_id=1, source_target_pairs={{0,1},{1,0},{2,3},{3,2},{4,5},{5,4},{6,7},{7,6},{8,9},{9,8},{10,11... | collective-permute-start | bytes 1544 | tf_op jit(solution)/shard_map/ppermute | solution.py:597
  9.0 5.9 %collective-permute-start.2 = (bf16[12,24,128]{2,1,0:T(8,128)(2,1)}, bf16[12,24,128]{2,1,0:T(8,128)(2,1)S(1)}, u32[]{:S(2)}, u32[]{:S(2)}) collective-permute-start(bf16[12,24,128]{2,1,0:T(8,128)(2,1)} %own_hbm.1), channel_id=1, source_target_pairs={{0,2},{1,3},{2,0},{3,1},{4,6},{5,7},{6,4},{7,5},{8,10},{9,11},{10,... | collective-permute-start | bytes 221192 | tf_op jit(solution)/shard_map/ppermute | solution.py:589
  10.2 6.7 %collective-permute-start.10 = (bf16[12,24,128]{2,1,0:T(8,128)(2,1)S(1)}, bf16[12,24,128]{2,1,0:T(8,128)(2,1)S(1)}, u32[]{:S(2)}, u32[]{:S(2)}) collective-permute-start(bf16[12,24,128]{2,1,0:T(8,128)(2,1)S(1)} %collective-permute-done.9.refs_2_), channel_id=1, source_target_pairs={{0,1},{1,0},{2,3},{3,2},{4,5},{5,4},{6,7},{7,6},{8,9},{9,8},{10,11... | collective-permute-start | bytes 221192 | tf_op jit(solution)/shard_map/ppermute | solution.py:608
  12.5 4.5 %collective-permute-start.8 = (bf16[12,24,128]{2,1,0:T(8,128)(2,1)S(1)}, bf16[12,24,128]{2,1,0:T(8,128)(2,1)S(1)}, u32[]{:S(2)}, u32[]{:S(2)}) collective-permute-start(bf16[12,24,128]{2,1,0:T(8,128)(2,1)S(1)} %collective-permute-done.7.refs_0_), channel_id=1, source_target_pairs={{0,1},{1,0},{2,3},{3,2},{4,5},{5,4},{6,7},{7,6},{8,9},{9,8},{10,11... | collective-permute-start | bytes 221192 | tf_op jit(solution)/shard_map/ppermute | solution.py:608
  13.3 4.7 %collective-permute-start.1 = (bf16[12,24,128]{2,1,0:T(8,128)(2,1)S(1)}, bf16[12,24,128]{2,1,0:T(8,128)(2,1)S(1)}, u32[]{:S(2)}, u32[]{:S(2)}) collective-permute-start(bf16[12,24,128]{2,1,0:T(8,128)(2,1)S(1)} %collective-permute-done.refs_4_), channel_id=1, source_target_pairs={{0,1},{1,0},{2,3},{3,2},{4,5},{5,4},{6,7},{7,6},{8,9},{9,8},{10,11... | collective-permute-start | bytes 221192 | tf_op jit(solution)/shard_map/ppermute | solution.py:608
  13.3 1.6 %collective-permute-start.3 = (bf16[128,4,64]{0,2,1:T(8,128)(2,1)}, bf16[128,4,64]{0,2,1:T(8,128)(2,1)S(1)}, u32[]{:S(2)}, u32[]{:S(2)}) collective-permute-start(bf16[128,4,64]{0,2,1:T(8,128)(2,1)} %param.15), channel_id=1, source_target_pairs={{0,1},{1,0},{2,3},{3,2},{4,5},{5,4},{6,7},{7,6},{8,9},{9,8},{10,11... | collective-permute-start | bytes 196616 | tf_op jit(solution)/shard_map/ppermute | solution.py:595

commit v5 on v4

--- a/solution.py
+++ b/solution.py
@@ -139,9 +139,14 @@
 F32 = jnp.float32
 BF16 = jnp.bfloat16
 WIDE = 64
+FLIP = True
 GROUP = 6
 LIMIT = 16 * 1024 * 1024
 STEPS = (((0, 1), (0, 1)), ((3, 1), (2, 1)), ((3, 0), (1, 0)), ((1, 1), (2, 0)))
+
+
+def moved(row, step, count, sign):
+    return row ^ step if FLIP else lax.rem(row + count + sign * step, count)
 
 
 def replicated(mesh):
@@ -205,6 +210,27 @@
     return value.reshape(block.shape), result.reshape(block.shape)
 
 
+def split_norm(value):
+    width = value.shape[-1]
+    high = value.astype(BF16)
+    low = (value - high.astype(F32)).astype(BF16)
+    ones = jnp.full((2 * width, width), 1.0 / width, BF16)
+    centred = value - dot(jnp.concatenate([high, low], axis=1), ones)
+    variance = jnp.mean(centred * centred, axis=-1, keepdims=True)
+    return centred * lax.rsqrt(variance + 1e-05)
+
+
+def sum_down(parts):
+    row = lax.broadcasted_iota(jnp.int32, parts[0].shape, 0)
+    for distance in (1, 2, 4):
+        keep = (row & distance) == 0
+        parts = [
+            jnp.where(keep, one, two) + pltpu.roll(jnp.where(keep, two, one), distance, 0)
+            for one, two in zip(parts[0::2], parts[1::2])
+        ]
+    return parts[0]
+
+
 def bias_rows(weights, tokens, turn_ref, row):
     both = dot(weights, tokens, NT)
     turn_ref[row] = both
@@ -212,7 +238,7 @@
 
 
 def prepare(
-    length_ref,
+    length_any,
     chain_hbm,
     own_hbm,
     proj_hbm,
@@ -252,6 +278,7 @@
     att_bias_own_ref,
     chain_bias_ref,
     out_ref,
+    length_ref,
     copy_sems,
 ):
     pairs = (
@@ -261,6 +288,7 @@
         (att_bias_hbm, att_bias_own_ref),
         (chain_bias_hbm, chain_bias_ref),
         (out_hbm, out_ref),
+        (length_any, length_ref),
         (mult_in_hbm, mult_in_ref),
         (mult_gate_hbm, mult_gate_ref),
         (mult_out_hbm, mult_out_ref),
@@ -278,9 +306,10 @@
     col_index = lax.axis_index("col")
     normed_ref[:, total:, :] = jnp.zeros((rows, WIDE - total, width), F32)
     att_bias_ref[...] = jnp.zeros(att_bias_ref.shape, F32)
-    for copy in copies[:6]:
-        copy.wait()
-    for ref, col in ((own_ref, col_index), (near_ref, 1 - col_index)):
+    for ref, col in ((near_ref, 1 - col_index), (own_ref, col_index)):
+        if ref is own_ref:
+            for copy in copies[:7]:
+                copy.wait()
         at = pl.ds(pl.multiple_of(col * cols, 8), cols)
         value, result = block_norm(ref)
         raw_ref[:, at, :] = value
@@ -319,7 +348,7 @@
         scores_ref[at] = scores[at]
         values_ref[at] = values[at]
         gates_ref[at] = gates[at]
-    for copy in copies[6:]:
+    for copy in copies[7:]:
         copy.wait()
 
 
@@ -327,7 +356,9 @@
     sub_index = lax.axis_index("sub")
     for ref, (row_step, col_step) in zip(block_refs, sources):
         rows, cols, _ = ref.shape
-        row_block = lax.axis_index("row") ^ jnp.where(sub_index == 0, *row_step)
+        row_block = moved(
+            lax.axis_index("row"), jnp.where(sub_index == 0, *row_step), lax.axis_size("row"), -1
+        )
         col_block = lax.axis_index("col") ^ jnp.where(sub_index == 0, *col_step)
         down = pl.ds(row_block * rows, rows)
         along = pl.ds(pl.multiple_of(col_block * cols, 8), cols)
@@ -338,7 +369,13 @@
 
 def whole_rows(att_bias_ref, normed_ref, turn_ref, rows, row_step):
     weights = att_bias_ref[...].astype(BF16)
-    start = (lax.axis_index("row") ^ jnp.where(lax.axis_index("sub") == 0, *row_step)) * rows
+    start = moved(
+        lax.axis_index("row"),
+        jnp.where(lax.axis_index("sub") == 0, *row_step),
+        lax.axis_size("row"),
+        -1,
+    )
+    start = start * rows
     for at in range(rows // 2):
         tokens = flat_pair(normed_ref, start + 2 * at).astype(BF16)
         bias_rows(weights, tokens, turn_ref, start + 2 * at)
@@ -371,7 +408,9 @@
     for row_step in row_steps:
         whole_rows(att_bias_ref, normed_ref, turn_ref, rows, row_step)
     other_rows = lax.axis_index("col") * lax.axis_size("sub") + sub_index
-    late_rows = row_index ^ jnp.where(sub_index == 0, *late_step)
+    late_rows = moved(
+        row_index, jnp.where(sub_index == 0, *late_step), lax.axis_size("row"), -1
+    )
     raw_other_ref[...] = raw_ref[pl.ds(other_rows * rows, rows)]
     normed_other_ref[...] = normed_ref[pl.ds(other_rows * rows, rows)]
     normed_late_ref[...] = normed_ref[pl.ds(late_rows * rows, rows)]
@@ -411,6 +450,7 @@
         right_ref,
         first_ref,
         tile_ref,
+        tri_ref,
     ) = refs
     rows, cols, width = block_ref.shape
     total = valid_ref.shape[0]
@@ -423,7 +463,9 @@
     side = 2 * WIDE
 
     row_step, col_step = source
-    late_rows = row_index ^ jnp.where(sub_index == 0, *row_step)
+    late_rows = moved(
+        row_index, jnp.where(sub_index == 0, *row_step), lax.axis_size("row"), -1
+    )
     col_block = col_index ^ jnp.where(sub_index == 0, *col_step)
     along = pl.ds(pl.multiple_of(col_block * cols, 8), cols)
     value, result = block_norm(block_ref)
@@ -434,13 +476,11 @@
     for at in range(rows // 2):
         tokens = flat_pair(late_ref, 2 * at).astype(BF16)
         bias_rows(weights, tokens, turn_ref, late_rows * rows + 2 * at)
-    raw_ref[...] = raw_early_ref[...]
-    normed_ref[...] = normed_early_ref[...]
-
-    @pl.when(other_rows == late_rows)
-    def _():
-        raw_ref[:, along, :] = value
-        normed_ref[:, along, :] = late_ref[:, along, :]
+    here = pl.ds(jnp.where(other_rows == late_rows, 0, rows), rows)
+    raw_ref[:rows] = raw_early_ref[...]
+    normed_ref[:rows] = normed_early_ref[...]
+    raw_ref[here, along, :] = value
+    normed_ref[here, along, :] = result
 
     for head in range(heads):
         value = turn_ref[:, head, :] + plain_bias_ref[head]
@@ -474,17 +514,20 @@
                     dot(values[at][head * head_dim : (head + 1) * head_dim], spread_weights)
                 )
             attended.append((jnp.concatenate(parts, axis=0) * gates[at]).astype(BF16))
-        return [dot(each, out_weights, TN) for each in attended]
+        updates = [dot(each, out_weights, TN) for each in attended]
+        return [
+            jnp.concatenate([each[:total], each[WIDE : WIDE + total]], axis=0) for each in updates
+        ]
 
     def halves(firsts, starts, column):
-        mixed = [norm(first).astype(BF16) for first in firsts]
+        mixed = [split_norm(first).astype(BF16) for first in firsts]
         boths = [dot(each, mult_in_ref[:, column : column + 2 * width]) for each in mixed]
         values = [jax.nn.sigmoid(both[:, width:]) * both[:, :width] for both in boths]
         results = []
         for value, start in zip(values, starts):
             for which in range(2):
                 row_valid = valid_ref[pl.ds(start + which, 1), :]
-                each = value[which * WIDE : which * WIDE + total] * (valid_ref[...] * row_valid)
+                each = value[which * total : (which + 1) * total] * (valid_ref[...] * row_valid)
                 results.append(each.astype(BF16).astype(F32))
         return results
 
@@ -503,7 +546,7 @@
                 [values_ref[at] for at in group],
                 [gates_ref[at] for at in group],
             )
-            raws = [flat_pair(raw_own_ref, 2 * at) for at in group]
+            raws = [raw_own_ref[2 * at : 2 * at + 2, :total, :] for at in group]
             starts = [row_index * rows + 2 * at for at in group]
         else:
             updates = attend(
@@ -512,11 +555,11 @@
                 [gates[at] for at in group],
             )
             starts = [start + 2 * at for at in group]
-            raws = [flat_pair(raw_ref, 2 * at) for at in group]
-        firsts = [raw + update for raw, update in zip(raws, updates)]
+            raws = [raw_ref[2 * at : 2 * at + 2, :total, :] for at in group]
+        firsts = [raw.reshape(2 * total, width) + update for raw, update in zip(raws, updates)]
         if own:
             for at, first in zip(group, firsts):
-                first_ref[2 * at : 2 * at + 2] = first.reshape(2, WIDE, width)
+                first_ref[2 * at : 2 * at + 2] = first.reshape(2, total, width)
         results = halves(firsts, starts, 0 if own else 2 * width)
         into_ref = left_ref if own else right_ref
         for at, each in enumerate(results):
@@ -527,24 +570,24 @@
             run(own, list(range(at, at + GROUP)))
 
     half = rows
-    for block in range(total // half):
-
-        @pl.when(other_rows == block)
-        def _():
-            tile_ref[:, :half, :] = first_ref[:, block * half : (block + 1) * half, :]
-
-    def triangle(step, carry):
-        left = left_ref[step]
-        sums = [
-            jnp.sum(left * right_ref[other], axis=0, keepdims=True) for other in range(half)
+    deep = tile_ref.shape[1]
+    tile_ref[:, :half, :] = first_ref[:, pl.ds(other_rows * half, half), :]
+
+    def partials(at, others):
+        left = left_ref[at].reshape(total // 8, 8, width)
+        return [
+            jnp.sum(left * right_ref[other].reshape(total // 8, 8, width), axis=0)
+            for other in others
         ]
-        first_ref[step, :half, :] = jnp.concatenate(sums, axis=0)
-        return carry
-
-    lax.fori_loop(0, rows, triangle, 0)
-    deep = tile_ref.shape[1]
+
+    for at in range(0, rows, 2):
+        for each in (at, at + 1):
+            tri_ref[each, :8, :] = sum_down(partials(each, range(8)))
+        both = sum_down(partials(at, range(8, half)) + partials(at + 1, range(8, half)))
+        tri_ref[at, 8:half, :] = both[: half - 8]
+        tri_ref[at + 1, 8:half, :] = both[half - 8 :]
     first = tile_ref[...].reshape(rows * deep, width)
-    tri = first_ref[:, :deep, :].reshape(rows * deep, width)
+    tri = tri_ref[...].reshape(rows * deep, width)
     mixed = norm(first).astype(BF16)
     gate = jax.nn.sigmoid(dot(mixed, mult_gate_ref[...]))
     second = first + gate * dot(norm(tri).astype(BF16), mult_out_ref[...])
@@ -579,9 +622,12 @@
     def place(row, col, sub):
         return (row * col_count + col) * sub_count + sub
 
+    def ahead(row, step):
+        return row ^ step if FLIP else (row + step) % row_count
+
     def exchange(value, offsets):
         routes = [
-            (place(row, col, sub), place(row ^ offsets[sub][0], col ^ offsets[sub][1], sub))
+            (place(row, col, sub), place(ahead(row, offsets[sub][0]), col ^ offsets[sub][1], sub))
             for row in range(row_count)
             for col in range(col_count)
             for sub in range(sub_count)
@@ -607,7 +653,6 @@
         if offsets[0] != offsets[1]:
             blocks.append(swap(value))
             sources.append(tuple((b, a) for a, b in mine))
-    smem = pl.BlockSpec(memory_space=pltpu.SMEM)
     vmem = pl.BlockSpec(memory_space=pltpu.VMEM)
     hbm = pl.BlockSpec(memory_space=pltpu.HBM)
     params = [
@@ -650,7 +695,7 @@
             shape((rows, 8, side), F32),
             *[shape(each.shape, each.dtype) for each in params[-5:]],
         ],
-        in_specs=[smem] + [hbm] * len(params) + [vmem] * len(early),
+        in_specs=[pl.BlockSpec(memory_space=pl.ANY)] + [hbm] * len(params) + [vmem] * len(early),
         out_specs=[vmem] * 17,
         scratch_shapes=[
             scratch(params[0]),
@@ -659,7 +704,8 @@
             scratch(params[3]),
             scratch(params[4]),
             scratch(params[5]),
-            pltpu.SemaphoreType.DMA((len(params),)),
+            pltpu.SMEM((1,), jnp.int32),
+            pltpu.SemaphoreType.DMA((len(params) + 1,)),
         ],
         compiler_params=pltpu.CompilerParams(vmem_limit_bytes=LIMIT),
     )(length, *params, *early)
@@ -683,12 +729,14 @@
         in_specs=[vmem] * len(operands),
         out_specs=vmem,
         scratch_shapes=[
-            *[pltpu.VMEM((rows, WIDE, width), F32)] * 3,
+            *[pltpu.VMEM((2 * rows, WIDE, width), F32)] * 2,
+            pltpu.VMEM((rows, WIDE, width), F32),
             pltpu.VMEM((total, 8, side), F32),
             pltpu.VMEM((heads * total, side), F32),
             pltpu.VMEM((rows, total, width), F32),
             pltpu.VMEM((rows, total, width), F32),
-            pltpu.VMEM((rows, WIDE, width), F32),
+            pltpu.VMEM((rows, total, width), F32),
+            pltpu.VMEM((rows, deep, width), F32),
             pltpu.VMEM((rows, deep, width), F32),
         ],
         compiler_params=pltpu.CompilerParams(vmem_limit_bytes=LIMIT),

time: 22.7 us -> 22.3 us (0.982)
  Pallas kernels: 7.63 us -> 7.21 us
    pallas_call x1, Pallas kernels: 4.55 us -> 4.16 us  [gathered(): pl.pallas_call(functools.partial(finish, source=sources[-1]), out_shape=s...]
where the time goes in v5:
time: 22.3 us; the launch traced here: 22.1 us
  starting transfers between devices  8.9 us (40%)
  Pallas kernels  7.21 us (32%)
  waiting for transfers between devices  5.35 us (24%)
  between operations  0.69 us (3%)
    ppermute x4, starting transfers between devices, exchange(): return lax.ppermute(value, axes, routes)  7.47 us
    pallas_call x1, Pallas kernels, gathered(): pl.pallas_call(functools.partial(finish, source=sources[-1]), out_shape=s...  4.16 us
    ppermute x4, waiting for transfers between devices, exchange(): return lax.ppermute(value, axes, routes)  2.97 us
    pallas_call x1, Pallas kernels, gathered(): pl.pallas_call(prepare, out_shape=[shape((3 * width, width), BF16), shape...  2.04 us
    pallas_call x1, Pallas kernels, gathered(): pl.pallas_call(functools.partial(collect, sources=tuple(sources[:-1]), ro...  1.01 us
    ppermute x1, waiting for transfers between devices, gathered(): chain_other = swap(chain_bias)  0.95 us
    ppermute x1, waiting for transfers between devices, gathered(): bias_other = swap(att_bias)  0.95 us
    ppermute x1, starting transfers between devices, gathered(): proj_other = swap(att_proj)  0.51 us
  transfers between devices with their start and end apart: 11, of which 5 were waited for; matrix products, arithmetic and copies ran while one was open for 0% of the time, Pallas kernels for 14%

profile of v5, /device:TPU:0, one launch (start us, length us, event | category | flops | bytes accessed | tf_op | source)
XLA Modules:
  0.0 22.1 jit_solution(13732910024380142546)
XLA Ops:
  0.0 5.1 %collective-permute-start.9 = (bf16[12,24,128]{2,1,0:T(8,128)(2,1)}, bf16[12,24,128]{2,1,0:T(8,128)(2,1)S(1)}, u32[]{:S(2)}, u32[]{:S(2)}) collective-permute-start(bf16[12,24,128]{2,1,0:T(8,128)(2,1)} %own_hbm.1), channel_id=1, source_target_pairs={{0,12},{1,5},{2,14},{3,7},{4,8},{5,1},{6,10},{7,3},{8,4},{9,13},{1... | collective-permute-start | bytes 221192 | tf_op jit(solution)/shard_map/ppermute | solution.py:635
  5.1 1.1 %collective-permute-start.7 = (bf16[12,24,128]{2,1,0:T(8,128)(2,1)}, bf16[12,24,128]{2,1,0:T(8,128)(2,1)S(1)}, u32[]{:S(2)}, u32[]{:S(2)}) collective-permute-start(bf16[12,24,128]{2,1,0:T(8,128)(2,1)} %own_hbm.1), channel_id=1, source_target_pairs={{0,14},{1,11},{2,12},{3,9},{4,10},{5,15},{6,8},{7,13},{8,6},{9,3},... | collective-permute-start | bytes 221192 | tf_op jit(solution)/shard_map/ppermute | solution.py:635
  6.2 0.0 collective-permute-start
  6.2 0.0 collective-permute-start.6
  6.2 0.5 %collective-permute-start.5 = (f32[2]{0:T(128)}, f32[2]{0:T(128)S(1)}, u32[]{:S(2)}, u32[]{:S(2)}) collective-permute-start(f32[2]{0:T(128)} %param.17), channel_id=1, source_target_pairs={{0,1},{1,0},{2,3},{3,2},{4,5},{5,4},{6,7},{7,6},{8,9},{9,8},{10,11... | collective-permute-start | bytes 32 | tf_op jit(solution)/shard_map/ppermute | solution.py:644
  6.7 1.0 %collective-permute-done.5 = f32[2]{0:T(128)S(1)} collective-permute-done((f32[2]{0:T(128)}, f32[2]{0:T(128)S(1)}, u32[]{:S(2)}, u32[]{:S(2)}) %collective-permute-start.5) | collective-permute-done | bytes 40 | tf_op jit(solution)/shard_map/ppermute | solution.py:644
  7.7 0.3 %collective-permute-start.4 = (bf16[128,2]{0,1:T(2,128)(2,1)}, bf16[128,2]{0,1:T(2,128)(2,1)S(1)}, u32[]{:S(2)}, u32[]{:S(2)}) collective-permute-start(bf16[128,2]{0,1:T(2,128)(2,1)} %param.16), channel_id=1, source_target_pairs={{0,1},{1,0},{2,3},{3,2},{4,5},{5,4},{6,7},{7,6},{8,9},{9,8},{10,11... | collective-permute-start | bytes 1544 | tf_op jit(solution)/shard_map/ppermute | solution.py:643
  8.0 1.0 %collective-permute-done.4 = bf16[128,2]{0,1:T(2,128)(2,1)S(1)} collective-permute-done((bf16[128,2]{0,1:T(2,128)(2,1)}, bf16[128,2]{0,1:T(2,128)(2,1)S(1)}, u32[]{:S(2)}, u32[]{:S(2)}) %collective-permute-start.4) | collective-permute-done | bytes 544 | tf_op jit(solution)/shard_map/ppermute | solution.py:643
  9.0 1.2 %collective-permute-start.2 = (bf16[12,24,128]{2,1,0:T(8,128)(2,1)}, bf16[12,24,128]{2,1,0:T(8,128)(2,1)S(1)}, u32[]{:S(2)}, u32[]{:S(2)}) collective-permute-start(bf16[12,24,128]{2,1,0:T(8,128)(2,1)} %own_hbm.1), channel_id=1, source_target_pairs={{0,2},{1,3},{2,0},{3,1},{4,6},{5,7},{6,4},{7,5},{8,10},{9,11},{10,... | collective-permute-start | bytes 221192 | tf_op jit(solution)/shard_map/ppermute | solution.py:635
  10.2 0.0 collective-permute-done.9.refs_2_
  10.2 0.1 collective-permute-start.10
  10.3 2.2 %collective-permute-done.7.refs_0_ = bf16[12,24,128]{2,1,0:T(8,128)(2,1)S(1)} collective-permute-done((bf16[12,24,128]{2,1,0:T(8,128)(2,1)}, bf16[12,24,128]{2,1,0:T(8,128)(2,1)S(1)}, u32[]{:S(2)}, u32[]{:S(2)}) %collective-permute-start.7) | collective-permute-done | bytes 73760 | tf_op jit(solution)/shard_map/ppermute | solution.py:635
  12.5 0.0 collective-permute-start.8
  12.5 0.7 %collective-permute-done.refs_4_ = bf16[12,24,128]{2,1,0:T(8,128)(2,1)S(1)} collective-permute-done((bf16[12,24,128]{2,1,0:T(8,128)(2,1)}, bf16[12,24,128]{2,1,0:T(8,128)(2,1)S(1)}, u32[]{:S(2)}, u32[]{:S(2)}) %collective-permute-start) | collective-permute-done | bytes 73760 | tf_op jit(solution)/shard_map/ppermute | solution.py:635
  13.3 0.0 collective-permute-start.1
  13.3 0.0 collective-permute-done.6.out_other_ref
  13.3 0.5 %collective-permute-start.3 = (bf16[128,4,64]{0,2,1:T(8,128)(2,1)}, bf16[128,4,64]{0,2,1:T(8,128)(2,1)S(1)}, u32[]{:S(2)}, u32[]{:S(2)}) collective-permute-start(bf16[128,4,64]{0,2,1:T(8,128)(2,1)} %param.15), channel_id=1, source_target_pairs={{0,1},{1,0},{2,3},{3,2},{4,5},{5,4},{6,7},{7,6},{8,9},{9,8},{10,11... | collective-permute-start | bytes 196616 | tf_op jit(solution)/shard_map/ppermute | solution.py:641
  14.4 0.5 %collective-permute-done.3 = bf16[128,4,64]{0,2,1:T(8,128)(2,1)S(1)} collective-permute-done((bf16[128,4,64]{0,2,1:T(8,128)(2,1)}, bf16[128,4,64]{0,2,1:T(8,128)(2,1)S(1)}, u32[]{:S(2)}, u32[]{:S(2)}) %collective-permute-start.3) | collective-permute-done | bytes 65568 | tf_op jit(solution)/shard_map/ppermute | solution.py:641
  14.9 0.0 collective-permute-done.2.near_ref
  14.9 2.0 %shard_map.118 = (bf16[384,128]{1,0:T(8,128)(2,1)S(1)}, bf16[128,128]{1,0:T(8,128)(2,1)S(1)}, bf16[128,128]{1,0:T(8,128)(2,1)S(1)}, f32[8,128]{1,0:T(8,128)S(1)}...) custom-call(s32[1]{0:T(128)S(6)} %copy.13.length_any, ...), custom_call_target="tpu_custom_call" | custom-call | tf_op jit(solution)/shard_map/pallas_call | solution.py:681
  16.9 0.0 collective-permute-done.10.refs_3_
  17.0 0.0 collective-permute-done.8.refs_1_
  17.0 1.0 %shard_map.119 = (f32[48,8,128]{2,1,0:T(8,128)S(1)}, f32[12,64,128]{2,1,0:T(8,128)S(1)}, f32[12,64,128]{2,1,0:T(8,128)S(1)}, f32[12,64,128]{2,1,0:T(8,128)S(1)}) custom-call(bf16[12,24,128]{2,1,0:T(8,128)(2,1)S(1)} %collective-permute-done.7.refs_0_, bf16[12,24,128]{2,1,0:T(8,128)(2,1)S(1)} %collective-permute-done.8.refs_1_, ...), custom_call_target="tpu_custom_call" | custom-call | tf_op jit(solution)/shard_map/pallas_call | solution.py:714
  18.0 0.0 collective-permute-done.1.refs_0_
  18.0 4.2 %shard_map.120 = bf16[12,12,128]{2,1,0:T(8,128)(2,1)} custom-call(bf16[12,24,128]{2,1,0:T(8,128)(2,1)S(1)} %collective-permute-done.1.refs_0_, bf16[384,128]{1,0:T(8,128)(2,1)S(1)} %get-tuple-element.26.refs_1_, bf16[128,128]{1,0:T(8,128)(2,1)S(1)} %get-tuple-element.27.refs_2_, bf16[128,128]{1,0:T(8,128)(2,1)S(1)} %get-tuple-element.28.refs_3_, ...), custom_call_target="tpu_custom_call" | custom-call | tf_op jit(solution)/shard_map/pallas_call | solution.py:726
Async XLA Ops:
  0.0 10.2 %collective-permute-start.9 = (bf16[12,24,128]{2,1,0:T(8,128)(2,1)}, bf16[12,24,128]{2,1,0:T(8,128)(2,1)S(1)}, u32[]{:S(2)}, u32[]{:S(2)}) collective-permute-start(bf16[12,24,128]{2,1,0:T(8,128)(2,1)} %own_hbm.1), channel_id=1, source_target_pairs={{0,12},{1,5},{2,14},{3,7},{4,8},{5,1},{6,10},{7,3},{8,4},{9,13},{1... | collective-permute-start | bytes 221192 | tf_op jit(solution)/shard_map/ppermute | solution.py:635
  5.1 7.4 %collective-permute-start.7 = (bf16[12,24,128]{2,1,0:T(8,128)(2,1)}, bf16[12,24,128]{2,1,0:T(8,128)(2,1)S(1)}, u32[]{:S(2)}, u32[]{:S(2)}) collective-permute-start(bf16[12,24,128]{2,1,0:T(8,128)(2,1)} %own_hbm.1), channel_id=1, source_target_pairs={{0,14},{1,11},{2,12},{3,9},{4,10},{5,15},{6,8},{7,13},{8,6},{9,3},... | collective-permute-start | bytes 221192 | tf_op jit(solution)/shard_map/ppermute | solution.py:635
  6.2 7.0 %collective-permute-start = (bf16[12,24,128]{2,1,0:T(8,128)(2,1)}, bf16[12,24,128]{2,1,0:T(8,128)(2,1)S(1)}, u32[]{:S(2)}, u32[]{:S(2)}) collective-permute-start(bf16[12,24,128]{2,1,0:T(8,128)(2,1)} %own_hbm.1), channel_id=1, source_target_pairs={{0,6},{1,9},{2,4},{3,11},{4,2},{5,13},{6,0},{7,15},{8,14},{9,1},{1... | collective-permute-start | bytes 221192 | tf_op jit(solution)/shard_map/ppermute | solution.py:635
  6.2 7.0 %collective-permute-start.6 = (bf16[64,128]{1,0:T(8,128)(2,1)}, bf16[64,128]{1,0:T(8,128)(2,1)S(1)}, u32[]{:S(2)}, u32[]{:S(2)}) collective-permute-start(bf16[64,128]{1,0:T(8,128)(2,1)} %out_hbm.1), channel_id=1, source_target_pairs={{0,1},{1,0},{2,3},{3,2},{4,5},{5,4},{6,7},{7,6},{8,9},{9,8},{10,11... | collective-permute-start | bytes 49160 | tf_op jit(solution)/shard_map/ppermute | solution.py:642
  6.2 1.5 %collective-permute-start.5 = (f32[2]{0:T(128)}, f32[2]{0:T(128)S(1)}, u32[]{:S(2)}, u32[]{:S(2)}) collective-permute-start(f32[2]{0:T(128)} %param.17), channel_id=1, source_target_pairs={{0,1},{1,0},{2,3},{3,2},{4,5},{5,4},{6,7},{7,6},{8,9},{9,8},{10,11... | collective-permute-start | bytes 32 | tf_op jit(solution)/shard_map/ppermute | solution.py:644
  7.7 1.3 %collective-permute-start.4 = (bf16[128,2]{0,1:T(2,128)(2,1)}, bf16[128,2]{0,1:T(2,128)(2,1)S(1)}, u32[]{:S(2)}, u32[]{:S(2)}) collective-permute-start(bf16[128,2]{0,1:T(2,128)(2,1)} %param.16), channel_id=1, source_target_pairs={{0,1},{1,0},{2,3},{3,2},{4,5},{5,4},{6,7},{7,6},{8,9},{9,8},{10,11... | collective-permute-start | bytes 1544 | tf_op jit(solution)/shard_map/ppermute | solution.py:643
  9.0 5.9 %collective-permute-start.2 = (bf16[12,24,128]{2,1,0:T(8,128)(2,1)}, bf16[12,24,128]{2,1,0:T(8,128)(2,1)S(1)}, u32[]{:S(2)}, u32[]{:S(2)}) collective-permute-start(bf16[12,24,128]{2,1,0:T(8,128)(2,1)} %own_hbm.1), channel_id=1, source_target_pairs={{0,2},{1,3},{2,0},{3,1},{4,6},{5,7},{6,4},{7,5},{8,10},{9,11},{10,... | collective-permute-start | bytes 221192 | tf_op jit(solution)/shard_map/ppermute | solution.py:635
  10.2 6.7 %collective-permute-start.10 = (bf16[12,24,128]{2,1,0:T(8,128)(2,1)S(1)}, bf16[12,24,128]{2,1,0:T(8,128)(2,1)S(1)}, u32[]{:S(2)}, u32[]{:S(2)}) collective-permute-start(bf16[12,24,128]{2,1,0:T(8,128)(2,1)S(1)} %collective-permute-done.9.refs_2_), channel_id=1, source_target_pairs={{0,1},{1,0},{2,3},{3,2},{4,5},{5,4},{6,7},{7,6},{8,9},{9,8},{10,11... | collective-permute-start | bytes 221192 | tf_op jit(solution)/shard_map/ppermute | solution.py:654
  12.5 4.4 %collective-permute-start.8 = (bf16[12,24,128]{2,1,0:T(8,128)(2,1)S(1)}, bf16[12,24,128]{2,1,0:T(8,128)(2,1)S(1)}, u32[]{:S(2)}, u32[]{:S(2)}) collective-permute-start(bf16[12,24,128]{2,1,0:T(8,128)(2,1)S(1)} %collective-permute-done.7.refs_0_), channel_id=1, source_target_pairs={{0,1},{1,0},{2,3},{3,2},{4,5},{5,4},{6,7},{7,6},{8,9},{9,8},{10,11... | collective-permute-start | bytes 221192 | tf_op jit(solution)/shard_map/ppermute | solution.py:654
  13.3 4.7 %collective-permute-start.1 = (bf16[12,24,128]{2,1,0:T(8,128)(2,1)S(1)}, bf16[12,24,128]{2,1,0:T(8,128)(2,1)S(1)}, u32[]{:S(2)}, u32[]{:S(2)}) collective-permute-start(bf16[12,24,128]{2,1,0:T(8,128)(2,1)S(1)} %collective-permute-done.refs_4_), channel_id=1, source_target_pairs={{0,1},{1,0},{2,3},{3,2},{4,5},{5,4},{6,7},{7,6},{8,9},{9,8},{10,11... | collective-permute-start | bytes 221192 | tf_op jit(solution)/shard_map/ppermute | solution.py:654
  13.3 1.6 %collective-permute-start.3 = (bf16[128,4,64]{0,2,1:T(8,128)(2,1)}, bf16[128,4,64]{0,2,1:T(8,128)(2,1)S(1)}, u32[]{:S(2)}, u32[]{:S(2)}) collective-permute-start(bf16[128,4,64]{0,2,1:T(8,128)(2,1)} %param.15), channel_id=1, source_target_pairs={{0,1},{1,0},{2,3},{3,2},{4,5},{5,4},{6,7},{7,6},{8,9},{9,8},{10,11... | collective-permute-start | bytes 196616 | tf_op jit(solution)/shard_map/ppermute | solution.py:641

commit v6 on v5

--- a/solution.py
+++ b/solution.py
@@ -139,10 +139,10 @@
 F32 = jnp.float32
 BF16 = jnp.bfloat16
 WIDE = 64
-FLIP = True
+FLIP = False
 GROUP = 6
 LIMIT = 16 * 1024 * 1024
-STEPS = (((0, 1), (0, 1)), ((3, 1), (2, 1)), ((3, 0), (1, 0)), ((1, 1), (2, 0)))
+STEPS = (((1, 0), (2, 1)), ((3, 0), (3, 1)), ((0, 1), (0, 1)), ((2, 0), (1, 1)))
 
 
 def moved(row, step, count, sign):
@@ -159,7 +159,9 @@
 
 
 def flat_pair(ref, start):
-    return ref[pl.ds(start, 2)].reshape(2 * ref.shape[1], ref.shape[2])
+    both = ref[pl.ds(start, 2)].astype(BF16)
+    pad = jnp.zeros((WIDE - both.shape[1], both.shape[2]), BF16)
+    return jnp.concatenate([both[0], pad, both[1], pad], axis=0)
 
 
 def head_masks(heads, width):
@@ -304,7 +306,6 @@
     heads = plain_bias_ref.shape[0]
     total = plain_bias_ref.shape[1]
     col_index = lax.axis_index("col")
-    normed_ref[:, total:, :] = jnp.zeros((rows, WIDE - total, width), F32)
     att_bias_ref[...] = jnp.zeros(att_bias_ref.shape, F32)
     for ref, col in ((near_ref, 1 - col_index), (own_ref, col_index)):
         if ref is own_ref:
@@ -337,7 +338,7 @@
         plain_bias_ref[head, :, :] = from_ref[:, at : at + 1] * same + masked
     down = lax.broadcasted_iota(jnp.int32, (total, width), 0)
     valid_ref[...] = (down < length).astype(F32)
-    tokens = [flat_pair(normed_ref, 2 * at).astype(BF16) for at in range(rows // 2)]
+    tokens = [flat_pair(normed_ref, 2 * at) for at in range(rows // 2)]
     weights = att_bias_ref[...].astype(BF16)
     for at in range(rows // 2):
         bias_rows(weights, tokens[at], turn_ref, 2 * at)
@@ -377,7 +378,7 @@
     )
     start = start * rows
     for at in range(rows // 2):
-        tokens = flat_pair(normed_ref, start + 2 * at).astype(BF16)
+        tokens = flat_pair(normed_ref, start + 2 * at)
         bias_rows(weights, tokens, turn_ref, start + 2 * at)
 
 
@@ -395,11 +396,9 @@
         raw_ref,
         normed_ref,
     ) = refs[count:]
-    total, wide, width = normed_ref.shape
     rows = raw_own_ref.shape[0]
     row_index = lax.axis_index("row")
     sub_index = lax.axis_index("sub")
-    normed_ref[:, total:, :] = jnp.zeros((total, wide - total, width), F32)
     scatter(refs[:count], sources, raw_ref, normed_ref)
     own_rows = pl.ds(row_index * rows, rows)
     raw_ref[own_rows] = raw_own_ref[...]
@@ -474,7 +473,7 @@
     turn_ref[...] = turn_early_ref[...]
     weights = att_bias_ref[...].astype(BF16)
     for at in range(rows // 2):
-        tokens = flat_pair(late_ref, 2 * at).astype(BF16)
+        tokens = flat_pair(late_ref, 2 * at)
         bias_rows(weights, tokens, turn_ref, late_rows * rows + 2 * at)
     here = pl.ds(jnp.where(other_rows == late_rows, 0, rows), rows)
     raw_ref[:rows] = raw_early_ref[...]
@@ -492,7 +491,7 @@
     pad = jnp.zeros((WIDE - total, side), BF16)
     out_weights = out_weights_ref[...]
 
-    def attend(scores, values, gates):
+    def soften(scores):
         weights = []
         for head in range(heads):
             at = slice(head * total, (head + 1) * total)
@@ -502,73 +501,72 @@
             weights.append(
                 [(part / jnp.sum(part, axis=0, keepdims=True)).astype(BF16) for part in parts]
             )
+        return list(zip(*weights))
+
+    def update(raws, weights, values, gates):
         attended = []
-        for at in range(len(scores)):
+        for each, value, gate in zip(weights, values, gates):
             parts = []
             for head in range(heads):
-                each = weights[head][at]
                 spread_weights = jnp.concatenate(
-                    [each * first_lanes, pad, each * second_lanes, pad], axis=0
+                    [each[head] * first_lanes, pad, each[head] * second_lanes, pad], axis=0
                 )
-                parts.append(
-                    dot(values[at][head * head_dim : (head + 1) * head_dim], spread_weights)
-                )
-            attended.append((jnp.concatenate(parts, axis=0) * gates[at]).astype(BF16))
+                parts.append(dot(value[head * head_dim : (head + 1) * head_dim], spread_weights))
+            attended.append((jnp.concatenate(parts, axis=0) * gate).astype(BF16))
         updates = [dot(each, out_weights, TN) for each in attended]
-        return [
+        updates = [
             jnp.concatenate([each[:total], each[WIDE : WIDE + total]], axis=0) for each in updates
         ]
-
-    def halves(firsts, starts, column):
+        return [raw.reshape(2 * total, width) + each for raw, each in zip(raws, updates)]
+
+    valid = valid_ref[...]
+
+    def side_of(firsts, column):
         mixed = [split_norm(first).astype(BF16) for first in firsts]
         boths = [dot(each, mult_in_ref[:, column : column + 2 * width]) for each in mixed]
         values = [jax.nn.sigmoid(both[:, width:]) * both[:, :width] for both in boths]
-        results = []
-        for value, start in zip(values, starts):
-            for which in range(2):
-                row_valid = valid_ref[pl.ds(start + which, 1), :]
-                each = value[which * total : (which + 1) * total] * (valid_ref[...] * row_valid)
-                results.append(each.astype(BF16).astype(F32))
-        return results
+        return [value[at : at + total] for value in values for at in (0, total)]
 
     steps = range(rows // 2)
-    start = other_rows * rows
-
-    tokens = [flat_pair(normed_ref, 2 * at).astype(BF16) for at in steps]
+
+    def own_first(group, weights):
+        return update(
+            [raw_own_ref[2 * at : 2 * at + 2] for at in group],
+            weights,
+            [values_ref[at] for at in group],
+            [gates_ref[at] for at in group],
+        )
+
+    def own_side(group, firsts):
+        for at, first in zip(group, firsts):
+            first_ref[2 * at : 2 * at + 2] = first.reshape(2, total, width)
+        for at, each in enumerate(side_of(firsts, 0)):
+            left_ref[2 * group[0] + at] = each * valid
+
+    def other_first(group, weights):
+        return update(
+            [raw_ref[2 * at : 2 * at + 2] for at in group],
+            weights,
+            [values[at] for at in group],
+            [gates[at] for at in group],
+        )
+
+    def other_side(group, firsts):
+        for at, each in enumerate(side_of(firsts, 2 * width)):
+            right_ref[2 * group[0] + at] = each
+
+    tokens = [flat_pair(normed_ref, 2 * at) for at in steps]
     scores, values, gates = project(
         tokens, turned_weights_ref[...], key_weights_ref[...], heads, total
     )
-
-    def run(own, group):
-        if own:
-            updates = attend(
-                [scores_ref[at] for at in group],
-                [values_ref[at] for at in group],
-                [gates_ref[at] for at in group],
-            )
-            raws = [raw_own_ref[2 * at : 2 * at + 2, :total, :] for at in group]
-            starts = [row_index * rows + 2 * at for at in group]
-        else:
-            updates = attend(
-                [scores[at] for at in group],
-                [values[at] for at in group],
-                [gates[at] for at in group],
-            )
-            starts = [start + 2 * at for at in group]
-            raws = [raw_ref[2 * at : 2 * at + 2, :total, :] for at in group]
-        firsts = [raw.reshape(2 * total, width) + update for raw, update in zip(raws, updates)]
-        if own:
-            for at, first in zip(group, firsts):
-                first_ref[2 * at : 2 * at + 2] = first.reshape(2, total, width)
-        results = halves(firsts, starts, 0 if own else 2 * width)
-        into_ref = left_ref if own else right_ref
-        for at, each in enumerate(results):
-            into_ref[2 * group[0] + at] = each
-
-    for own in (True, False):
-        for at in range(0, rows // 2, GROUP):
-            run(own, list(range(at, at + GROUP)))
-
+    groups = [list(steps)[at : at + GROUP] for at in range(0, len(steps), GROUP)]
+    for group in groups:
+        other = soften([scores[at] for at in group])
+        own = soften([scores_ref[at] for at in group])
+        other = other_first(group, other)
+        own = own_first(group, own)
+        other_side(group, other)
+        own_side(group, own)
     half = rows
     deep = tile_ref.shape[1]
     tile_ref[:, :half, :] = first_ref[:, pl.ds(other_rows * half, half), :]
@@ -587,6 +585,9 @@
         tri_ref[at, 8:half, :] = both[: half - 8]
         tri_ref[at + 1, 8:half, :] = both[half - 8 :]
     first = tile_ref[...].reshape(rows * deep, width)
+    row_valid = valid_ref[pl.ds(row_index * rows, rows), :].reshape(rows, 1, width)
+    other_valid = valid_ref[pl.ds(other_rows * half, half), :].reshape(1, half, width)
+    tri_ref[:, :half, :] = tri_ref[:, :half, :] * (row_valid * other_valid)
     tri = tri_ref[...].reshape(rows * deep, width)
     mixed = norm(first).astype(BF16)
     gate = jax.nn.sigmoid(dot(mixed, mult_gate_ref[...]))
@@ -687,8 +688,8 @@
             shape((8, width), F32),
             shape((heads, total, side), F32),
             shape((total, width), F32),
-            shape((rows, WIDE, width), F32),
-            shape((rows, WIDE, width), F32),
+            shape((rows, total, width), F32),
+            shape((rows, total, width), F32),
             shape((rows // 2, heads * total, side), F32),
             shape((rows // 2, width, side), BF16),
             shape((rows // 2, width, side), F32),
@@ -715,10 +716,10 @@
         functools.partial(
             collect, sources=tuple(sources[:-1]), row_steps=tuple(zip(*others)), late_step=last
         ),
-        out_shape=[shape((total, 8, side), F32)] + [shape((rows, WIDE, width), F32)] * 3,
+        out_shape=[shape((total, 8, side), F32)] + [shape((rows, total, width), F32)] * 3,
         in_specs=[vmem] * (len(blocks) + 3),
         out_specs=[vmem] * 4,
-        scratch_shapes=[pltpu.VMEM((total, WIDE, width), F32)] * 2,
+        scratch_shapes=[pltpu.VMEM((total, total, width), F32)] * 2,
         compiler_params=pltpu.CompilerParams(vmem_limit_bytes=LIMIT),
     )(*blocks[:-1], ready[3], ready[6], ready[7], ready[11])
     operands = [blocks[-1], *ready, *merged]
@@ -729,8 +730,8 @@
         in_specs=[vmem] * len(operands),
         out_specs=vmem,
         scratch_shapes=[
-            *[pltpu.VMEM((2 * rows, WIDE, width), F32)] * 2,
-            pltpu.VMEM((rows, WIDE, width), F32),
+            *[pltpu.VMEM((2 * rows, total, width), F32)] * 2,
+            pltpu.VMEM((rows, total, width), F32),
             pltpu.VMEM((total, 8, side), F32),
             pltpu.VMEM((heads * total, side), F32),
             pltpu.VMEM((rows, total, width), F32),

time: 22.3 us -> 22.3 us (level)
  starting transfers between devices: 8.9 us -> 10 us
  waiting for transfers between devices: 5.35 us -> 4.39 us
    ppermute x3, starting transfers between devices: 0.07 us -> 1.58 us  [gathered(): blocks.append(swap(value))]
    ppermute x4, waiting for transfers between devices: 2.97 us -> 1.5 us  [exchange(): return lax.ppermute(value, axes, routes)]
    ppermute x1, starting transfers between devices: 0.01 us -> 0.82 us  [gathered(): out_other = swap(att_out)]
    ppermute x4, starting transfers between devices: 7.47 us -> 6.93 us  [exchange(): return lax.ppermute(value, axes, routes)]
    ppermute x1, starting transfers between devices: 0.51 us -> 0.01 us  [gathered(): chain_other = swap(chain_bias)]
    ppermute x1, waiting for transfers between devices: 0.95 us -> 1.29 us  [gathered(): chain_other = swap(chain_bias)]
  transfers between devices with their start and end apart: 11 -> 11, of which waited for: 5 -> 4; matrix products, arithmetic and copies ran while one was open for 0% -> 0% of each run, Pallas kernels for 14% -> 13%
where the time goes in v6:
time: 22.3 us; the launch traced here: 22.1 us
  starting transfers between devices  10 us (45%)
  Pallas kernels  7.06 us (32%)
  waiting for transfers between devices  4.39 us (20%)
  between operations  0.69 us (3%)
    ppermute x4, starting transfers between devices, exchange(): return lax.ppermute(value, axes, routes)  6.93 us
    pallas_call x1, Pallas kernels, gathered(): pl.pallas_call(functools.partial(finish, source=sources[-1]), out_shape=s...  4.09 us
    pallas_call x1, Pallas kernels, gathered(): pl.pallas_call(prepare, out_shape=[shape((3 * width, width), BF16), shape...  2.04 us
    ppermute x3, starting transfers between devices, gathered(): blocks.append(swap(value))  1.58 us
    ppermute x4, waiting for transfers between devices, exchange(): return lax.ppermute(value, axes, routes)  1.5 us
    ppermute x1, waiting for transfers between devices, gathered(): chain_other = swap(chain_bias)  1.29 us
    ppermute x1, waiting for transfers between devices, gathered(): bias_other = swap(att_bias)  1.13 us
    pallas_call x1, Pallas kernels, gathered(): pl.pallas_call(functools.partial(collect, sources=tuple(sources[:-1]), ro...  0.93 us
  transfers between devices with their start and end apart: 11, of which 4 were waited for; matrix products, arithmetic and copies ran while one was open for 0% of the time, Pallas kernels for 13%

profile of v6, /device:TPU:0, one launch (start us, length us, event | category | flops | bytes accessed | tf_op | source)
XLA Modules:
  0.0 22.1 jit_solution(6986948910628499090)
XLA Ops:
  0.0 5.1 %collective-permute-start.9 = (bf16[12,24,128]{2,1,0:T(8,128)(2,1)}, bf16[12,24,128]{2,1,0:T(8,128)(2,1)S(1)}, u32[]{:S(2)}, u32[]{:S(2)}) collective-permute-start(bf16[12,24,128]{2,1,0:T(8,128)(2,1)} %own_hbm.1), channel_id=1, source_target_pairs={{0,12},{1,15},{2,14},{3,13},{4,0},{5,3},{6,2},{7,1},{8,4},{9,7},{1... | collective-permute-start | bytes 221192 | tf_op jit(solution)/shard_map/ppermute | solution.py:636
  5.1 0.0 collective-permute-start.7
  5.1 1.0 %collective-permute-start = (bf16[12,24,128]{2,1,0:T(8,128)(2,1)}, bf16[12,24,128]{2,1,0:T(8,128)(2,1)S(1)}, u32[]{:S(2)}, u32[]{:S(2)}) collective-permute-start(bf16[12,24,128]{2,1,0:T(8,128)(2,1)} %own_hbm.1), channel_id=1, source_target_pairs={{0,8},{1,7},{2,10},{3,5},{4,12},{5,11},{6,14},{7,9},{8,0},{9,15},{... | collective-permute-start | bytes 221192 | tf_op jit(solution)/shard_map/ppermute | solution.py:636
  6.1 0.8 %collective-permute-start.6 = (bf16[64,128]{1,0:T(8,128)(2,1)}, bf16[64,128]{1,0:T(8,128)(2,1)S(1)}, u32[]{:S(2)}, u32[]{:S(2)}) collective-permute-start(bf16[64,128]{1,0:T(8,128)(2,1)} %out_hbm.1), channel_id=1, source_target_pairs={{0,1},{1,0},{2,3},{3,2},{4,5},{5,4},{6,7},{7,6},{8,9},{9,8},{10,11... | collective-permute-start | bytes 49160 | tf_op jit(solution)/shard_map/ppermute | solution.py:643
  6.9 0.0 collective-permute-start.5
  6.9 1.3 %collective-permute-done.5 = f32[2]{0:T(128)S(1)} collective-permute-done((f32[2]{0:T(128)}, f32[2]{0:T(128)S(1)}, u32[]{:S(2)}, u32[]{:S(2)}) %collective-permute-start.5) | collective-permute-done | bytes 40 | tf_op jit(solution)/shard_map/ppermute | solution.py:645
  8.2 0.2 collective-permute-start.4
  8.4 1.1 %collective-permute-done.4 = bf16[128,2]{0,1:T(2,128)(2,1)S(1)} collective-permute-done((bf16[128,2]{0,1:T(2,128)(2,1)}, bf16[128,2]{0,1:T(2,128)(2,1)S(1)}, u32[]{:S(2)}, u32[]{:S(2)}) %collective-permute-start.4) | collective-permute-done | bytes 544 | tf_op jit(solution)/shard_map/ppermute | solution.py:644
  9.5 0.8 %collective-permute-start.2 = (bf16[12,24,128]{2,1,0:T(8,128)(2,1)}, bf16[12,24,128]{2,1,0:T(8,128)(2,1)S(1)}, u32[]{:S(2)}, u32[]{:S(2)}) collective-permute-start(bf16[12,24,128]{2,1,0:T(8,128)(2,1)} %own_hbm.1), channel_id=1, source_target_pairs={{0,2},{1,3},{2,0},{3,1},{4,6},{5,7},{6,4},{7,5},{8,10},{9,11},{10,... | collective-permute-start | bytes 221192 | tf_op jit(solution)/shard_map/ppermute | solution.py:636
  10.3 0.0 collective-permute-done.9.refs_2_
  10.3 0.1 collective-permute-start.10
  10.4 1.5 %collective-permute-done.7.refs_0_ = bf16[12,24,128]{2,1,0:T(8,128)(2,1)S(1)} collective-permute-done((bf16[12,24,128]{2,1,0:T(8,128)(2,1)}, bf16[12,24,128]{2,1,0:T(8,128)(2,1)S(1)}, u32[]{:S(2)}, u32[]{:S(2)}) %collective-permute-start.7) | collective-permute-done | bytes 73760 | tf_op jit(solution)/shard_map/ppermute | solution.py:636
  11.9 1.5 %collective-permute-start.8 = (bf16[12,24,128]{2,1,0:T(8,128)(2,1)S(1)}, bf16[12,24,128]{2,1,0:T(8,128)(2,1)S(1)}, u32[]{:S(2)}, u32[]{:S(2)}) collective-permute-start(bf16[12,24,128]{2,1,0:T(8,128)(2,1)S(1)} %collective-permute-done.7.refs_0_), channel_id=1, source_target_pairs={{0,1},{1,0},{2,3},{3,2},{4,5},{5,4},{6,7},{7,6},{8,9},{9,8},{10,11... | collective-permute-start | bytes 221192 | tf_op jit(solution)/shard_map/ppermute | solution.py:655
  13.4 0.0 collective-permute-done.refs_4_
  13.4 0.0 collective-permute-start.1
  13.4 0.0 collective-permute-done.6.out_other_ref
  13.4 0.5 %collective-permute-start.3 = (bf16[128,4,64]{0,2,1:T(8,128)(2,1)}, bf16[128,4,64]{0,2,1:T(8,128)(2,1)S(1)}, u32[]{:S(2)}, u32[]{:S(2)}) collective-permute-start(bf16[128,4,64]{0,2,1:T(8,128)(2,1)} %param.15), channel_id=1, source_target_pairs={{0,1},{1,0},{2,3},{3,2},{4,5},{5,4},{6,7},{7,6},{8,9},{9,8},{10,11... | collective-permute-start | bytes 196616 | tf_op jit(solution)/shard_map/ppermute | solution.py:642
  14.6 0.5 %collective-permute-done.3 = bf16[128,4,64]{0,2,1:T(8,128)(2,1)S(1)} collective-permute-done((bf16[128,4,64]{0,2,1:T(8,128)(2,1)}, bf16[128,4,64]{0,2,1:T(8,128)(2,1)S(1)}, u32[]{:S(2)}, u32[]{:S(2)}) %collective-permute-start.3) | collective-permute-done | bytes 65568 | tf_op jit(solution)/shard_map/ppermute | solution.py:642
  15.0 0.0 collective-permute-done.2.near_ref
  15.1 2.0 %shard_map.118 = (bf16[384,128]{1,0:T(8,128)(2,1)S(1)}, bf16[128,128]{1,0:T(8,128)(2,1)S(1)}, bf16[128,128]{1,0:T(8,128)(2,1)S(1)}, f32[8,128]{1,0:T(8,128)S(1)}...) custom-call(s32[1]{0:T(128)S(6)} %copy.13.length_any, ...), custom_call_target="tpu_custom_call" | custom-call | tf_op jit(solution)/shard_map/pallas_call | solution.py:682
  17.1 0.0 collective-permute-done.10.refs_3_
  17.1 0.0 collective-permute-done.8.refs_1_
  17.1 0.9 %shard_map.119 = (f32[48,8,128]{2,1,0:T(8,128)S(1)}, f32[12,48,128]{2,1,0:T(8,128)S(1)}, f32[12,48,128]{2,1,0:T(8,128)S(1)}, f32[12,48,128]{2,1,0:T(8,128)S(1)}) custom-call(bf16[12,24,128]{2,1,0:T(8,128)(2,1)S(1)} %collective-permute-done.7.refs_0_, bf16[12,24,128]{2,1,0:T(8,128)(2,1)S(1)} %collective-permute-done.8.refs_1_, ...), custom_call_target="tpu_custom_call" | custom-call | tf_op jit(solution)/shard_map/pallas_call | solution.py:715
  18.1 0.0 collective-permute-done.1.refs_0_
  18.1 4.1 %shard_map.120 = bf16[12,12,128]{2,1,0:T(8,128)(2,1)} custom-call(bf16[12,24,128]{2,1,0:T(8,128)(2,1)S(1)} %collective-permute-done.1.refs_0_, bf16[384,128]{1,0:T(8,128)(2,1)S(1)} %get-tuple-element.26.refs_1_, bf16[128,128]{1,0:T(8,128)(2,1)S(1)} %get-tuple-element.27.refs_2_, bf16[128,128]{1,0:T(8,128)(2,1)S(1)} %get-tuple-element.28.refs_3_, ...), custom_call_target="tpu_custom_call" | custom-call | tf_op jit(solution)/shard_map/pallas_call | solution.py:727
Async XLA Ops:
  0.0 10.3 %collective-permute-start.9 = (bf16[12,24,128]{2,1,0:T(8,128)(2,1)}, bf16[12,24,128]{2,1,0:T(8,128)(2,1)S(1)}, u32[]{:S(2)}, u32[]{:S(2)}) collective-permute-start(bf16[12,24,128]{2,1,0:T(8,128)(2,1)} %own_hbm.1), channel_id=1, source_target_pairs={{0,12},{1,15},{2,14},{3,13},{4,0},{5,3},{6,2},{7,1},{8,4},{9,7},{1... | collective-permute-start | bytes 221192 | tf_op jit(solution)/shard_map/ppermute | solution.py:636
  5.1 6.8 %collective-permute-start.7 = (bf16[12,24,128]{2,1,0:T(8,128)(2,1)}, bf16[12,24,128]{2,1,0:T(8,128)(2,1)S(1)}, u32[]{:S(2)}, u32[]{:S(2)}) collective-permute-start(bf16[12,24,128]{2,1,0:T(8,128)(2,1)} %own_hbm.1), channel_id=1, source_target_pairs={{0,4},{1,11},{2,6},{3,9},{4,8},{5,15},{6,10},{7,13},{8,12},{9,3},{... | collective-permute-start | bytes 221192 | tf_op jit(solution)/shard_map/ppermute | solution.py:636
  5.1 8.3 %collective-permute-start = (bf16[12,24,128]{2,1,0:T(8,128)(2,1)}, bf16[12,24,128]{2,1,0:T(8,128)(2,1)S(1)}, u32[]{:S(2)}, u32[]{:S(2)}) collective-permute-start(bf16[12,24,128]{2,1,0:T(8,128)(2,1)} %own_hbm.1), channel_id=1, source_target_pairs={{0,8},{1,7},{2,10},{3,5},{4,12},{5,11},{6,14},{7,9},{8,0},{9,15},{... | collective-permute-start | bytes 221192 | tf_op jit(solution)/shard_map/ppermute | solution.py:636
  6.1 7.3 %collective-permute-start.6 = (bf16[64,128]{1,0:T(8,128)(2,1)}, bf16[64,128]{1,0:T(8,128)(2,1)S(1)}, u32[]{:S(2)}, u32[]{:S(2)}) collective-permute-start(bf16[64,128]{1,0:T(8,128)(2,1)} %out_hbm.1), channel_id=1, source_target_pairs={{0,1},{1,0},{2,3},{3,2},{4,5},{5,4},{6,7},{7,6},{8,9},{9,8},{10,11... | collective-permute-start | bytes 49160 | tf_op jit(solution)/shard_map/ppermute | solution.py:643
  6.9 1.3 %collective-permute-start.5 = (f32[2]{0:T(128)}, f32[2]{0:T(128)S(1)}, u32[]{:S(2)}, u32[]{:S(2)}) collective-permute-start(f32[2]{0:T(128)} %param.17), channel_id=1, source_target_pairs={{0,1},{1,0},{2,3},{3,2},{4,5},{5,4},{6,7},{7,6},{8,9},{9,8},{10,11... | collective-permute-start | bytes 32 | tf_op jit(solution)/shard_map/ppermute | solution.py:645
  8.2 1.3 %collective-permute-start.4 = (bf16[128,2]{0,1:T(2,128)(2,1)}, bf16[128,2]{0,1:T(2,128)(2,1)S(1)}, u32[]{:S(2)}, u32[]{:S(2)}) collective-permute-start(bf16[128,2]{0,1:T(2,128)(2,1)} %param.16), channel_id=1, source_target_pairs={{0,1},{1,0},{2,3},{3,2},{4,5},{5,4},{6,7},{7,6},{8,9},{9,8},{10,11... | collective-permute-start | bytes 1544 | tf_op jit(solution)/shard_map/ppermute | solution.py:644
  9.5 5.5 %collective-permute-start.2 = (bf16[12,24,128]{2,1,0:T(8,128)(2,1)}, bf16[12,24,128]{2,1,0:T(8,128)(2,1)S(1)}, u32[]{:S(2)}, u32[]{:S(2)}) collective-permute-start(bf16[12,24,128]{2,1,0:T(8,128)(2,1)} %own_hbm.1), channel_id=1, source_target_pairs={{0,2},{1,3},{2,0},{3,1},{4,6},{5,7},{6,4},{7,5},{8,10},{9,11},{10,... | collective-permute-start | bytes 221192 | tf_op jit(solution)/shard_map/ppermute | solution.py:636
  10.3 6.8 %collective-permute-start.10 = (bf16[12,24,128]{2,1,0:T(8,128)(2,1)S(1)}, bf16[12,24,128]{2,1,0:T(8,128)(2,1)S(1)}, u32[]{:S(2)}, u32[]{:S(2)}) collective-permute-start(bf16[12,24,128]{2,1,0:T(8,128)(2,1)S(1)} %collective-permute-done.9.refs_2_), channel_id=1, source_target_pairs={{0,1},{1,0},{2,3},{3,2},{4,5},{5,4},{6,7},{7,6},{8,9},{9,8},{10,11... | collective-permute-start | bytes 221192 | tf_op jit(solution)/shard_map/ppermute | solution.py:655
  11.9 5.2 %collective-permute-start.8 = (bf16[12,24,128]{2,1,0:T(8,128)(2,1)S(1)}, bf16[12,24,128]{2,1,0:T(8,128)(2,1)S(1)}, u32[]{:S(2)}, u32[]{:S(2)}) collective-permute-start(bf16[12,24,128]{2,1,0:T(8,128)(2,1)S(1)} %collective-permute-done.7.refs_0_), channel_id=1, source_target_pairs={{0,1},{1,0},{2,3},{3,2},{4,5},{5,4},{6,7},{7,6},{8,9},{9,8},{10,11... | collective-permute-start | bytes 221192 | tf_op jit(solution)/shard_map/ppermute | solution.py:655
  13.4 4.6 %collective-permute-start.1 = (bf16[12,24,128]{2,1,0:T(8,128)(2,1)S(1)}, bf16[12,24,128]{2,1,0:T(8,128)(2,1)S(1)}, u32[]{:S(2)}, u32[]{:S(2)}) collective-permute-start(bf16[12,24,128]{2,1,0:T(8,128)(2,1)S(1)} %collective-permute-done.refs_4_), channel_id=1, source_target_pairs={{0,1},{1,0},{2,3},{3,2},{4,5},{5,4},{6,7},{7,6},{8,9},{9,8},{10,11... | collective-permute-start | bytes 221192 | tf_op jit(solution)/shard_map/ppermute | solution.py:655
  13.4 1.6 %collective-permute-start.3 = (bf16[128,4,64]{0,2,1:T(8,128)(2,1)}, bf16[128,4,64]{0,2,1:T(8,128)(2,1)S(1)}, u32[]{:S(2)}, u32[]{:S(2)}) collective-permute-start(bf16[128,4,64]{0,2,1:T(8,128)(2,1)} %param.15), channel_id=1, source_target_pairs={{0,1},{1,0},{2,3},{3,2},{4,5},{5,4},{6,7},{7,6},{8,9},{9,8},{10,11... | collective-permute-start | bytes 196616 | tf_op jit(solution)/shard_map/ppermute | solution.py:642
